TPU v7x, 512 devices: a whole 4x8x8 slice. The times are simulated.
512 devices in a mesh: port: 16 (over y_lo, x), tile: 32 (over y_hi, z, core).
Axes of the slice: x: 4, y: 8 (y_hi: 2, y_lo: 4; y = y_hi * 4 + y_lo), z: 8, core: 2. Of those that a mesh axis runs over, the one named last changes fastest.
Arguments:
- electric: float32 [16, 3, 6, 512, 640], P('port', None, None, 'tile'), may hold values from -6 to 6
- magnetic: float32 [16, 3, 6, 512, 640], P('port', None, None, 'tile'), may hold values from -6 to 6
- adjoint_electric: float32 [16, 3, 6, 512, 640], P('port', None, None, 'tile'), may hold values from -6 to 6
- adjoint_magnetic: float32 [16, 3, 6, 512, 640], P('port', None, None, 'tile'), may hold values from -6 to 6
- region_labels: int32 [6, 512, 640], P(None, 'tile'), may hold values from 0 to 7
- permittivity_table: float32 [8], replicated, may hold values from 1 to 12
- conductivity_table: float32 [8], replicated, may hold values from 0.05 to 2
- port_cells: int32 [16], P('port'), may hold values from 0 to 1966079
- port_amplitude: float32 [16, 3], P('port'), may hold values from -8 to 8
Outputs:
- earlier_electric: float32 [16, 3, 6, 512, 640], P('port', None, None, 'tile')
- earlier_magnetic: float32 [16, 3, 6, 512, 640], P('port', None, None, 'tile')
- gradient_permittivity: float32 [6, 512, 640], P(None, 'tile', 'port')
- gradient_conductivity: float32 [6, 512, 640], P(None, 'tile', 'port')
All inputs are finite; a program needn't handle non-finite values.
Results may differ from a plain program's by a relative error of at most 0.0003.
Values sent between devices are 32-bit elements; how exact they have to be, the bound alone decides.
No kernel may reach another device: no remote copies, remote signals or barrier semaphores. Data moves between devices by JAX's collectives and lax.ppermute only.
A program may use at most 64 MiB of HBM per device.

v0:
```python
import jax
import jax.numpy as jnp
from jax import lax
from jax.sharding import PartitionSpec as P

TIMESTEP = 0.5
HALF_STEP = 0.25


def from_behind(value, axis, steps):
    count = lax.axis_size(axis)
    first, last = (max(0, -steps), min(count, count - steps))
    return lax.ppermute(value, axis, [(source, source + steps) for source in range(first, last)])


def step_ahead(values, dimension, beyond):
    following = jnp.concatenate(
        [lax.slice_in_dim(values, 1, values.shape[dimension], axis=dimension), beyond],
        axis=dimension,
    )
    return following - values


def step_behind(values, dimension, before):
    preceding = jnp.concatenate(
        [before, lax.slice_in_dim(values, 0, values.shape[dimension] - 1, axis=dimension)],
        axis=dimension,
    )
    return values - preceding


def zero_layer(values, dimension):
    return jnp.zeros_like(lax.slice_in_dim(values, 0, 1, axis=dimension))


def curl_electric(field, next_second, next_third):
    first = step_ahead(field[2], 2, zero_layer(field[2], 2)) - step_ahead(
        field[1], 0, zero_layer(field[1], 0)
    )
    second = step_ahead(field[0], 0, zero_layer(field[0], 0)) - step_ahead(field[2], 1, next_third)
    third = step_ahead(field[1], 1, next_second) - step_ahead(field[0], 2, zero_layer(field[0], 2))
    return jnp.stack([first, second, third])


def curl_magnetic(field, prev_second, prev_third):
    first = step_behind(field[2], 2, zero_layer(field[2], 2)) - step_behind(
        field[1], 0, zero_layer(field[1], 0)
    )
    second = step_behind(field[0], 0, zero_layer(field[0], 0)) - step_behind(
        field[2], 1, prev_third
    )
    third = step_behind(field[1], 1, prev_second) - step_behind(
        field[0], 2, zero_layer(field[0], 2)
    )
    return jnp.stack([first, second, third])


def on_device(
    electric,
    magnetic,
    adjoint_electric,
    adjoint_magnetic,
    region_labels,
    permittivity_table,
    conductivity_table,
    port_cells,
    port_amplitude,
):
    field = electric[0]
    mag_field = magnetic[0]
    adj_field = adjoint_electric[0]
    adj_mag = adjoint_magnetic[0]
    depth, columns, width = region_labels.shape
    tile_index = lax.axis_index("tile")
    offset = tile_index * columns
    total_rows = columns * lax.axis_size("tile")
    corr_a = adj_field[0] * field[0] + adj_field[1] * field[1] + adj_field[2] * field[2]
    permittivity = jnp.zeros((depth, columns, width), jnp.float32)
    conductivity = jnp.zeros((depth, columns, width), jnp.float32)
    for region in range(permittivity_table.shape[0]):
        matches = region_labels == region
        permittivity = jnp.where(matches, permittivity_table[region], permittivity)
        conductivity = jnp.where(matches, conductivity_table[region], conductivity)
    denominator = permittivity + HALF_STEP * conductivity
    update_gain = (permittivity - HALF_STEP * conductivity) / denominator
    source_gain = TIMESTEP / denominator
    scaled = source_gain[None] * adj_field
    upper = from_behind((field[1:3, :, 0:1, :], scaled[1:3, :, 0:1, :]), "tile", -1)
    field_next, scaled_next = upper
    forward_magnetic = mag_field - TIMESTEP * curl_electric(field, field_next[0], field_next[1])
    new_magnetic = adj_mag + curl_electric(scaled, scaled_next[0], scaled_next[1])
    forward_rim, adjoint_rim = from_behind(
        (forward_magnetic[1:3, :, -1:, :], new_magnetic[1:3, :, -1:, :]), "tile", 1
    )
    positions = (
        lax.broadcasted_iota(jnp.int32, (depth, columns, width), 0) * (total_rows * width)
        + (lax.broadcasted_iota(jnp.int32, (depth, columns, width), 1) + offset) * width
        + lax.broadcasted_iota(jnp.int32, (depth, columns, width), 2)
    )
    hits = (positions == port_cells[0]).astype(jnp.float32)
    source = port_amplitude[0][:, None, None, None] * hits[None]
    drive = curl_magnetic(forward_magnetic, forward_rim[0], forward_rim[1]) - source
    corr_b = adj_field[0] * drive[0] + adj_field[1] * drive[1] + adj_field[2] * drive[2]
    summed_a, summed_b = (
        lax.psum_scatter(corr_a, "port", scatter_dimension=2, tiled=True),
        lax.psum_scatter(corr_b, "port", scatter_dimension=2, tiled=True),
    )
    new_electric = update_gain[None] * adj_field - TIMESTEP * curl_magnetic(
        new_magnetic, adjoint_rim[0], adjoint_rim[1]
    )
    share = width // lax.axis_size("port")
    begin = lax.axis_index("port") * share
    perm_share = lax.dynamic_slice_in_dim(permittivity, begin, share, 2)
    cond_share = lax.dynamic_slice_in_dim(conductivity, begin, share, 2)
    denom_share = perm_share + HALF_STEP * cond_share
    factor = TIMESTEP / (denom_share * denom_share)
    gradient_perm = factor * (cond_share * summed_a - summed_b)
    gradient_cond = factor * (-perm_share * summed_a - HALF_STEP * summed_b)
    return (new_electric[None], new_magnetic[None], gradient_perm, gradient_cond)


def solution(mesh):
    return jax.shard_map(
        on_device,
        mesh=mesh,
        in_specs=(
            P("port", None, None, "tile", None),
            P("port", None, None, "tile", None),
            P("port", None, None, "tile", None),
            P("port", None, None, "tile", None),
            P(None, "tile", None),
            P(),
            P(),
            P("port"),
            P("port", None),
        ),
        out_specs=(
            P("port", None, None, "tile", None),
            P("port", None, None, "tile", None),
            P(None, "tile", "port"),
            P(None, "tile", "port"),
        ),
        check_vma=False,
    )
```

profile of v0, /device:TPU:64, one launch (start us, length us, event | category | flops | bytes accessed | tf_op | source)
XLA Modules:
  0.0 238.8 jit_solution(7694957850522913474)
XLA Ops:
  7.2 0.0 all-reduce.21.cloned.1.call-start
  7.2 1.0 slice.370
  8.2 1.9 collective-permute-start.2
  10.1 0.0 copy-start.19
  10.1 1.2 broadcast_compare_fusion
  11.4 0.0 copy-start.20
  11.4 0.7 fusion.25
  12.1 0.7 fusion.26
  12.7 10.4 %subtract_divide_fusion = (f32[6,16,640]{2,1,0:T(8,128)S(1)}, f32[6,16,640]{2,1,0:T(8,128)S(1)}, f32[6,16,640]{2,1,0:T(8,128)S(1)}) fusion(pred[6,16,640]{2,1,0:T(8,128)(4,1)S(1)} %get-tuple-element.49, pred[6,16,640]{2,1,0:T(8,128)(4,1)S(1)} %get-tuple-element.48, pred[6,16,640]{2,1,0:T(8,128)(4,1)S(1)} %get-tuple-element.47, ...), kind=kLoop, calls=%fused_computation.60 | loop fusion | flops 1228800 | bytes 1228864 | tf_op jit(solution)/shard_map/div | solution.py:85
  23.2 0.0 copy-start.1
  23.2 0.1 bitcast_multiply_fusion
  23.3 0.6 slice.351
  23.9 7.0 %collective-permute-start = (f32[2,6,1,640]{3,2,1,0:T(1,128)}, f32[2,6,1,640]{3,2,1,0:T(1,128)S(1)}, u32[]{:S(2)}, u32[]{:S(2)}) collective-permute-start(f32[2,6,1,640]{3,2,1,0:T(1,128)} %slice.351), channel_id=1, source_target_pairs={{1,0},{2,1},{3,2},{4,3},{5,4},{6,5},{7,6},{8,7},{9,8},{10,9},{11,1... | collective-permute-start | bytes 92168 | tf_op jit(solution)/shard_map/ppermute | solution.py:13
  31.0 0.9 slice_bitcast_fusion.12
  31.8 0.8 slice_bitcast_fusion.22
  32.6 0.8 slice_bitcast_fusion.11
  33.5 0.8 slice_bitcast_fusion.20
  34.9 0.8 fusion.23
  35.7 0.8 slice.368
  36.5 0.7 slice.369
  37.3 0.1 slice.345
  37.4 0.7 slice.350
  38.1 0.3 copy-done.13
  38.5 0.9 copy-done.12
  39.4 0.8 slice.374
  40.2 1.7 slice.353
  41.9 0.8 slice.355
  42.8 1.3 dynamic-slice
  44.7 1.1 fusion.16
  45.8 0.1 copy-done.10
  45.9 0.1 copy-done.16
  46.0 0.1 copy-done.17
  46.1 0.9 fusion.21
  47.0 0.3 copy-done.18
  47.3 0.1 fusion.1
  47.4 0.1 slice_bitcast_fusion.5
  47.5 0.0 copy-start.8
  47.6 0.0 collective-permute-done
  47.6 0.7 copy-done.15
  48.3 0.1 copy-done.4
  48.5 0.1 copy-done.7
  48.6 0.1 copy-done.8
  48.7 0.1 copy-done.14
  48.8 0.2 subtract_subtract_fusion
  49.0 0.9 copy-done.2
  49.9 0.1 maximum_add_fusion
  50.0 0.8 slice_bitcast_fusion.8
  50.8 1.9 collective-permute-start.3
  52.8 1.9 collective-permute-start.1
  54.7 0.9 maximum_add_fusion.1
  55.7 0.4 collective-permute-done.3
  56.1 0.3 subtract_bitcast_fusion
  56.4 0.0 copy-start.21
  56.4 0.6 copy-done.3
  57.0 0.1 copy-done.21
  57.1 0.1 maximum_subtract_fusion
  57.2 0.8 fusion.3
  58.0 0.0 all-reduce.21.cloned.1.call-update
  58.0 0.9 copy-done.5
  58.9 0.1 copy-done.6
  59.0 0.3 subtract_bitcast_fusion.2
  59.3 1.0 fusion
  60.3 169.9 %all-reduce.21.cloned.1.call-done = (f32[6,16,640]{2,1,0:T(8,128)}, f32[6,16,640]{2,1,0:T(8,128)}) async-done(((f32[6,16,640]{2,1,0:T(8,128)}, f32[6,16,640]{2,1,0:T(8,128)}), (f32[6,16,640]{2,1,0:T(8,128)}, f32[6,16,640]{2,1,0:T(8,128)})) %all-reduce.21.cloned.1.call-update) | async-done | bytes 491536
  230.2 1.7 subtract_multiply_fusion
  (37 shorter events, 0.3 us)
Async XLA Ops:
  7.2 223.0 %all-reduce.21.cloned.1.call-start = ((), (), s32[]{:S(2)}) async-start(), calls=%async_computation | async-start | bytes 983040
  8.2 36.5 %collective-permute-start.2 = (f32[2,6,1,640]{3,2,1,0:T(1,128)S(1)}, f32[2,6,1,640]{3,2,1,0:T(1,128)S(1)}, u32[]{:S(2)}, u32[]{:S(2)}) collective-permute-start(f32[2,6,1,640]{3,2,1,0:T(1,128)S(1)} %slice.370), channel_id=1, source_target_pairs={{1,0},{2,1},{3,2},{4,3},{5,4},{6,5},{7,6},{8,7},{9,8},{10,9},{11,1... | collective-permute-start | bytes 92168 | tf_op jit(solution)/shard_map/ppermute | solution.py:13
  10.1 1.3 copy-start.19
  11.4 0.7 copy-start.20
  12.7 10.5 %copy-start = (f32[1,3,6,16,640]{4,3,2,1,0:T(8,128)S(1)}, f32[1,3,6,16,640]{4,3,2,1,0:T(8,128)}, u32[]{:S(2)}) copy-start(f32[1,3,6,16,640]{4,3,2,1,0:T(8,128)} %param.11) | copy-start | bytes 2211844
  23.2 7.7 %copy-start.1 = (f32[1,3,6,16,640]{4,3,2,1,0:T(8,128)S(1)}, f32[1,3,6,16,640]{4,3,2,1,0:T(8,128)}, u32[]{:S(2)}) copy-start(f32[1,3,6,16,640]{4,3,2,1,0:T(8,128)} %param.9) | copy-start | bytes 2211844
  23.9 23.7 %collective-permute-start = (f32[2,6,1,640]{3,2,1,0:T(1,128)}, f32[2,6,1,640]{3,2,1,0:T(1,128)S(1)}, u32[]{:S(2)}, u32[]{:S(2)}) collective-permute-start(f32[2,6,1,640]{3,2,1,0:T(1,128)} %slice.351), channel_id=1, source_target_pairs={{1,0},{2,1},{3,2},{4,3},{5,4},{6,5},{7,6},{8,7},{9,8},{10,9},{11,1... | collective-permute-start | bytes 92168 | tf_op jit(solution)/shard_map/ppermute | solution.py:13
  37.4 1.0 copy-start.13
  38.4 0.9 copy-start.12
  40.2 1.7 copy-start.11
  44.7 1.1 copy-start.9
  44.7 1.2 copy-start.10
  44.7 1.3 copy-start.16
  44.7 1.4 copy-start.17
  46.1 1.2 copy-start.18
  47.4 0.9 copy-start.15
  47.5 1.0 copy-start.4
  47.5 1.1 copy-start.7
  47.5 1.2 copy-start.8
  47.5 1.3 copy-start.14
  48.8 1.1 copy-start.2
  50.8 5.2 %collective-permute-start.3 = (f32[2,6,1,640]{3,2,1,0:T(1,128)S(1)}, f32[2,6,1,640]{3,2,1,0:T(1,128)S(1)}, u32[]{:S(2)}, u32[]{:S(2)}) collective-permute-start(f32[2,6,1,640]{3,2,1,0:T(1,128)S(1)} %slice.381), channel_id=1, source_target_pairs={{0,1},{1,2},{2,3},{3,4},{4,5},{5,6},{6,7},{7,8},{8,9},{9,10},{10,1... | collective-permute-start | bytes 92168 | tf_op jit(solution)/shard_map/ppermute | solution.py:13
  52.8 5.3 %collective-permute-start.1 = (f32[2,6,1,640]{3,2,1,0:T(1,128)S(1)}, f32[2,6,1,640]{3,2,1,0:T(1,128)S(1)}, u32[]{:S(2)}, u32[]{:S(2)}) collective-permute-start(f32[2,6,1,640]{3,2,1,0:T(1,128)S(1)} %slice.362), channel_id=1, source_target_pairs={{0,1},{1,2},{2,3},{3,4},{4,5},{5,6},{6,7},{7,8},{8,9},{9,10},{10,1... | collective-permute-start | bytes 92168 | tf_op jit(solution)/shard_map/ppermute | solution.py:13
  56.1 0.9 copy-start.3
  56.4 0.7 copy-start.21
  58.0 0.9 copy-start.5
  58.0 1.1 copy-start.6
Sparse Core Ops, SparseCore 0:
  58.1 172.0 all-reduce.20
where the time goes:
time: 240 us; the launch traced here: 239 us
  waiting for transfers between devices  170 us (71%)
  other arithmetic  20 us (8%)
  local copies, waits for them, and re-layouts  19.9 us (8%)
  between operations  15.7 us (7%)
  starting transfers between devices  12.8 us (5%)
    unnamed x2, waiting for transfers between devices  170 us
    ppermute x4, starting transfers between devices, from_behind(): lax.ppermute(value, axis, [(source, source + steps) for source in range(f...  12.8 us
    div x1, other arithmetic, on_device(): update_gain = (permittivity - HALF_STEP * conductivity) / denominator  10.4 us
    slice x10, local copies, waits for them, and re-layouts, step_ahead(): lax.slice_in_dim(values, 1, values.shape[dimension], axis=dimension)  7.37 us
    unnamed x45, local copies, waits for them, and re-layouts  6.92 us
  transfers between devices with their start and end apart: 5, of which 2 were waited for; matrix products, arithmetic and copies ran while one was open for 13% of the time, Pallas kernels for 0%

commit v1 on v0

--- a/solution.py
+++ b/solution.py
@@ -5,6 +5,7 @@
 
 TIMESTEP = 0.5
 HALF_STEP = 0.25
+PLANES = 3
 
 
 def from_behind(value, axis, steps):
@@ -101,14 +102,17 @@
     source = port_amplitude[0][:, None, None, None] * hits[None]
     drive = curl_magnetic(forward_magnetic, forward_rim[0], forward_rim[1]) - source
     corr_b = adj_field[0] * drive[0] + adj_field[1] * drive[1] + adj_field[2] * drive[2]
-    summed_a, summed_b = (
-        lax.psum_scatter(corr_a, "port", scatter_dimension=2, tiled=True),
-        lax.psum_scatter(corr_b, "port", scatter_dimension=2, tiled=True),
-    )
+    ports = lax.axis_size("port")
+    share = width // ports
+    groups = depth // PLANES
+    packed = jnp.stack([corr_a, corr_b]).reshape(2, groups, PLANES, columns, ports, share)
+    packed = packed.transpose(4, 0, 1, 3, 2, 5).reshape(ports, 2 * groups, columns, PLANES * share)
+    gathered = lax.all_to_all(packed, "port", 0, 0, tiled=True)
+    summed = jnp.sum(gathered, axis=0).reshape(2, groups, columns, PLANES, share)
+    summed_a, summed_b = summed.transpose(0, 1, 3, 2, 4).reshape(2, depth, columns, share)
     new_electric = update_gain[None] * adj_field - TIMESTEP * curl_magnetic(
         new_magnetic, adjoint_rim[0], adjoint_rim[1]
     )
-    share = width // lax.axis_size("port")
     begin = lax.axis_index("port") * share
     perm_share = lax.dynamic_slice_in_dim(permittivity, begin, share, 2)
     cond_share = lax.dynamic_slice_in_dim(conductivity, begin, share, 2)

time: 240 us -> 95.2 us (0.40)
  the two profiles are of different devices: /device:TPU:64 before, /device:TPU:48 now
where the time goes in v1:
time: 95.2 us; the launch traced here: 94.3 us
  local copies, waits for them, and re-layouts  29.2 us (31%)
  starting transfers between devices  25.7 us (27%)
  other arithmetic  22.9 us (24%)
  waiting for transfers between devices  14.7 us (15%)
  between operations  1.66 us (2%)
    ppermute x4, starting transfers between devices, from_behind(): lax.ppermute(value, axis, [(source, source + steps) for source in range(f...  18.1 us
    div x1, other arithmetic, on_device(): update_gain = (permittivity - HALF_STEP * conductivity) / denominator  10.9 us
    slice x10, local copies, waits for them, and re-layouts, step_ahead(): lax.slice_in_dim(values, 1, values.shape[dimension], axis=dimension)  8.89 us
    all_to_all x1, waiting for transfers between devices, on_device(): gathered = lax.all_to_all(packed, 'port', 0, 0, tiled=True)  8.22 us
    all_to_all x1, starting transfers between devices, on_device(): gathered = lax.all_to_all(packed, 'port', 0, 0, tiled=True)  7.61 us
    ppermute x4, waiting for transfers between devices, from_behind(): lax.ppermute(value, axis, [(source, source + steps) for source in range(f...  6.5 us
    add x2, local copies, waits for them, and re-layouts, on_device(): adj_field[0] * field[0] + adj_field[1] * field[1] + adj_field[2] * field[2]  4.06 us
    reshape x1, local copies, waits for them, and re-layouts, on_device(): packed.transpose(4, 0, 1, 3, 2, 5)  3.41 us
  transfers between devices with their start and end apart: 5, of which 2 were waited for; matrix products, arithmetic and copies ran while one was open for 48% of the time, Pallas kernels for 0%

profile of v1, /device:TPU:48, one launch (start us, length us, event | category | flops | bytes accessed | tf_op | source)
XLA Modules:
  0.0 94.3 jit_solution(9831579083463394359)
XLA Ops:
  0.6 0.0 copy-start
  0.6 1.6 %slice.372 = f32[2,6,1,640]{3,2,1,0:T(1,128)} slice(f32[3,6,16,640]{3,2,1,0:T(8,128)} %bitcast.191), slice={[1:3], [0:6], [0:1], [0:640]} | slice | bytes 61440 | tf_op jit(solution)/shard_map/slice | solution.py:89
  2.3 11.7 %collective-permute-start.2 = (f32[2,6,1,640]{3,2,1,0:T(1,128)}, f32[2,6,1,640]{3,2,1,0:T(1,128)S(1)}, u32[]{:S(2)}, u32[]{:S(2)}) collective-permute-start(f32[2,6,1,640]{3,2,1,0:T(1,128)} %slice.372), channel_id=1, source_target_pairs={{1,0},{2,1},{3,2},{4,3},{5,4},{6,5},{7,6},{8,7},{9,8},{10,9},{11,1... | collective-permute-start | bytes 92168 | tf_op jit(solution)/shard_map/ppermute | solution.py:14
  14.0 1.2 %broadcast_compare_fusion = (pred[6,16,640]{2,1,0:T(8,128)(4,1)S(1)}, pred[6,16,640]{2,1,0:T(8,128)(4,1)S(1)}, pred[6,16,640]{2,1,0:T(8,128)(4,1)S(1)}, pred[6,1...) fusion(s32[6,16,640]{2,1,0:T(8,128)} %param.13), kind=kLoop, calls=%fused_computation.68 | loop fusion | flops 491520 | bytes 737280 | tf_op jit(solution)/shard_map/eq | solution.py:82
  15.2 0.0 copy-start.1
  15.3 1.6 %fusion.24 = (f32[1]{0:T(128)}, f32[1]{0:T(128)}, f32[1]{0:T(128)}, f32[1]{0:T(128)}, f32[1]{0:T(128)}, /*index=5*/f32[1]{0:T(128)}, f32[1]{0:T(128)}, f32[1]{0:T(128)}) fusion(f32[8]{0:T(128)} %param.14), kind=kLoop, calls=%fused_computation.95 | loop fusion | bytes 64 | tf_op jit(solution)/shard_map/slice | solution.py:83
  16.9 1.6 %fusion.25 = (f32[1]{0:T(128)}, f32[1]{0:T(128)}, f32[1]{0:T(128)}, f32[1]{0:T(128)}, f32[1]{0:T(128)}, /*index=5*/f32[1]{0:T(128)}, f32[1]{0:T(128)}, f32[1]{0:T(128)}) fusion(f32[8]{0:T(128)} %param.15), kind=kLoop, calls=%fused_computation.96 | loop fusion | bytes 64 | tf_op jit(solution)/shard_map/slice | solution.py:84
  18.5 10.9 %subtract_divide_fusion = (f32[6,16,640]{2,1,0:T(8,128)}, f32[6,16,640]{2,1,0:T(8,128)S(1)}, f32[6,16,640]{2,1,0:T(8,128)S(1)}) fusion(pred[6,16,640]{2,1,0:T(8,128)(4,1)S(1)} %get-tuple-element.48, pred[6,16,640]{2,1,0:T(8,128)(4,1)S(1)} %get-tuple-element.47, pred[6,16,640]{2,1,0:T(8,128)(4,1)S(1)} %get-tuple-element.46, ...), kind=kLoop, calls=%fused_computation.51 | loop fusion | flops 1228800 | bytes 1228864 | tf_op jit(solution)/shard_map/div | solution.py:86
  29.4 0.7 copy-done.3
  30.1 0.1 copy-done.4
  30.2 0.0 copy-done
  30.2 0.1 bitcast_multiply_fusion
  30.3 0.6 slice.353
  30.9 2.6 %collective-permute-start = (f32[2,6,1,640]{3,2,1,0:T(1,128)}, f32[2,6,1,640]{3,2,1,0:T(1,128)}, u32[]{:S(2)}, u32[]{:S(2)}) collective-permute-start(f32[2,6,1,640]{3,2,1,0:T(1,128)} %slice.353), channel_id=1, source_target_pairs={{1,0},{2,1},{3,2},{4,3},{5,4},{6,5},{7,6},{8,7},{9,8},{10,9},{11,1... | collective-permute-start | bytes 92168 | tf_op jit(solution)/shard_map/ppermute | solution.py:14
  33.5 0.0 copy-done.1
  33.5 0.8 multiply_add_fusion
  34.3 0.8 slice_bitcast_fusion.19
  35.1 0.8 slice_bitcast_fusion.8
  35.9 0.8 slice_bitcast_fusion.17
  37.3 0.8 fusion.18
  38.1 0.8 slice.370
  39.0 0.7 slice.371
  39.7 0.1 slice.347
  39.8 0.7 slice.352
  40.5 0.7 slice.374
  41.2 0.8 slice.376
  42.0 2.4 %add.110 = f32[1,2,3,16,16,40]{5,4,3,2,1,0:T(8,128)} reshape(f32[1,1,6,16,640]{4,3,2,1,0:T(8,128)} %get-tuple-element.7) | data formatting | bytes 491520 | tf_op jit(solution)/shard_map/add | solution.py:78
  44.4 1.7 %copy.15 = f32[1,2,3,16,16,40]{5,2,3,1,0,4:T(4,128)S(1)} copy(f32[1,2,3,16,16,40]{5,4,3,2,1,0:T(8,128)} %add.110) | data formatting | bytes 491520 | tf_op jit(solution)/shard_map/add | solution.py:78
  46.1 1.7 %slice.355 = f32[6,15,640]{2,1,0:T(8,128)} slice(f32[6,16,640]{2,1,0:T(8,128)} %get-tuple-element.39), slice={[0:6], [1:16], [0:640]} | slice | bytes 460800 | tf_op jit(solution)/shard_map/slice | solution.py:19
  47.8 1.8 %slice.357 = f32[6,16,639]{2,1,0:T(8,128)} slice(f32[6,16,640]{2,1,0:T(8,128)} %get-tuple-element.38), slice={[0:6], [0:16], [1:640]} | slice | bytes 490752 | tf_op jit(solution)/shard_map/slice | solution.py:19
  49.5 0.0 collective-permute-done.2
  49.6 1.6 %subtract_bitcast_fusion.1 = (f32[1,6,16,640]{3,2,1,0:T(8,128)S(1)}, f32[1,6,16,640]{3,2,1,0:T(8,128)S(1)}, f32[1,6,16,640]{3,2,1,0:T(8,128)S(1)}) fusion(f32[5,16,640]{2,1,0:T(8,128)} %get-tuple-element.22, f32[6,16,639]{2,1,0:T(8,128)} %slice.370, f32[1,3,6,16,640]{4,3,2,1,0:T(8,128)S(1)} %copy-done.1, f32[6,1,640]{2,1,0:T(1,128)S(1)} %get-tuple-element.54, ...), kind=kLoop, calls=%fused_computation.47 | loop fusion | flops 675840 | bytes 2866432 | tf_op jit(solution)/shard_map/stack | solution.py:43
  51.2 0.0 copy-start.7
  51.2 0.0 copy-start.10
  51.2 0.1 fusion.1
  51.3 0.0 copy-start.2
  51.4 0.1 slice_bitcast_fusion.2
  51.5 0.0 collective-permute-done
  51.5 0.9 slice_bitcast_fusion.27
  52.4 0.0 copy-done.13
  52.4 0.2 subtract_subtract_fusion
  52.6 0.2 copy-done.2
  52.8 0.1 maximum_add_fusion
  52.9 0.8 slice_bitcast_fusion.5
  53.7 0.6 slice.364
  54.3 1.9 %collective-permute-start.3 = (f32[2,6,1,640]{3,2,1,0:T(1,128)S(1)}, f32[2,6,1,640]{3,2,1,0:T(1,128)S(1)}, u32[]{:S(2)}, u32[]{:S(2)}) collective-permute-start(f32[2,6,1,640]{3,2,1,0:T(1,128)S(1)} %slice.383), channel_id=1, source_target_pairs={{0,1},{1,2},{2,3},{3,4},{4,5},{5,6},{6,7},{7,8},{8,9},{9,10},{10,1... | collective-permute-start | bytes 92168 | tf_op jit(solution)/shard_map/ppermute | solution.py:14
  56.2 1.9 %collective-permute-start.1 = (f32[2,6,1,640]{3,2,1,0:T(1,128)}, f32[2,6,1,640]{3,2,1,0:T(1,128)}, u32[]{:S(2)}, u32[]{:S(2)}) collective-permute-start(f32[2,6,1,640]{3,2,1,0:T(1,128)} %slice.364), channel_id=1, source_target_pairs={{0,1},{1,2},{2,3},{3,4},{4,5},{5,6},{6,7},{7,8},{8,9},{9,10},{10,1... | collective-permute-start | bytes 92168 | tf_op jit(solution)/shard_map/ppermute | solution.py:14
  58.2 0.9 %maximum_add_fusion.1 = f32[1,3,6,16,640]{4,3,2,1,0:T(8,128)} fusion(f32[1,3,6,16,640]{4,3,2,1,0:T(8,128)S(1)} %copy-done.2, f32[1,1,6,16,640]{4,3,2,1,0:T(8,128)S(1)} %bitcast.199, f32[1,1,6,16,640]{4,3,2,1,0:T(8,128)S(1)} %bitcast.201, f32[1,1,6,16,640]{4,3,2,1,0:T(8,128)S(1)} %bitcast.197), kind=kLoop, calls=%fused_computation.4 | loop fusion | flops 552960 | bytes 2211840 | tf_op jit(solution)/shard_map/add | solution.py:92
  59.2 6.5 %collective-permute-done.3 = f32[2,6,1,640]{3,2,1,0:T(1,128)S(1)} collective-permute-done((f32[2,6,1,640]{3,2,1,0:T(1,128)S(1)}, f32[2,6,1,640]{3,2,1,0:T(1,128)S(1)}, u32[]{:S(2)}, u32[]{:S(2)}) %collective-permute-start.3) | collective-permute-done | bytes 30752 | tf_op jit(solution)/shard_map/ppermute | solution.py:14
  65.7 0.3 subtract_bitcast_fusion
  66.0 0.1 maximum_subtract_fusion
  66.1 0.8 fusion.2
  66.9 1.5 %stack.83 = f32[1,2,3,16,16,40]{5,4,3,2,1,0:T(8,128)S(1)} reshape(f32[1,6,16,640]{3,2,1,0:T(8,128)} %fusion.2) | data formatting | bytes 491520 | tf_op jit(solution)/shard_map/stack | solution.py:108
  68.4 0.5 copy.16
  68.9 2.0 %maximum_bitcast_fusion = f32[16,2,2,16,3,40]{5,4,3,2,1,0:T(4,128)} fusion(f32[1,2,3,16,16,40]{5,2,3,1,0,4:T(4,128)S(1)} %copy.16, f32[1,2,3,16,16,40]{5,2,3,1,0,4:T(4,128)S(1)} %copy.15), kind=kLoop, calls=%fused_computation | loop fusion | flops 122880 | bytes 983040 | tf_op jit(solution)/shard_map/transpose | solution.py:109
  71.0 3.4 %reshape.174 = f32[16,4,16,120]{3,2,1,0:T(8,128)} reshape(f32[16,2,2,16,3,40]{5,4,3,2,1,0:T(4,128)} %maximum_bitcast_fusion) | data formatting | bytes 983040 | tf_op jit(solution)/shard_map/reshape | solution.py:109
  74.4 7.6 %all-to-all-start = ((f32[16,4,16,120]{3,2,1,0:T(8,128)}), f32[16,4,16,120]{3,2,1,0:T(8,128)S(1)}, u32[]{:S(2)}, u32[]{:S(2)}) async-start(f32[16,4,16,120]{3,2,1,0:T(8,128)} %reshape.174), calls=%async_computation | async-start | bytes 1048576 | tf_op jit(solution)/shard_map/all_to_all | solution.py:110
  82.0 0.0 collective-permute-done.1
  82.0 0.8 slice_bitcast_fusion.25
  82.9 0.3 subtract_bitcast_fusion.2
  83.1 1.0 %fusion = f32[1,3,6,16,640]{4,3,2,1,0:T(8,128)} fusion(f32[1,1,6,16,640]{4,3,2,1,0:T(8,128)S(1)} %get-tuple-element.25, f32[1,1,6,16,640]{4,3,2,1,0:T(8,128)S(1)} %get-tuple-element.26, f32[1,1,6,16,640]{4,3,2,1,0:T(8,128)S(1)} %get-tuple-element.24, f32[1,3,6,16,640]{4,3,2,1,0:T(8,128)S(1)} %copy-done, f32[6,16,640]{2,1,0:T(8,128)S(1)} %copy-done.5), kind=kLoop, calls=%fused_computation.3 | loop fusion | flops 921600 | bytes 2457600 | tf_op jit(solution)/shard_map/sub | solution.py:113
  84.1 8.2 %all-to-all-done = f32[16,4,16,120]{3,2,1,0:T(8,128)S(1)} async-done(((f32[16,4,16,120]{3,2,1,0:T(8,128)}), f32[16,4,16,120]{3,2,1,0:T(8,128)S(1)}, u32[]{:S(2)}, u32[]{:S(2)}) %all-to-all-start) | async-done | bytes 491552 | tf_op jit(solution)/shard_map/all_to_all | solution.py:110
  92.4 0.1 reshape.175
  92.6 1.7 %fusion.22 = (f32[6,16,40]{2,1,0:T(8,128)}, f32[6,16,40]{2,1,0:T(8,128)}) fusion(f32[1,2,3,16,40]{4,3,2,1,0:T(8,128)S(1)} %copy.18, f32[1,2,3,16,40]{4,3,2,1,0:T(8,128)S(1)} %copy.17, f32[6,16,640]{2,1,0:T(8,128)} %copy-done.4, s32[]{:T(128)S(6)} %select_n.69, f32[6,16,640]{2,1,0:T(8,128)} %copy-done.3), kind=kLoop, calls=%fused_computation.80 | loop fusion | flops 46080 | bytes 92164 | tf_op jit(solution)/shard_map/mul | solution.py:122
  (33 shorter events, 0.3 us)
Async XLA Ops:
  0.6 29.6 %copy-start = (f32[1,3,6,16,640]{4,3,2,1,0:T(8,128)S(1)}, f32[1,3,6,16,640]{4,3,2,1,0:T(8,128)}, u32[]{:S(2)}) copy-start(f32[1,3,6,16,640]{4,3,2,1,0:T(8,128)} %param.11) | copy-start | bytes 2211844
  2.3 47.3 %collective-permute-start.2 = (f32[2,6,1,640]{3,2,1,0:T(1,128)}, f32[2,6,1,640]{3,2,1,0:T(1,128)S(1)}, u32[]{:S(2)}, u32[]{:S(2)}) collective-permute-start(f32[2,6,1,640]{3,2,1,0:T(1,128)} %slice.372), channel_id=1, source_target_pairs={{1,0},{2,1},{3,2},{4,3},{5,4},{6,5},{7,6},{8,7},{9,8},{10,9},{11,1... | collective-permute-start | bytes 92168 | tf_op jit(solution)/shard_map/ppermute | solution.py:14
  15.2 18.2 %copy-start.1 = (f32[1,3,6,16,640]{4,3,2,1,0:T(8,128)S(1)}, f32[1,3,6,16,640]{4,3,2,1,0:T(8,128)}, u32[]{:S(2)}) copy-start(f32[1,3,6,16,640]{4,3,2,1,0:T(8,128)} %param.9) | copy-start | bytes 2211844
  29.4 0.7 copy-start.3
  29.4 0.8 copy-start.4
  30.9 20.5 %collective-permute-start = (f32[2,6,1,640]{3,2,1,0:T(1,128)}, f32[2,6,1,640]{3,2,1,0:T(1,128)}, u32[]{:S(2)}, u32[]{:S(2)}) collective-permute-start(f32[2,6,1,640]{3,2,1,0:T(1,128)} %slice.353), channel_id=1, source_target_pairs={{1,0},{2,1},{3,2},{4,3},{5,4},{6,5},{7,6},{8,7},{9,8},{10,9},{11,1... | collective-permute-start | bytes 92168 | tf_op jit(solution)/shard_map/ppermute | solution.py:14
  49.5 1.7 %copy-start.14 = (f32[1,3,6,16,640]{4,3,2,1,0:T(8,128)S(1)}, f32[1,3,6,16,640]{4,3,2,1,0:T(8,128)}, u32[]{:S(2)}) copy-start(f32[1,3,6,16,640]{4,3,2,1,0:T(8,128)} %param.10) | copy-start | bytes 2211844
  51.2 1.2 %copy-start.7 = (f32[6,15,640]{2,1,0:T(8,128)S(1)}, f32[6,15,640]{2,1,0:T(8,128)}, u32[]{:S(2)}) copy-start(f32[6,15,640]{2,1,0:T(8,128)} %slice.352) | copy-start | bytes 691204
  51.2 1.2 %copy-start.10 = (f32[6,15,640]{2,1,0:T(8,128)S(1)}, f32[6,15,640]{2,1,0:T(8,128)}, u32[]{:S(2)}) copy-start(f32[6,15,640]{2,1,0:T(8,128)} %slice.355) | copy-start | bytes 691204
  51.2 1.2 %copy-start.11 = (f32[6,16,639]{2,1,0:T(8,128)S(1)}, f32[6,16,639]{2,1,0:T(8,128)}, u32[]{:S(2)}) copy-start(f32[6,16,639]{2,1,0:T(8,128)} %slice.357) | copy-start | bytes 736132
  51.2 1.2 %copy-start.12 = (f32[5,16,640]{2,1,0:T(8,128)S(1)}, f32[5,16,640]{2,1,0:T(8,128)}, u32[]{:S(2)}) copy-start(f32[5,16,640]{2,1,0:T(8,128)} %get-tuple-element.35) | copy-start | bytes 614404
  51.2 1.2 %copy-start.13 = (f32[5,16,640]{2,1,0:T(8,128)S(1)}, f32[5,16,640]{2,1,0:T(8,128)}, u32[]{:S(2)}) copy-start(f32[5,16,640]{2,1,0:T(8,128)} %get-tuple-element.36) | copy-start | bytes 614404
  51.3 1.4 %copy-start.2 = (f32[1,3,6,16,640]{4,3,2,1,0:T(8,128)S(1)}, f32[1,3,6,16,640]{4,3,2,1,0:T(8,128)}, u32[]{:S(2)}) copy-start(f32[1,3,6,16,640]{4,3,2,1,0:T(8,128)} %param.12) | copy-start | bytes 2211844
  54.3 11.3 %collective-permute-start.3 = (f32[2,6,1,640]{3,2,1,0:T(1,128)S(1)}, f32[2,6,1,640]{3,2,1,0:T(1,128)S(1)}, u32[]{:S(2)}, u32[]{:S(2)}) collective-permute-start(f32[2,6,1,640]{3,2,1,0:T(1,128)S(1)} %slice.383), channel_id=1, source_target_pairs={{0,1},{1,2},{2,3},{3,4},{4,5},{5,6},{6,7},{7,8},{8,9},{9,10},{10,1... | collective-permute-start | bytes 92168 | tf_op jit(solution)/shard_map/ppermute | solution.py:14
  56.2 25.8 %collective-permute-start.1 = (f32[2,6,1,640]{3,2,1,0:T(1,128)}, f32[2,6,1,640]{3,2,1,0:T(1,128)}, u32[]{:S(2)}, u32[]{:S(2)}) collective-permute-start(f32[2,6,1,640]{3,2,1,0:T(1,128)} %slice.364), channel_id=1, source_target_pairs={{0,1},{1,2},{2,3},{3,4},{4,5},{5,6},{6,7},{7,8},{8,9},{9,10},{10,1... | collective-permute-start | bytes 92168 | tf_op jit(solution)/shard_map/ppermute | solution.py:14
  59.1 6.8 %copy-start.6 = (f32[6,16,640]{2,1,0:T(8,128)S(1)}, f32[6,16,640]{2,1,0:T(8,128)}, u32[]{:S(2)}) copy-start(f32[6,16,640]{2,1,0:T(8,128)} %fusion.18) | copy-start | bytes 737284
  59.1 6.9 %copy-start.15 = (f32[1,3]{1,0:T(1,128)S(1)}, f32[1,3]{1,0:T(1,128)}, u32[]{:S(2)}) copy-start(f32[1,3]{1,0:T(1,128)} %param.17) | copy-start | bytes 40
  71.0 11.9 %copy-start.8 = (f32[6,16,640]{2,1,0:T(8,128)S(1)}, f32[6,16,640]{2,1,0:T(8,128)}, u32[]{:S(2)}) copy-start(f32[6,16,640]{2,1,0:T(8,128)} %get-tuple-element.30) | copy-start | bytes 737284
  71.0 11.9 %copy-start.9 = (f32[6,16,640]{2,1,0:T(8,128)S(1)}, f32[6,16,640]{2,1,0:T(8,128)}, u32[]{:S(2)}) copy-start(f32[6,16,640]{2,1,0:T(8,128)} %get-tuple-element.31) | copy-start | bytes 737284
  74.4 18.0 %all-to-all-start = ((f32[16,4,16,120]{3,2,1,0:T(8,128)}), f32[16,4,16,120]{3,2,1,0:T(8,128)S(1)}, u32[]{:S(2)}, u32[]{:S(2)}) async-start(f32[16,4,16,120]{3,2,1,0:T(8,128)} %reshape.174), calls=%async_computation | async-start | bytes 1048576 | tf_op jit(solution)/shard_map/all_to_all | solution.py:110
  82.0 1.2 %copy-start.5 = (f32[6,16,640]{2,1,0:T(8,128)S(1)}, f32[6,16,640]{2,1,0:T(8,128)}, u32[]{:S(2)}) copy-start(f32[6,16,640]{2,1,0:T(8,128)} %get-tuple-element.4) | copy-start | bytes 737284

commit v2 on v0

v2 whole, which is shorter than its diff:
```python
import functools

import jax
import jax.numpy as jnp
from jax import lax
from jax.experimental import pallas as pl
from jax.experimental.pallas import tpu as pltpu
from jax.sharding import PartitionSpec as P

TIMESTEP = 0.5
HALF_STEP = 0.25
PLANES = 3
LANES = 128
VMEM = pltpu.VMEM
SMEM = pltpu.SMEM


def from_behind(value, axis, steps):
    count = lax.axis_size(axis)
    first, last = (max(0, -steps), min(count, count - steps))
    return lax.ppermute(value, axis, [(source, source + steps) for source in range(first, last)])


def lane_iota(shape):
    return lax.broadcasted_iota(jnp.int32, shape, len(shape) - 1)


def row_iota(shape):
    return lax.broadcasted_iota(jnp.int32, shape, len(shape) - 2)


def lane_next(value):
    width = value.shape[1]
    return jnp.where(lane_iota(value.shape) == width - 1, 0.0, pltpu.roll(value, width - 1, 1))


def lane_prev(value):
    return jnp.where(lane_iota(value.shape) == 0, 0.0, pltpu.roll(value, 1, 1))


def row_next(value, beyond):
    rows = value.shape[0]
    return jnp.where(row_iota(value.shape) == rows - 1, beyond, pltpu.roll(value, rows - 1, 0))


def row_prev(value, before):
    return jnp.where(row_iota(value.shape) == 0, before, pltpu.roll(value, 1, 0))


def look_up(labels, entries):
    count = len(entries)
    level = list(entries)
    bit = 1
    while len(level) > 1:
        odd = (labels & bit) != 0
        level = [
            jnp.where(odd, level[i + 1], level[i]) if i + 1 < len(level) else level[i]
            for i in range(0, len(level), 2)
        ]
        bit *= 2
    assert count <= bit
    return level[0]


def region_values(perm_ref, cond_ref):
    shape = (1, LANES)
    perm = [jnp.full(shape, perm_ref[r], jnp.float32) for r in range(perm_ref.shape[0])]
    cond = [jnp.full(shape, cond_ref[r], jnp.float32) for r in range(cond_ref.shape[0])]
    return perm, cond


def widen(entries, width):
    return [jnp.concatenate([entry] * (width // LANES), axis=1) for entry in entries]


def gains(perm_ref, cond_ref, width):
    perm, cond = region_values(perm_ref, cond_ref)
    denominator = [p + HALF_STEP * c for p, c in zip(perm, cond, strict=True)]
    source = [TIMESTEP / d for d in denominator]
    update = [(p - HALF_STEP * c) / d for p, c, d in zip(perm, cond, denominator, strict=True)]
    return widen(source, width), widen(update, width)


def edge_kernel(e, m, ae, am, labels, perm, cond, up, down):
    depth, rows, width = labels.shape
    source, _ = gains(perm, cond, width)
    last = rows - 1

    def row(ref, c, z, r):
        if z == depth:
            return jnp.zeros((1, width), jnp.float32)
        return ref[0, c, z, r : r + 1, :]

    scaled = []
    for z in range(depth):
        gain = look_up(labels[z, last : last + 1, :], source)
        scaled.append([gain * row(ae, c, z, last) for c in range(3)])
    scaled.append([jnp.zeros((1, width), jnp.float32)] * 3)
    for z in range(depth):
        ex, ey, ez = (row(e, c, z, last) for c in range(3))
        sx, sy, sz = scaled[z]
        up[z : z + 1, :] = row(m, 1, z, last) - TIMESTEP * ((row(e, 0, z + 1, last) - ex) + ez)
        up[depth + z : depth + z + 1, :] = row(m, 2, z, last) + TIMESTEP * (ey + (lane_next(ex) - ex))
        up[2 * depth + z : 2 * depth + z + 1, :] = row(am, 1, z, last) + ((scaled[z + 1][0] - sx) + sz)
        up[3 * depth + z : 3 * depth + z + 1, :] = row(am, 2, z, last) - (sy + (lane_next(sx) - sx))
        gain = look_up(labels[z, 0:1, :], source)
        down[z : z + 1, :] = row(e, 1, z, 0)
        down[depth + z : depth + z + 1, :] = row(e, 2, z, 0)
        down[2 * depth + z : 2 * depth + z + 1, :] = gain * row(ae, 1, z, 0)
        down[3 * depth + z : 3 * depth + z + 1, :] = gain * row(ae, 2, z, 0)


def pack(planes, share, ports):
    rows = planes[0].shape[0]
    lane = lane_iota((rows, LANES))
    blocks = []
    for port in range(ports):
        tile, offset = divmod(port * share, LANES)
        pieces = []
        for j, plane in enumerate(planes):
            piece = plane[:, tile * LANES : (tile + 1) * LANES]
            if offset + share > LANES:
                piece = jnp.where(
                    lane >= offset, piece, plane[:, (tile + 1) * LANES : (tile + 2) * LANES]
                )
            shift = (j * share - offset) % LANES
            pieces.append(pltpu.roll(piece, shift, 1) if shift else piece)
        block = pieces[-1]
        for j in range(len(planes) - 2, -1, -1):
            block = jnp.where(lane < (j + 1) * share, pieces[j], block)
        blocks.append(block)
    return blocks


def correlation_kernel(ports, e, m, ae, above, below, cells, amplitude, packed):
    _, _, depth, rows, width = e.shape
    share = width // ports
    tile = lax.axis_index("tile")
    plane_cells = lax.axis_size("tile") * rows * width
    target = cells[0] - tile * (rows * width)
    inside = jnp.where(tile > 0, 1.0, 0.0)
    position = row_iota((rows, width)) * width + lane_iota((rows, width))

    def at(ref, c, z):
        return ref[0, c, z] if z < depth else jnp.zeros((rows, width), jnp.float32)

    zero = jnp.zeros((rows, width), jnp.float32)
    fx_prev, fy_prev = zero, zero
    sums_a, sums_b = [], []
    for z in range(depth):
        ex, ey, ez = (at(e, c, z) for c in range(3))
        next_y, next_z = below[z : z + 1, :], below[depth + z : depth + z + 1, :]
        fx = at(m, 0, z) - TIMESTEP * ((lane_next(ez) - ez) - (at(e, 1, z + 1) - ey))
        fy = at(m, 1, z) - TIMESTEP * ((at(e, 0, z + 1) - ex) - (row_next(ez, next_z) - ez))
        fz = at(m, 2, z) - TIMESTEP * ((row_next(ey, next_y) - ey) - (lane_next(ex) - ex))
        prev_y = inside * (above[z : z + 1, :] + TIMESTEP * ez[0:1])
        prev_z = inside * (above[depth + z : depth + z + 1, :] - TIMESTEP * ey[0:1])
        hit = position == target - z * plane_cells
        drive_x = ((fz - lane_prev(fz)) - (fy - fy_prev)) - jnp.where(hit, amplitude[0, 0], 0.0)
        drive_y = ((fx - fx_prev) - (fz - row_prev(fz, prev_z))) - jnp.where(hit, amplitude[0, 1], 0.0)
        drive_z = ((fy - row_prev(fy, prev_y)) - (fx - lane_prev(fx))) - jnp.where(
            hit, amplitude[0, 2], 0.0
        )
        ax, ay, az = (at(ae, c, z) for c in range(3))
        sums_a.append(ax * ex + ay * ey + az * ez)
        sums_b.append(ax * drive_x + ay * drive_y + az * drive_z)
        fx_prev, fy_prev = fx, fy
        if z % PLANES == PLANES - 1:
            group = z // PLANES
            for f, sums in enumerate((sums_a, sums_b)):
                for port, block in enumerate(pack(sums, share, ports)):
                    packed[port, f * (depth // PLANES) + group] = block
            sums_a, sums_b = [], []


def field_kernel(ae, am, labels, above, below, perm, cond, new_e, new_m):
    depth, rows, width = labels.shape
    source, update = gains(perm, cond, width)
    inside = jnp.where(lax.axis_index("tile") > 0, 1.0, 0.0)
    zero = jnp.zeros((rows, width), jnp.float32)

    def scaled(z):
        if z == depth:
            return [zero] * 3
        gain = look_up(labels[z], source)
        return [gain * ae[0, c, z] for c in range(3)]

    nx_prev, ny_prev = zero, zero
    here = scaled(0)
    for z in range(depth):
        after = scaled(z + 1)
        sx, sy, sz = here
        next_y = below[2 * depth + z : 2 * depth + z + 1, :]
        next_z = below[3 * depth + z : 3 * depth + z + 1, :]
        nx = am[0, 0, z] + ((lane_next(sz) - sz) - (after[1] - sy))
        ny = am[0, 1, z] + ((after[0] - sx) - (row_next(sz, next_z) - sz))
        nz = am[0, 2, z] + ((row_next(sy, next_y) - sy) - (lane_next(sx) - sx))
        prev_y = inside * (above[2 * depth + z : 2 * depth + z + 1, :] - sz[0:1])
        prev_z = inside * (above[3 * depth + z : 3 * depth + z + 1, :] + sy[0:1])
        new_m[0, 0, z] = nx
        new_m[0, 1, z] = ny
        new_m[0, 2, z] = nz
        gain = look_up(labels[z], update)
        new_e[0, 0, z] = gain * ae[0, 0, z] - TIMESTEP * ((nz - lane_prev(nz)) - (ny - ny_prev))
        new_e[0, 1, z] = gain * ae[0, 1, z] - TIMESTEP * ((nx - nx_prev) - (nz - row_prev(nz, prev_z)))
        new_e[0, 2, z] = gain * ae[0, 2, z] - TIMESTEP * ((ny - row_prev(ny, prev_y)) - (nx - lane_prev(nx)))
        nx_prev, ny_prev = nx, ny
        here = after


def gradient_kernel(gathered, labels, perm, cond, grad_perm, grad_cond):
    ports, slabs, rows, _ = gathered.shape
    depth, _, share = grad_perm.shape
    width = labels.shape[2]
    groups = depth // PLANES
    begin = lax.axis_index("port") * share
    perms, conds = region_values(perm, cond)
    denominators = [p + HALF_STEP * c for p, c in zip(perms, conds, strict=True)]
    factors = [TIMESTEP / (d * d) for d in denominators]
    sums = []
    for slab in range(slabs):
        total = gathered[0, slab]
        for port in range(1, ports):
            total = total + gathered[port, slab]
        sums.append(total)
    for z in range(depth):
        group, j = divmod(z, PLANES)
        corr_a, corr_b = (
            pltpu.roll(sums[f * groups + group], (LANES - j * share) % LANES, 1) if j else sums[f * groups + group]
            for f in range(2)
        )
        mine = pltpu.roll(labels[z], lax.rem(width - begin, width), 1)[:, :LANES]
        factor = look_up(mine, factors)
        permittivity = look_up(mine, perms)
        conductivity = look_up(mine, conds)
        by_perm = factor * (conductivity * corr_a - corr_b)
        by_cond = factor * (-permittivity * corr_a - HALF_STEP * corr_b)
        grad_perm[z] = by_perm[:, :share]
        grad_cond[z] = by_cond[:, :share]


def spec(space):
    return pl.BlockSpec(memory_space=space)


def call(kernel, inputs, spaces, outs, flops, moved):
    return pl.pallas_call(
        kernel,
        out_shape=outs,
        in_specs=[spec(space) for space in spaces],
        out_specs=jax.tree.map(lambda _: spec(VMEM), outs),
        cost_estimate=pl.CostEstimate(flops=flops, bytes_accessed=moved, transcendentals=0),
    )(*inputs)


def on_device(
    electric,
    magnetic,
    adjoint_electric,
    adjoint_magnetic,
    region_labels,
    permittivity_table,
    conductivity_table,
    port_cells,
    port_amplitude,
):
    depth, rows, width = region_labels.shape
    ports = lax.axis_size("port")
    share = width // ports
    cells = depth * rows * width

    def array(*shape):
        return jax.ShapeDtypeStruct(shape, jnp.float32)

    edge = array(4 * depth, width)
    up, down = call(
        edge_kernel,
        (electric, magnetic, adjoint_electric, adjoint_magnetic, region_labels, permittivity_table, conductivity_table),
        (VMEM,) * 5 + (SMEM,) * 2,
        (edge, edge),
        10 * cells,
        cells * 4,
    )
    below = from_behind(down, "tile", -1)
    above = from_behind(up, "tile", 1)
    packed = call(
        functools.partial(correlation_kernel, ports),
        (electric, magnetic, adjoint_electric, above, below, port_cells, port_amplitude),
        (VMEM,) * 5 + (SMEM,) * 2,
        array(ports, 2 * depth // PLANES, rows, LANES),
        60 * cells,
        cells * 4 * 11,
    )
    gathered = lax.all_to_all(packed, "port", 0, 0, tiled=True)
    new_electric, new_magnetic = call(
        field_kernel,
        (adjoint_electric, adjoint_magnetic, region_labels, above, below, permittivity_table, conductivity_table),
        (VMEM,) * 5 + (SMEM,) * 2,
        (array(1, 3, depth, rows, width), array(1, 3, depth, rows, width)),
        80 * cells,
        cells * 4 * 13,
    )
    gradient = array(depth, rows, share)
    gradient_perm, gradient_cond = call(
        gradient_kernel,
        (gathered, region_labels, permittivity_table, conductivity_table),
        (VMEM,) * 2 + (SMEM,) * 2,
        (gradient, gradient),
        4 * cells,
        cells * 4 * 3,
    )
    return (new_electric, new_magnetic, gradient_perm, gradient_cond)


def solution(mesh):
    return jax.shard_map(
        on_device,
        mesh=mesh,
        in_specs=(
            P("port", None, None, "tile", None),
            P("port", None, None, "tile", None),
            P("port", None, None, "tile", None),
            P("port", None, None, "tile", None),
            P(None, "tile", None),
            P(),
            P(),
            P("port"),
            P("port", None),
        ),
        out_specs=(
            P("port", None, None, "tile", None),
            P("port", None, None, "tile", None),
            P(None, "tile", "port"),
            P(None, "tile", "port"),
        ),
        check_vma=False,
    )
```

time: 240 us -> 44.3 us (0.18)
  the two profiles are of different devices: /device:TPU:64 before, /device:TPU:48 now
where the time goes in v2:
time: 44.3 us; the launch traced here: 43.9 us
  starting transfers between devices  21 us (47%)
  Pallas kernels  11.2 us (25%)
  waiting for transfers between devices  9.01 us (20%)
  local copies, waits for them, and re-layouts  1.41 us (3%)
  between operations  1.31 us (3%)
    ppermute x2, starting transfers between devices, from_behind(): lax.ppermute(value, axis, [(source, source + steps) for source in range(f...  13.6 us
    pallas_call x4, Pallas kernels, call(): pl.pallas_call(kernel, out_shape=outs, in_specs=[spec(space) for space in...  11.2 us
    all_to_all x1, starting transfers between devices, on_device(): gathered = lax.all_to_all(packed, 'port', 0, 0, tiled=True)  7.35 us
    all_to_all x1, waiting for transfers between devices, on_device(): gathered = lax.all_to_all(packed, 'port', 0, 0, tiled=True)  7.18 us
    ppermute x2, waiting for transfers between devices, from_behind(): lax.ppermute(value, axis, [(source, source + steps) for source in range(f...  1.83 us
    unnamed x6, local copies, waits for them, and re-layouts  1.41 us
  transfers between devices with their start and end apart: 3, of which 2 were waited for; matrix products, arithmetic and copies ran while one was open for 0% of the time, Pallas kernels for 7%

profile of v2, /device:TPU:48, one launch (start us, length us, event | category | flops | bytes accessed | tf_op | source)
XLA Modules:
  0.0 43.9 jit_solution(12595914716499119938)
XLA Ops:
  0.6 2.7 %shard_map.120 = (f32[24,640]{1,0:T(8,128)}, f32[24,640]{1,0:T(8,128)}) custom-call(f32[1,3,6,16,640]{4,3,2,1,0:T(8,128)} %e.3, f32[1,3,6,16,640]{4,3,2,1,0:T(8,128)} %m.3, f32[1,3,6,16,640]{4,3,2,1,0:T(8,128)} %ae.5, f32[1,3,6,16,640]{4,3,2,1,0:T(8,128)} %am.3, s32[6,16,640]{2,1,0:T(8,128)} %labels.5, f32[8]{0:T(128)} %perm.5, f32[8]{0:T(128)} %cond.5), custom_call_target="tpu_custom_call" | custom-call | flops 614400 | bytes 245760 | tf_op jit(solution)/shard_map/pallas_call | solution.py:247
  3.3 1.9 %collective-permute-start = (f32[24,640]{1,0:T(8,128)}, f32[24,640]{1,0:T(8,128)S(1)}, u32[]{:S(2)}, u32[]{:S(2)}) collective-permute-start(f32[24,640]{1,0:T(8,128)} %get-tuple-element.10), channel_id=1, source_target_pairs={{0,1},{1,2},{2,3},{3,4},{4,5},{5,6},{6,7},{7,8},{8,9},{9,10},{10,1... | collective-permute-start | bytes 184328 | tf_op jit(solution)/shard_map/ppermute | solution.py:21
  5.2 11.7 %collective-permute-start.1 = (f32[24,640]{1,0:T(8,128)}, f32[24,640]{1,0:T(8,128)S(1)}, u32[]{:S(2)}, u32[]{:S(2)}) collective-permute-start(f32[24,640]{1,0:T(8,128)} %get-tuple-element.11), channel_id=1, source_target_pairs={{1,0},{2,1},{3,2},{4,3},{5,4},{6,5},{7,6},{8,7},{9,8},{10,9},{11,1... | collective-permute-start | bytes 184328 | tf_op jit(solution)/shard_map/ppermute | solution.py:21
  17.6 0.0 collective-permute-done.above
  17.6 0.0 copy-start.1
  17.6 1.8 %collective-permute-done.1.below = f32[24,640]{1,0:T(8,128)S(1)} collective-permute-done((f32[24,640]{1,0:T(8,128)}, f32[24,640]{1,0:T(8,128)S(1)}, u32[]{:S(2)}, u32[]{:S(2)}) %collective-permute-start.1) | collective-permute-done | bytes 61472 | tf_op jit(solution)/shard_map/ppermute | solution.py:21
  19.4 0.0 copy-done.1
  19.4 0.0 copy-start.2
  19.4 0.6 %copy-done.2 = f32[24,640]{1,0:T(8,128)} copy-done((f32[24,640]{1,0:T(8,128)}, f32[24,640]{1,0:T(8,128)S(1)}, u32[]{:S(2)}) %copy-start.2) | copy-done | bytes 61464
  20.1 3.4 %shard_map.122 = f32[16,4,16,128]{3,2,1,0:T(8,128)} custom-call(f32[1,3,6,16,640]{4,3,2,1,0:T(8,128)} %e.3, f32[1,3,6,16,640]{4,3,2,1,0:T(8,128)} %m.3, f32[1,3,6,16,640]{4,3,2,1,0:T(8,128)} %ae.5, f32[24,640]{1,0:T(8,128)} %copy-done.1, f32[24,640]{1,0:T(8,128)} %copy-done.2, s32[1]{0:T(128)S(6)} %copy.13.cells, f32[1,3]{1,0:T(1,128)} %amplitude.1), custom_call_target="tpu_custom_call" | custom-call | flops 3686400 | bytes 2703360 | tf_op jit(solution)/shard_map/pallas_call | solution.py:247
  23.5 7.4 %all-to-all-start = ((f32[16,4,16,128]{3,2,1,0:T(8,128)}), f32[16,4,16,128]{3,2,1,0:T(8,128)S(1)}, u32[]{:S(2)}, u32[]{:S(2)}) async-start(f32[16,4,16,128]{3,2,1,0:T(8,128)} %shard_map.122), calls=%async_computation | async-start | bytes 1048576 | tf_op jit(solution)/shard_map/all_to_all | solution.py:294
  30.8 3.2 %shard_map.121 = (f32[1,3,6,16,640]{4,3,2,1,0:T(8,128)}, f32[1,3,6,16,640]{4,3,2,1,0:T(8,128)}) custom-call(f32[1,3,6,16,640]{4,3,2,1,0:T(8,128)} %ae.5, f32[1,3,6,16,640]{4,3,2,1,0:T(8,128)} %am.3, s32[6,16,640]{2,1,0:T(8,128)} %labels.5, f32[24,640]{1,0:T(8,128)} %copy-done.1, f32[24,640]{1,0:T(8,128)} %copy-done.2, f32[8]{0:T(128)} %perm.5, f32[8]{0:T(128)} %cond.5), custom_call_target="tpu_custom_call" | custom-call | flops 4915200 | bytes 3194880 | tf_op jit(solution)/shard_map/pallas_call | solution.py:247
  34.0 7.2 %all-to-all-done.gathered = f32[16,4,16,128]{3,2,1,0:T(8,128)S(1)} async-done(((f32[16,4,16,128]{3,2,1,0:T(8,128)}), f32[16,4,16,128]{3,2,1,0:T(8,128)S(1)}, u32[]{:S(2)}, u32[]{:S(2)}) %all-to-all-start) | async-done | bytes 524320 | tf_op jit(solution)/shard_map/all_to_all | solution.py:294
  41.2 0.0 copy-start
  41.2 0.8 %copy-done = f32[16,4,16,128]{3,2,1,0:T(8,128)} copy-done((f32[16,4,16,128]{3,2,1,0:T(8,128)}, f32[16,4,16,128]{3,2,1,0:T(8,128)S(1)}, u32[]{:S(2)}) %copy-start) | copy-done | bytes 524312
  42.0 1.9 %shard_map.123 = (f32[6,16,40]{2,1,0:T(8,128)}, f32[6,16,40]{2,1,0:T(8,128)}) custom-call(f32[16,4,16,128]{3,2,1,0:T(8,128)} %copy-done, s32[6,16,640]{2,1,0:T(8,128)} %labels.5, f32[8]{0:T(128)} %perm.5, f32[8]{0:T(128)} %cond.5), custom_call_target="tpu_custom_call" | custom-call | flops 245760 | bytes 737280 | tf_op jit(solution)/shard_map/pallas_call | solution.py:247
Async XLA Ops:
  3.3 14.3 %collective-permute-start = (f32[24,640]{1,0:T(8,128)}, f32[24,640]{1,0:T(8,128)S(1)}, u32[]{:S(2)}, u32[]{:S(2)}) collective-permute-start(f32[24,640]{1,0:T(8,128)} %get-tuple-element.10), channel_id=1, source_target_pairs={{0,1},{1,2},{2,3},{3,4},{4,5},{5,6},{6,7},{7,8},{8,9},{9,10},{10,1... | collective-permute-start | bytes 184328 | tf_op jit(solution)/shard_map/ppermute | solution.py:21
  5.2 14.2 %collective-permute-start.1 = (f32[24,640]{1,0:T(8,128)}, f32[24,640]{1,0:T(8,128)S(1)}, u32[]{:S(2)}, u32[]{:S(2)}) collective-permute-start(f32[24,640]{1,0:T(8,128)} %get-tuple-element.11), channel_id=1, source_target_pairs={{1,0},{2,1},{3,2},{4,3},{5,4},{6,5},{7,6},{8,7},{9,8},{10,9},{11,1... | collective-permute-start | bytes 184328 | tf_op jit(solution)/shard_map/ppermute | solution.py:21
  17.6 1.8 %copy-start.1 = (f32[24,640]{1,0:T(8,128)}, f32[24,640]{1,0:T(8,128)S(1)}, u32[]{:S(2)}) copy-start(f32[24,640]{1,0:T(8,128)S(1)} %collective-permute-done.above) | copy-start | bytes 184324
  19.4 0.6 %copy-start.2 = (f32[24,640]{1,0:T(8,128)}, f32[24,640]{1,0:T(8,128)S(1)}, u32[]{:S(2)}) copy-start(f32[24,640]{1,0:T(8,128)S(1)} %collective-permute-done.1.below) | copy-start | bytes 184324
  23.5 17.7 %all-to-all-start = ((f32[16,4,16,128]{3,2,1,0:T(8,128)}), f32[16,4,16,128]{3,2,1,0:T(8,128)S(1)}, u32[]{:S(2)}, u32[]{:S(2)}) async-start(f32[16,4,16,128]{3,2,1,0:T(8,128)} %shard_map.122), calls=%async_computation | async-start | bytes 1048576 | tf_op jit(solution)/shard_map/all_to_all | solution.py:294
  41.2 0.8 %copy-start = (f32[16,4,16,128]{3,2,1,0:T(8,128)}, f32[16,4,16,128]{3,2,1,0:T(8,128)S(1)}, u32[]{:S(2)}) copy-start(f32[16,4,16,128]{3,2,1,0:T(8,128)S(1)} %all-to-all-done.gathered) | copy-start | bytes 1572868

commit v3 on v2

--- a/solution.py
+++ b/solution.py
@@ -13,12 +13,13 @@
 LANES = 128
 VMEM = pltpu.VMEM
 SMEM = pltpu.SMEM
-
-
-def from_behind(value, axis, steps):
-    count = lax.axis_size(axis)
-    first, last = (max(0, -steps), min(count, count - steps))
-    return lax.ppermute(value, axis, [(source, source + steps) for source in range(first, last)])
+ANY = pl.ANY
+HBM_BLOCK = None
+
+
+def swap(value, axis, first):
+    pairs = range(first, lax.axis_size(axis) - 1, 2)
+    return lax.ppermute(value, axis, [(i, i + 1) for i in pairs] + [(i + 1, i) for i in pairs])
 
 
 def lane_iota(shape):
@@ -81,33 +82,63 @@
     return widen(source, width), widen(update, width)
 
 
-def edge_kernel(e, m, ae, am, labels, perm, cond, up, down):
-    depth, rows, width = labels.shape
+def edge_kernel(e, m, ae, am, labels, perm, cond, near, far, e_last, m_last, ae_last, am_last, e_first, ae_first, marks, sems):
+    _, _, depth, rows, width = e.shape
+    last = rows - 1
+    moves = (
+        (ae.at[0, :, :, pl.ds(last, 1)], ae_last),
+        (ae.at[0, pl.ds(1, 2), :, pl.ds(0, 1)], ae_first),
+        (labels.at[:, pl.ds(last, 1)], marks.at[0]),
+        (labels.at[:, pl.ds(0, 1)], marks.at[1]),
+        (e.at[0, :, :, pl.ds(last, 1)], e_last),
+        (e.at[0, pl.ds(1, 2), :, pl.ds(0, 1)], e_first),
+        (m.at[0, pl.ds(1, 2), :, pl.ds(last, 1)], m_last),
+        (am.at[0, pl.ds(1, 2), :, pl.ds(last, 1)], am_last),
+    )
+    copies = [pltpu.make_async_copy(src, dst, sems.at[i]) for i, (src, dst) in enumerate(moves)]
+    for copy in copies:
+        copy.start()
     source, _ = gains(perm, cond, width)
-    last = rows - 1
-
-    def row(ref, c, z, r):
-        if z == depth:
-            return jnp.zeros((1, width), jnp.float32)
-        return ref[0, c, z, r : r + 1, :]
+    odd = lax.rem(lax.axis_index("tile"), 2) == 1
+    for copy in copies:
+        copy.wait()
+    zero = jnp.zeros((1, width), jnp.float32)
+
+    def row(ref, c, z):
+        return ref[c, z] if z < depth else zero
 
     scaled = []
     for z in range(depth):
-        gain = look_up(labels[z, last : last + 1, :], source)
-        scaled.append([gain * row(ae, c, z, last) for c in range(3)])
-    scaled.append([jnp.zeros((1, width), jnp.float32)] * 3)
-    for z in range(depth):
-        ex, ey, ez = (row(e, c, z, last) for c in range(3))
+        gain = look_up(marks[0, z], source)
+        scaled.append([gain * row(ae_last, c, z) for c in range(3)])
+    scaled.append([zero] * 3)
+    for z in range(depth):
+        ex, ey, ez = (row(e_last, c, z) for c in range(3))
         sx, sy, sz = scaled[z]
-        up[z : z + 1, :] = row(m, 1, z, last) - TIMESTEP * ((row(e, 0, z + 1, last) - ex) + ez)
-        up[depth + z : depth + z + 1, :] = row(m, 2, z, last) + TIMESTEP * (ey + (lane_next(ex) - ex))
-        up[2 * depth + z : 2 * depth + z + 1, :] = row(am, 1, z, last) + ((scaled[z + 1][0] - sx) + sz)
-        up[3 * depth + z : 3 * depth + z + 1, :] = row(am, 2, z, last) - (sy + (lane_next(sx) - sx))
-        gain = look_up(labels[z, 0:1, :], source)
-        down[z : z + 1, :] = row(e, 1, z, 0)
-        down[depth + z : depth + z + 1, :] = row(e, 2, z, 0)
-        down[2 * depth + z : 2 * depth + z + 1, :] = gain * row(ae, 1, z, 0)
-        down[3 * depth + z : 3 * depth + z + 1, :] = gain * row(ae, 2, z, 0)
+        gain = look_up(marks[1, z], source)
+        up = (
+            m_last[0, z] - TIMESTEP * ((row(e_last, 0, z + 1) - ex) + ez),
+            m_last[1, z] + TIMESTEP * (ey + (lane_next(ex) - ex)),
+            am_last[0, z] + ((scaled[z + 1][0] - sx) + sz),
+            am_last[1, z] - (sy + (lane_next(sx) - sx)),
+        )
+        down = (e_first[0, z], e_first[1, z], gain * ae_first[0, z], gain * ae_first[1, z])
+        for i, (above, below) in enumerate(zip(up, down, strict=True)):
+            at = i * depth + z
+            near[at : at + 1, :] = jnp.where(odd, below, above)
+            far[at : at + 1, :] = jnp.where(odd, above, below)
+
+
+def from_tiles(near, far):
+    odd = lax.rem(lax.axis_index("tile"), 2) == 1
+
+    def above(i):
+        return jnp.where(odd, near[i : i + 1, :], far[i : i + 1, :])
+
+    def below(i):
+        return jnp.where(odd, far[i : i + 1, :], near[i : i + 1, :])
+
+    return above, below
 
 
 def pack(planes, share, ports):
@@ -132,10 +163,11 @@
     return blocks
 
 
-def correlation_kernel(ports, e, m, ae, above, below, cells, amplitude, packed):
+def correlation_kernel(ports, e, m, ae, near, far, cells, amplitude, packed):
     _, _, depth, rows, width = e.shape
     share = width // ports
     tile = lax.axis_index("tile")
+    above, below = from_tiles(near, far)
     plane_cells = lax.axis_size("tile") * rows * width
     target = cells[0] - tile * (rows * width)
     inside = jnp.where(tile > 0, 1.0, 0.0)
@@ -149,12 +181,12 @@
     sums_a, sums_b = [], []
     for z in range(depth):
         ex, ey, ez = (at(e, c, z) for c in range(3))
-        next_y, next_z = below[z : z + 1, :], below[depth + z : depth + z + 1, :]
+        next_y, next_z = below(z), below(depth + z)
         fx = at(m, 0, z) - TIMESTEP * ((lane_next(ez) - ez) - (at(e, 1, z + 1) - ey))
         fy = at(m, 1, z) - TIMESTEP * ((at(e, 0, z + 1) - ex) - (row_next(ez, next_z) - ez))
         fz = at(m, 2, z) - TIMESTEP * ((row_next(ey, next_y) - ey) - (lane_next(ex) - ex))
-        prev_y = inside * (above[z : z + 1, :] + TIMESTEP * ez[0:1])
-        prev_z = inside * (above[depth + z : depth + z + 1, :] - TIMESTEP * ey[0:1])
+        prev_y = inside * (above(z) + TIMESTEP * ez[0:1])
+        prev_z = inside * (above(depth + z) - TIMESTEP * ey[0:1])
         hit = position == target - z * plane_cells
         drive_x = ((fz - lane_prev(fz)) - (fy - fy_prev)) - jnp.where(hit, amplitude[0, 0], 0.0)
         drive_y = ((fx - fx_prev) - (fz - row_prev(fz, prev_z))) - jnp.where(hit, amplitude[0, 1], 0.0)
@@ -173,9 +205,10 @@
             sums_a, sums_b = [], []
 
 
-def field_kernel(ae, am, labels, above, below, perm, cond, new_e, new_m):
+def field_kernel(ae, am, labels, near, far, perm, cond, new_e, new_m):
     depth, rows, width = labels.shape
     source, update = gains(perm, cond, width)
+    above, below = from_tiles(near, far)
     inside = jnp.where(lax.axis_index("tile") > 0, 1.0, 0.0)
     zero = jnp.zeros((rows, width), jnp.float32)
 
@@ -190,13 +223,13 @@
     for z in range(depth):
         after = scaled(z + 1)
         sx, sy, sz = here
-        next_y = below[2 * depth + z : 2 * depth + z + 1, :]
-        next_z = below[3 * depth + z : 3 * depth + z + 1, :]
+        next_y = below(2 * depth + z)
+        next_z = below(3 * depth + z)
         nx = am[0, 0, z] + ((lane_next(sz) - sz) - (after[1] - sy))
         ny = am[0, 1, z] + ((after[0] - sx) - (row_next(sz, next_z) - sz))
         nz = am[0, 2, z] + ((row_next(sy, next_y) - sy) - (lane_next(sx) - sx))
-        prev_y = inside * (above[2 * depth + z : 2 * depth + z + 1, :] - sz[0:1])
-        prev_z = inside * (above[3 * depth + z : 3 * depth + z + 1, :] + sy[0:1])
+        prev_y = inside * (above(2 * depth + z) - sz[0:1])
+        prev_z = inside * (above(3 * depth + z) + sy[0:1])
         new_m[0, 0, z] = nx
         new_m[0, 1, z] = ny
         new_m[0, 2, z] = nz
@@ -239,16 +272,14 @@
         grad_cond[z] = by_cond[:, :share]
 
 
-def spec(space):
-    return pl.BlockSpec(memory_space=space)
-
-
-def call(kernel, inputs, spaces, outs, flops, moved):
+def call(kernel, inputs, spaces, outs, out_spaces, flops, moved, scratch=()):
+    inputs = [pltpu.with_memory_space_constraint(x, VMEM) if space is VMEM else x for x, space in zip(inputs, spaces, strict=True)]
     return pl.pallas_call(
         kernel,
-        out_shape=outs,
-        in_specs=[spec(space) for space in spaces],
-        out_specs=jax.tree.map(lambda _: spec(VMEM), outs),
+        out_shape=tuple(space(out.shape, out.dtype) if space is VMEM else out for out, space in zip(outs, out_spaces, strict=True)),
+        in_specs=[pl.BlockSpec(memory_space=VMEM if space is HBM_BLOCK else space) for space in spaces],
+        out_specs=tuple(pl.BlockSpec(memory_space=VMEM) for _ in outs),
+        scratch_shapes=scratch,
         cost_estimate=pl.CostEstimate(flops=flops, bytes_accessed=moved, transcendentals=0),
     )(*inputs)
 
@@ -273,30 +304,35 @@
         return jax.ShapeDtypeStruct(shape, jnp.float32)
 
     edge = array(4 * depth, width)
-    up, down = call(
+    near, far = call(
         edge_kernel,
         (electric, magnetic, adjoint_electric, adjoint_magnetic, region_labels, permittivity_table, conductivity_table),
-        (VMEM,) * 5 + (SMEM,) * 2,
+        (ANY,) * 5 + (SMEM,) * 2,
         (edge, edge),
+        (VMEM, VMEM),
         10 * cells,
         cells * 4,
-    )
-    below = from_behind(down, "tile", -1)
-    above = from_behind(up, "tile", 1)
-    packed = call(
+        [
+            VMEM((count, depth, 1, width), jnp.float32) for count in (3, 2, 3, 2, 2, 2)
+        ] + [VMEM((2, depth, 1, width), jnp.int32), pltpu.SemaphoreType.DMA((8,))],
+    )
+    near, far = swap(near, "tile", 0), swap(far, "tile", 1)
+    (packed,) = call(
         functools.partial(correlation_kernel, ports),
-        (electric, magnetic, adjoint_electric, above, below, port_cells, port_amplitude),
+        (electric, magnetic, adjoint_electric, near, far, port_cells, port_amplitude),
         (VMEM,) * 5 + (SMEM,) * 2,
-        array(ports, 2 * depth // PLANES, rows, LANES),
+        (array(ports, 2 * depth // PLANES, rows, LANES),),
+        (VMEM,),
         60 * cells,
         cells * 4 * 11,
     )
     gathered = lax.all_to_all(packed, "port", 0, 0, tiled=True)
     new_electric, new_magnetic = call(
         field_kernel,
-        (adjoint_electric, adjoint_magnetic, region_labels, above, below, permittivity_table, conductivity_table),
-        (VMEM,) * 5 + (SMEM,) * 2,
+        (adjoint_electric, adjoint_magnetic, region_labels, near, far, permittivity_table, conductivity_table),
+        (VMEM, HBM_BLOCK, HBM_BLOCK, VMEM, VMEM) + (SMEM,) * 2,
         (array(1, 3, depth, rows, width), array(1, 3, depth, rows, width)),
+        (HBM_BLOCK,) * 2,
         80 * cells,
         cells * 4 * 13,
     )
@@ -306,6 +342,7 @@
         (gathered, region_labels, permittivity_table, conductivity_table),
         (VMEM,) * 2 + (SMEM,) * 2,
         (gradient, gradient),
+        (HBM_BLOCK,) * 2,
         4 * cells,
         cells * 4 * 3,
     )

time: 44.3 us -> 42.4 us (0.957)
  Pallas kernels: 11.2 us -> 8.92 us
  starting transfers between devices: 21 us -> 21.6 us
    pallas_call x4, Pallas kernels: 11.2 us -> 8.92 us  [call(): pl.pallas_call(kernel, out_shape=tuple((space(out.shape, out.dtype) if sp...]
    ppermute x2, starting transfers between devices: 13.6 us -> 14.3 us  [swap(): lax.ppermute(value, axis, [(i, i + 1) for i in pairs] + [(i + 1, i) for i...]
    unnamed x6 -> x8, local copies, waits for them, and re-layouts: 1.41 us -> 1.13 us
where the time goes in v3:
time: 42.4 us; the launch traced here: 42 us
  starting transfers between devices  21.6 us (51%)
  waiting for transfers between devices  9.03 us (21%)
  Pallas kernels  8.92 us (21%)
  between operations  1.34 us (3%)
  local copies, waits for them, and re-layouts  1.13 us (3%)
    ppermute x2, starting transfers between devices, swap(): lax.ppermute(value, axis, [(i, i + 1) for i in pairs] + [(i + 1, i) for i...  14.3 us
    pallas_call x4, Pallas kernels, call(): pl.pallas_call(kernel, out_shape=tuple((space(out.shape, out.dtype) if sp...  8.92 us
    all_to_all x1, waiting for transfers between devices, on_device(): gathered = lax.all_to_all(packed, 'port', 0, 0, tiled=True)  7.36 us
    all_to_all x1, starting transfers between devices, on_device(): gathered = lax.all_to_all(packed, 'port', 0, 0, tiled=True)  7.26 us
    ppermute x2, waiting for transfers between devices, swap(): lax.ppermute(value, axis, [(i, i + 1) for i in pairs] + [(i + 1, i) for i...  1.67 us
    unnamed x8, local copies, waits for them, and re-layouts  1.13 us
  transfers between devices with their start and end apart: 3, of which 2 were waited for; matrix products, arithmetic and copies ran while one was open for 0% of the time, Pallas kernels for 7%

profile of v3, /device:TPU:48, one launch (start us, length us, event | category | flops | bytes accessed | tf_op | source)
XLA Modules:
  0.0 42.0 jit_solution(16596233451963774836)
XLA Ops:
  0.6 0.0 copy-start
  0.6 0.0 copy-start.2
  0.7 1.9 %shard_map.120 = (f32[24,640]{1,0:T(8,128)S(1)}, f32[24,640]{1,0:T(8,128)S(1)}) custom-call(f32[1,3,6,16,640]{4,3,2,1,0:T(8,128)} %e.3, f32[1,3,6,16,640]{4,3,2,1,0:T(8,128)} %m.3, f32[1,3,6,16,640]{4,3,2,1,0:T(8,128)} %ae.5, f32[1,3,6,16,640]{4,3,2,1,0:T(8,128)} %am.3, s32[6,16,640]{2,1,0:T(8,128)} %labels.5, f32[8]{0:T(128)} %perm.5, f32[8]{0:T(128)} %cond.5), custom_call_target="tpu_custom_call" | custom-call | flops 614400 | bytes 245760 | tf_op jit(solution)/shard_map/pallas_call | solution.py:277
  2.6 1.9 %collective-permute-start = (f32[24,640]{1,0:T(8,128)S(1)}, f32[24,640]{1,0:T(8,128)S(1)}, u32[]{:S(2)}, u32[]{:S(2)}) collective-permute-start(f32[24,640]{1,0:T(8,128)S(1)} %get-tuple-element.10), channel_id=1, source_target_pairs={{0,1},{2,3},{4,5},{6,7},{8,9},{10,11},{12,13},{14,15},{16,17},{18,... | collective-permute-start | bytes 184328 | tf_op jit(solution)/shard_map/ppermute | solution.py:22
  4.5 12.4 %collective-permute-start.1 = (f32[24,640]{1,0:T(8,128)S(1)}, f32[24,640]{1,0:T(8,128)S(1)}, u32[]{:S(2)}, u32[]{:S(2)}) collective-permute-start(f32[24,640]{1,0:T(8,128)S(1)} %get-tuple-element.11), channel_id=1, source_target_pairs={{1,2},{3,4},{5,6},{7,8},{9,10},{11,12},{13,14},{15,16},{17,18},{19... | collective-permute-start | bytes 184328 | tf_op jit(solution)/shard_map/ppermute | solution.py:22
  17.5 0.0 collective-permute-done.near
  17.6 1.7 %collective-permute-done.1.far = f32[24,640]{1,0:T(8,128)S(1)} collective-permute-done((f32[24,640]{1,0:T(8,128)S(1)}, f32[24,640]{1,0:T(8,128)S(1)}, u32[]{:S(2)}, u32[]{:S(2)}) %collective-permute-start.1) | collective-permute-done | bytes 61472 | tf_op jit(solution)/shard_map/ppermute | solution.py:22
  19.2 0.0 copy-done
  19.2 0.0 copy-done.2
  19.2 0.0 copy-start.1
  19.2 1.1 %copy-done.1 = f32[1,3,6,16,640]{4,3,2,1,0:T(8,128)S(1)} copy-done((f32[1,3,6,16,640]{4,3,2,1,0:T(8,128)S(1)}, f32[1,3,6,16,640]{4,3,2,1,0:T(8,128)}, u32[]{:S(2)}) %copy-start.1) | copy-done | bytes 737304
  20.3 2.5 %shard_map.122 = f32[16,4,16,128]{3,2,1,0:T(8,128)} custom-call(f32[1,3,6,16,640]{4,3,2,1,0:T(8,128)S(1)} %copy-done.1, f32[1,3,6,16,640]{4,3,2,1,0:T(8,128)S(1)} %copy-done.2, f32[1,3,6,16,640]{4,3,2,1,0:T(8,128)S(1)} %copy-done, f32[24,640]{1,0:T(8,128)S(1)} %collective-permute-done.near, f32[24,640]{1,0:T(8,128)S(1)} %collective-permute-done.1.far, ...), custom_call_target="tpu_custom_call" | custom-call | flops 3686400 | bytes 2703360 | tf_op jit(solution)/shard_map/pallas_call | solution.py:277
  22.8 7.3 %all-to-all-start = ((f32[16,4,16,128]{3,2,1,0:T(8,128)}), f32[16,4,16,128]{3,2,1,0:T(8,128)S(1)}, u32[]{:S(2)}, u32[]{:S(2)}) async-start(f32[16,4,16,128]{3,2,1,0:T(8,128)} %shard_map.122), calls=%async_computation | async-start | bytes 1048576 | tf_op jit(solution)/shard_map/all_to_all | solution.py:329
  30.1 0.0 copy-start.3
  30.1 3.0 %shard_map.121 = (f32[1,3,6,16,640]{4,3,2,1,0:T(8,128)}, f32[1,3,6,16,640]{4,3,2,1,0:T(8,128)}) custom-call(f32[1,3,6,16,640]{4,3,2,1,0:T(8,128)S(1)} %copy-done, f32[1,3,6,16,640]{4,3,2,1,0:T(8,128)} %am.3, s32[6,16,640]{2,1,0:T(8,128)} %labels.5, f32[24,640]{1,0:T(8,128)S(1)} %collective-permute-done.near, f32[24,640]{1,0:T(8,128)S(1)} %collective-permute-done.1.far, ...), custom_call_target="tpu_custom_call" | custom-call | flops 4915200 | bytes 3194880 | tf_op jit(solution)/shard_map/pallas_call | solution.py:277
  33.1 7.4 %all-to-all-done.gathered = f32[16,4,16,128]{3,2,1,0:T(8,128)S(1)} async-done(((f32[16,4,16,128]{3,2,1,0:T(8,128)}), f32[16,4,16,128]{3,2,1,0:T(8,128)S(1)}, u32[]{:S(2)}, u32[]{:S(2)}) %all-to-all-start) | async-done | bytes 524320 | tf_op jit(solution)/shard_map/all_to_all | solution.py:329
  40.5 0.0 copy-done.3
  40.5 1.5 %shard_map.123 = (f32[6,16,40]{2,1,0:T(8,128)}, f32[6,16,40]{2,1,0:T(8,128)}) custom-call(f32[16,4,16,128]{3,2,1,0:T(8,128)S(1)} %all-to-all-done.gathered, s32[6,16,640]{2,1,0:T(8,128)S(1)} %copy-done.3, f32[8]{0:T(128)} %perm.5, f32[8]{0:T(128)} %cond.5), custom_call_target="tpu_custom_call" | custom-call | flops 245760 | bytes 737280 | tf_op jit(solution)/shard_map/pallas_call | solution.py:277
Async XLA Ops:
  0.6 18.6 %copy-start = (f32[1,3,6,16,640]{4,3,2,1,0:T(8,128)S(1)}, f32[1,3,6,16,640]{4,3,2,1,0:T(8,128)}, u32[]{:S(2)}) copy-start(f32[1,3,6,16,640]{4,3,2,1,0:T(8,128)} %ae.5) | copy-start | bytes 2211844
  0.6 18.6 %copy-start.2 = (f32[1,3,6,16,640]{4,3,2,1,0:T(8,128)S(1)}, f32[1,3,6,16,640]{4,3,2,1,0:T(8,128)}, u32[]{:S(2)}) copy-start(f32[1,3,6,16,640]{4,3,2,1,0:T(8,128)} %m.3) | copy-start | bytes 2211844
  2.6 15.0 %collective-permute-start = (f32[24,640]{1,0:T(8,128)S(1)}, f32[24,640]{1,0:T(8,128)S(1)}, u32[]{:S(2)}, u32[]{:S(2)}) collective-permute-start(f32[24,640]{1,0:T(8,128)S(1)} %get-tuple-element.10), channel_id=1, source_target_pairs={{0,1},{2,3},{4,5},{6,7},{8,9},{10,11},{12,13},{14,15},{16,17},{18,... | collective-permute-start | bytes 184328 | tf_op jit(solution)/shard_map/ppermute | solution.py:22
  4.5 14.7 %collective-permute-start.1 = (f32[24,640]{1,0:T(8,128)S(1)}, f32[24,640]{1,0:T(8,128)S(1)}, u32[]{:S(2)}, u32[]{:S(2)}) collective-permute-start(f32[24,640]{1,0:T(8,128)S(1)} %get-tuple-element.11), channel_id=1, source_target_pairs={{1,2},{3,4},{5,6},{7,8},{9,10},{11,12},{13,14},{15,16},{17,18},{19... | collective-permute-start | bytes 184328 | tf_op jit(solution)/shard_map/ppermute | solution.py:22
  19.2 1.1 %copy-start.1 = (f32[1,3,6,16,640]{4,3,2,1,0:T(8,128)S(1)}, f32[1,3,6,16,640]{4,3,2,1,0:T(8,128)}, u32[]{:S(2)}) copy-start(f32[1,3,6,16,640]{4,3,2,1,0:T(8,128)} %e.3) | copy-start | bytes 2211844
  22.8 17.6 %all-to-all-start = ((f32[16,4,16,128]{3,2,1,0:T(8,128)}), f32[16,4,16,128]{3,2,1,0:T(8,128)S(1)}, u32[]{:S(2)}, u32[]{:S(2)}) async-start(f32[16,4,16,128]{3,2,1,0:T(8,128)} %shard_map.122), calls=%async_computation | async-start | bytes 1048576 | tf_op jit(solution)/shard_map/all_to_all | solution.py:329
  30.1 10.4 %copy-start.3 = (s32[6,16,640]{2,1,0:T(8,128)S(1)}, s32[6,16,640]{2,1,0:T(8,128)}, u32[]{:S(2)}) copy-start(s32[6,16,640]{2,1,0:T(8,128)} %labels.5) | copy-start | bytes 737284

commit v4 on v3

--- a/solution.py
+++ b/solution.py
@@ -11,9 +11,11 @@
 HALF_STEP = 0.25
 PLANES = 3
 LANES = 128
+EDGE = 8
+VMEM_LIMIT = 12 << 20
 VMEM = pltpu.VMEM
 SMEM = pltpu.SMEM
-ANY = pl.ANY
+HBM = pltpu.HBM
 HBM_BLOCK = None
 
 
@@ -82,51 +84,47 @@
     return widen(source, width), widen(update, width)
 
 
-def edge_kernel(e, m, ae, am, labels, perm, cond, near, far, e_last, m_last, ae_last, am_last, e_first, ae_first, marks, sems):
+def edge_kernel(e, m, ae, am, labels, perms, conds, near, far, perm, cond, e_last, m_last, ae_last, am_last, e_first, ae_first, marks, sems):
     _, _, depth, rows, width = e.shape
     last = rows - 1
+    planes = pl.ds(0, depth)
     moves = (
-        (ae.at[0, :, :, pl.ds(last, 1)], ae_last),
-        (ae.at[0, pl.ds(1, 2), :, pl.ds(0, 1)], ae_first),
-        (labels.at[:, pl.ds(last, 1)], marks.at[0]),
-        (labels.at[:, pl.ds(0, 1)], marks.at[1]),
-        (e.at[0, :, :, pl.ds(last, 1)], e_last),
-        (e.at[0, pl.ds(1, 2), :, pl.ds(0, 1)], e_first),
-        (m.at[0, pl.ds(1, 2), :, pl.ds(last, 1)], m_last),
-        (am.at[0, pl.ds(1, 2), :, pl.ds(last, 1)], am_last),
+        (perms, perm),
+        (conds, cond),
+        (ae.at[0, :, :, last], ae_last.at[:, planes]),
+        (ae.at[0, pl.ds(1, 2), :, 0], ae_first.at[:, planes]),
+        (labels.at[:, last], marks.at[0, planes]),
+        (labels.at[:, 0], marks.at[1, planes]),
+        (e.at[0, :, :, last], e_last.at[:, planes]),
+        (e.at[0, pl.ds(1, 2), :, 0], e_first.at[:, planes]),
+        (m.at[0, pl.ds(1, 2), :, last], m_last.at[:, planes]),
+        (am.at[0, pl.ds(1, 2), :, last], am_last.at[:, planes]),
     )
     copies = [pltpu.make_async_copy(src, dst, sems.at[i]) for i, (src, dst) in enumerate(moves)]
     for copy in copies:
         copy.start()
-    source, _ = gains(perm, cond, width)
     odd = lax.rem(lax.axis_index("tile"), 2) == 1
+
+    def plane_next(value):
+        return jnp.where(row_iota(value.shape) < depth - 1, pltpu.roll(value, EDGE - 1, 0), 0.0)
+
     for copy in copies:
         copy.wait()
-    zero = jnp.zeros((1, width), jnp.float32)
-
-    def row(ref, c, z):
-        return ref[c, z] if z < depth else zero
-
-    scaled = []
-    for z in range(depth):
-        gain = look_up(marks[0, z], source)
-        scaled.append([gain * row(ae_last, c, z) for c in range(3)])
-    scaled.append([zero] * 3)
-    for z in range(depth):
-        ex, ey, ez = (row(e_last, c, z) for c in range(3))
-        sx, sy, sz = scaled[z]
-        gain = look_up(marks[1, z], source)
-        up = (
-            m_last[0, z] - TIMESTEP * ((row(e_last, 0, z + 1) - ex) + ez),
-            m_last[1, z] + TIMESTEP * (ey + (lane_next(ex) - ex)),
-            am_last[0, z] + ((scaled[z + 1][0] - sx) + sz),
-            am_last[1, z] - (sy + (lane_next(sx) - sx)),
-        )
-        down = (e_first[0, z], e_first[1, z], gain * ae_first[0, z], gain * ae_first[1, z])
-        for i, (above, below) in enumerate(zip(up, down, strict=True)):
-            at = i * depth + z
-            near[at : at + 1, :] = jnp.where(odd, below, above)
-            far[at : at + 1, :] = jnp.where(odd, above, below)
+    source, _ = gains(perm, cond, width)
+    last_gain, first_gain = (look_up(marks[i], source) for i in range(2))
+    ex, ey, ez = (e_last[c] for c in range(3))
+    sx, sy, sz = (last_gain * ae_last[c] for c in range(3))
+    up = (
+        m_last[0] - TIMESTEP * ((plane_next(ex) - ex) + ez),
+        m_last[1] + TIMESTEP * (ey + (lane_next(ex) - ex)),
+        am_last[0] + ((plane_next(sx) - sx) + sz),
+        am_last[1] - (sy + (lane_next(sx) - sx)),
+    )
+    down = (e_first[0], e_first[1], first_gain * ae_first[0], first_gain * ae_first[1])
+    for i, (above, below) in enumerate(zip(up, down, strict=True)):
+        at = i * depth
+        near[at : at + depth, :] = jnp.where(odd, below, above)[:depth]
+        far[at : at + depth, :] = jnp.where(odd, above, below)[:depth]
 
 
 def from_tiles(near, far):
@@ -163,7 +161,7 @@
     return blocks
 
 
-def correlation_kernel(ports, e, m, ae, near, far, cells, amplitude, packed):
+def correlation_kernel(ports, e, m, ae, near, far, cells, amplitude, packed, stage, sems):
     _, _, depth, rows, width = e.shape
     share = width // ports
     tile = lax.axis_index("tile")
@@ -178,7 +176,7 @@
 
     zero = jnp.zeros((rows, width), jnp.float32)
     fx_prev, fy_prev = zero, zero
-    sums_a, sums_b = [], []
+    sums_a, sums_b, copies = [], [], []
     for z in range(depth):
         ex, ey, ez = (at(e, c, z) for c in range(3))
         next_y, next_z = below(z), below(depth + z)
@@ -200,13 +198,37 @@
         if z % PLANES == PLANES - 1:
             group = z // PLANES
             for f, sums in enumerate((sums_a, sums_b)):
+                slab = f * (depth // PLANES) + group
                 for port, block in enumerate(pack(sums, share, ports)):
-                    packed[port, f * (depth // PLANES) + group] = block
+                    stage[port, slab] = block
+                copies.append(pltpu.make_async_copy(stage.at[:, slab], packed.at[:, slab], sems.at[slab]))
+                copies[-1].start()
             sums_a, sums_b = [], []
-
-
-def field_kernel(ae, am, labels, near, far, perm, cond, new_e, new_m):
+    for copy in copies:
+        copy.wait()
+
+
+def share_factors(ports, labels, perm, cond, factors):
     depth, rows, width = labels.shape
+    share = width // ports
+    begin = lax.axis_index("port") * share
+    perms, conds = region_values(perm, cond)
+    denominators = [p + HALF_STEP * c for p, c in zip(perms, conds, strict=True)]
+    scales = [TIMESTEP / (d * d) for d in denominators]
+    lane = lane_iota((rows, LANES))
+    for group in range(depth // PLANES):
+        mine = None
+        for j in range(PLANES - 1, -1, -1):
+            shift = lax.rem(width - begin + j * share, width)
+            piece = pltpu.roll(labels[group * PLANES + j], shift, 1)[:, :LANES]
+            mine = piece if mine is None else jnp.where(lane < (j + 1) * share, piece, mine)
+        for i, entries in enumerate((scales, perms, conds)):
+            factors[i, group] = look_up(mine, entries)
+
+
+def field_kernel(ports, ae, am, labels, near, far, perm, cond, new_e, new_m, factors):
+    depth, rows, width = labels.shape
+    share_factors(ports, labels, perm, cond, factors)
     source, update = gains(perm, cond, width)
     above, below = from_tiles(near, far)
     inside = jnp.where(lax.axis_index("tile") > 0, 1.0, 0.0)
@@ -241,45 +263,36 @@
         here = after
 
 
-def gradient_kernel(gathered, labels, perm, cond, grad_perm, grad_cond):
+def gradient_kernel(gathered, factors, grad_perm, grad_cond):
     ports, slabs, rows, _ = gathered.shape
     depth, _, share = grad_perm.shape
-    width = labels.shape[2]
     groups = depth // PLANES
-    begin = lax.axis_index("port") * share
-    perms, conds = region_values(perm, cond)
-    denominators = [p + HALF_STEP * c for p, c in zip(perms, conds, strict=True)]
-    factors = [TIMESTEP / (d * d) for d in denominators]
     sums = []
     for slab in range(slabs):
         total = gathered[0, slab]
         for port in range(1, ports):
             total = total + gathered[port, slab]
         sums.append(total)
-    for z in range(depth):
-        group, j = divmod(z, PLANES)
-        corr_a, corr_b = (
-            pltpu.roll(sums[f * groups + group], (LANES - j * share) % LANES, 1) if j else sums[f * groups + group]
-            for f in range(2)
-        )
-        mine = pltpu.roll(labels[z], lax.rem(width - begin, width), 1)[:, :LANES]
-        factor = look_up(mine, factors)
-        permittivity = look_up(mine, perms)
-        conductivity = look_up(mine, conds)
+    for group in range(groups):
+        corr_a, corr_b = sums[group], sums[groups + group]
+        factor, permittivity, conductivity = (factors[i, group] for i in range(3))
         by_perm = factor * (conductivity * corr_a - corr_b)
         by_cond = factor * (-permittivity * corr_a - HALF_STEP * corr_b)
-        grad_perm[z] = by_perm[:, :share]
-        grad_cond[z] = by_cond[:, :share]
+        for j in range(PLANES):
+            for ref, value in ((grad_perm, by_perm), (grad_cond, by_cond)):
+                moved = pltpu.roll(value, LANES - j * share, 1) if j else value
+                ref[group * PLANES + j] = moved[:, :share]
 
 
 def call(kernel, inputs, spaces, outs, out_spaces, flops, moved, scratch=()):
-    inputs = [pltpu.with_memory_space_constraint(x, VMEM) if space is VMEM else x for x, space in zip(inputs, spaces, strict=True)]
+    inputs = [pltpu.with_memory_space_constraint(x, space) if space in (VMEM, HBM) else x for x, space in zip(inputs, spaces, strict=True)]
     return pl.pallas_call(
         kernel,
         out_shape=tuple(space(out.shape, out.dtype) if space is VMEM else out for out, space in zip(outs, out_spaces, strict=True)),
         in_specs=[pl.BlockSpec(memory_space=VMEM if space is HBM_BLOCK else space) for space in spaces],
-        out_specs=tuple(pl.BlockSpec(memory_space=VMEM) for _ in outs),
+        out_specs=tuple(pl.BlockSpec(memory_space=VMEM if space is HBM_BLOCK else space) for space in out_spaces),
         scratch_shapes=scratch,
+        compiler_params=pltpu.CompilerParams(vmem_limit_bytes=VMEM_LIMIT),
         cost_estimate=pl.CostEstimate(flops=flops, bytes_accessed=moved, transcendentals=0),
     )(*inputs)
 
@@ -307,40 +320,42 @@
     near, far = call(
         edge_kernel,
         (electric, magnetic, adjoint_electric, adjoint_magnetic, region_labels, permittivity_table, conductivity_table),
-        (ANY,) * 5 + (SMEM,) * 2,
+        (HBM,) * 7,
         (edge, edge),
         (VMEM, VMEM),
         10 * cells,
-        cells * 4,
-        [
-            VMEM((count, depth, 1, width), jnp.float32) for count in (3, 2, 3, 2, 2, 2)
-        ] + [VMEM((2, depth, 1, width), jnp.int32), pltpu.SemaphoreType.DMA((8,))],
+        cells * 4 * 14,
+        [SMEM(permittivity_table.shape, jnp.float32)] * 2 + [
+            VMEM((count, EDGE, width), jnp.float32) for count in (3, 2, 3, 2, 2, 2)
+        ] + [VMEM((2, EDGE, width), jnp.int32), pltpu.SemaphoreType.DMA((10,))],
     )
     near, far = swap(near, "tile", 0), swap(far, "tile", 1)
+    shares = array(ports, 2 * depth // PLANES, rows, LANES)
     (packed,) = call(
         functools.partial(correlation_kernel, ports),
         (electric, magnetic, adjoint_electric, near, far, port_cells, port_amplitude),
         (VMEM,) * 5 + (SMEM,) * 2,
-        (array(ports, 2 * depth // PLANES, rows, LANES),),
-        (VMEM,),
+        (shares,),
+        (HBM,),
         60 * cells,
         cells * 4 * 11,
+        [VMEM(shares.shape, jnp.float32), pltpu.SemaphoreType.DMA((shares.shape[1],))],
     )
     gathered = lax.all_to_all(packed, "port", 0, 0, tiled=True)
-    new_electric, new_magnetic = call(
-        field_kernel,
+    new_electric, new_magnetic, factors = call(
+        functools.partial(field_kernel, ports),
         (adjoint_electric, adjoint_magnetic, region_labels, near, far, permittivity_table, conductivity_table),
         (VMEM, HBM_BLOCK, HBM_BLOCK, VMEM, VMEM) + (SMEM,) * 2,
-        (array(1, 3, depth, rows, width), array(1, 3, depth, rows, width)),
-        (HBM_BLOCK,) * 2,
+        (array(1, 3, depth, rows, width), array(1, 3, depth, rows, width), array(3, depth // PLANES, rows, LANES)),
+        (HBM_BLOCK, HBM_BLOCK, VMEM),
         80 * cells,
         cells * 4 * 13,
     )
     gradient = array(depth, rows, share)
     gradient_perm, gradient_cond = call(
         gradient_kernel,
-        (gathered, region_labels, permittivity_table, conductivity_table),
-        (VMEM,) * 2 + (SMEM,) * 2,
+        (gathered, factors),
+        (VMEM,) * 2,
         (gradient, gradient),
         (HBM_BLOCK,) * 2,
         4 * cells,

time: 42.4 us -> 39.8 us (0.939)
  Pallas kernels: 8.92 us -> 6.74 us
  local copies, waits for them, and re-layouts: 1.13 us -> 0.04 us
  waiting for transfers between devices: 9.03 us -> 9.57 us
    pallas_call x4, Pallas kernels: 8.92 us -> 6.74 us  [call(): pl.pallas_call(kernel, out_shape=tuple((space(out.shape, out.dtype) if sp...]
    unnamed x8 -> x16, local copies, waits for them, and re-layouts: 1.13 us -> 0.04 us
    all_to_all x1, waiting for transfers between devices: 7.36 us -> 7.9 us  [on_device(): gathered = lax.all_to_all(packed, 'port', 0, 0, tiled=True)]
  transfers between devices with their start and end apart: 3 -> 3, of which waited for: 2 -> 2; matrix products, arithmetic and copies ran while one was open for 0% -> 0% of each run, Pallas kernels for 7% -> 6%
where the time goes in v4:
time: 39.8 us; the launch traced here: 39.5 us
  starting transfers between devices  21.7 us (55%)
  waiting for transfers between devices  9.57 us (24%)
  Pallas kernels  6.74 us (17%)
  between operations  1.42 us (4%)
    ppermute x2, starting transfers between devices, swap(): lax.ppermute(value, axis, [(i, i + 1) for i in pairs] + [(i + 1, i) for i...  14.3 us
    all_to_all x1, waiting for transfers between devices, on_device(): gathered = lax.all_to_all(packed, 'port', 0, 0, tiled=True)  7.9 us
    all_to_all x1, starting transfers between devices, on_device(): gathered = lax.all_to_all(packed, 'port', 0, 0, tiled=True)  7.4 us
    pallas_call x4, Pallas kernels, call(): pl.pallas_call(kernel, out_shape=tuple((space(out.shape, out.dtype) if sp...  6.74 us
    ppermute x2, waiting for transfers between devices, swap(): lax.ppermute(value, axis, [(i, i + 1) for i in pairs] + [(i + 1, i) for i...  1.67 us
  transfers between devices with their start and end apart: 3, of which 2 were waited for; matrix products, arithmetic and copies ran while one was open for 0% of the time, Pallas kernels for 6%

profile of v4, /device:TPU:48, one launch (start us, length us, event | category | flops | bytes accessed | tf_op | source)
XLA Modules:
  0.0 39.5 jit_solution(12023379772841842740)
XLA Ops:
  0.6 0.0 copy-start
  0.6 0.0 copy-start.2
  0.7 0.0 copy-start.1
  0.7 1.2 %shard_map.120 = (f32[24,640]{1,0:T(8,128)S(1)}, f32[24,640]{1,0:T(8,128)S(1)}) custom-call(f32[1,3,6,16,640]{4,3,2,1,0:T(8,128)} %e.3, f32[1,3,6,16,640]{4,3,2,1,0:T(8,128)} %m.3, f32[1,3,6,16,640]{4,3,2,1,0:T(8,128)} %ae.5, f32[1,3,6,16,640]{4,3,2,1,0:T(8,128)} %am.3, s32[6,16,640]{2,1,0:T(8,128)} %labels.3, f32[8]{0:T(128)} %perm.1, f32[8]{0:T(128)} %cond.1), custom_call_target="tpu_custom_call" | custom-call | flops 614400 | bytes 3440640 | tf_op jit(solution)/shard_map/pallas_call | solution.py:289
  1.9 1.9 %collective-permute-start = (f32[24,640]{1,0:T(8,128)S(1)}, f32[24,640]{1,0:T(8,128)S(1)}, u32[]{:S(2)}, u32[]{:S(2)}) collective-permute-start(f32[24,640]{1,0:T(8,128)S(1)} %get-tuple-element.11), channel_id=1, source_target_pairs={{0,1},{2,3},{4,5},{6,7},{8,9},{10,11},{12,13},{14,15},{16,17},{18,... | collective-permute-start | bytes 184328 | tf_op jit(solution)/shard_map/ppermute | solution.py:24
  3.8 0.0 copy-start.7
  3.8 12.4 %collective-permute-start.1 = (f32[24,640]{1,0:T(8,128)S(1)}, f32[24,640]{1,0:T(8,128)S(1)}, u32[]{:S(2)}, u32[]{:S(2)}) collective-permute-start(f32[24,640]{1,0:T(8,128)S(1)} %get-tuple-element.12), channel_id=1, source_target_pairs={{1,2},{3,4},{5,6},{7,8},{9,10},{11,12},{13,14},{15,16},{17,18},{19... | collective-permute-start | bytes 184328 | tf_op jit(solution)/shard_map/ppermute | solution.py:24
  16.9 0.0 collective-permute-done.near
  16.9 1.7 %collective-permute-done.1.far = f32[24,640]{1,0:T(8,128)S(1)} collective-permute-done((f32[24,640]{1,0:T(8,128)S(1)}, f32[24,640]{1,0:T(8,128)S(1)}, u32[]{:S(2)}, u32[]{:S(2)}) %collective-permute-start.1) | collective-permute-done | bytes 61472 | tf_op jit(solution)/shard_map/ppermute | solution.py:24
  18.6 0.0 copy-done
  18.6 0.0 copy-done.2
  18.6 0.0 copy-done.1
  18.6 0.0 copy-done.7
  18.6 2.3 %shard_map.122 = f32[16,4,16,128]{3,2,1,0:T(8,128)} custom-call(f32[1,3,6,16,640]{4,3,2,1,0:T(8,128)S(1)} %copy-done.1, f32[1,3,6,16,640]{4,3,2,1,0:T(8,128)S(1)} %copy-done.2, f32[1,3,6,16,640]{4,3,2,1,0:T(8,128)S(1)} %copy-done, f32[24,640]{1,0:T(8,128)S(1)} %collective-permute-done.near, f32[24,640]{1,0:T(8,128)S(1)} %collective-permute-done.1.far, ...), custom_call_target="tpu_custom_call" | custom-call | flops 3686400 | bytes 2703360 | tf_op jit(solution)/shard_map/pallas_call | solution.py:289
  20.9 0.0 copy-start.3
  20.9 0.0 copy-start.4
  20.9 0.0 copy-start.5
  21.0 0.0 copy-start.6
  21.0 7.4 %all-to-all-start = ((f32[16,4,16,128]{3,2,1,0:T(8,128)}), f32[16,4,16,128]{3,2,1,0:T(8,128)S(1)}, u32[]{:S(2)}, u32[]{:S(2)}) async-start(f32[16,4,16,128]{3,2,1,0:T(8,128)} %shard_map.122), calls=%async_computation | async-start | bytes 1048576 | tf_op jit(solution)/shard_map/all_to_all | solution.py:344
  28.4 0.0 copy-done.3
  28.4 0.0 copy-done.4
  28.4 0.0 copy-done.5
  28.4 0.0 copy-done.6
  28.4 2.4 %shard_map.121 = (f32[1,3,6,16,640]{4,3,2,1,0:T(8,128)}, f32[1,3,6,16,640]{4,3,2,1,0:T(8,128)}, f32[3,2,16,128]{3,2,1,0:T(8,128)S(1)}) custom-call(f32[1,3,6,16,640]{4,3,2,1,0:T(8,128)S(1)} %copy-done, f32[1,3,6,16,640]{4,3,2,1,0:T(8,128)S(1)} %copy-done.3, s32[6,16,640]{2,1,0:T(8,128)S(1)} %copy-done.4, f32[24,640]{1,0:T(8,128)S(1)} %collective-permute-done.near, ...), custom_call_target="tpu_custom_call" | custom-call | flops 4915200 | bytes 3194880 | tf_op jit(solution)/shard_map/pallas_call | solution.py:289
  30.8 7.9 %all-to-all-done.gathered = f32[16,4,16,128]{3,2,1,0:T(8,128)S(1)} async-done(((f32[16,4,16,128]{3,2,1,0:T(8,128)}), f32[16,4,16,128]{3,2,1,0:T(8,128)S(1)}, u32[]{:S(2)}, u32[]{:S(2)}) %all-to-all-start) | async-done | bytes 524320 | tf_op jit(solution)/shard_map/all_to_all | solution.py:344
  38.7 0.7 %shard_map.123 = (f32[6,16,40]{2,1,0:T(8,128)}, f32[6,16,40]{2,1,0:T(8,128)}) custom-call(f32[16,4,16,128]{3,2,1,0:T(8,128)S(1)} %all-to-all-done.gathered, f32[3,2,16,128]{3,2,1,0:T(8,128)S(1)} %get-tuple-element.15.factors), custom_call_target="tpu_custom_call" | custom-call | flops 245760 | bytes 737280 | tf_op jit(solution)/shard_map/pallas_call | solution.py:289
Async XLA Ops:
  0.6 17.9 %copy-start = (f32[1,3,6,16,640]{4,3,2,1,0:T(8,128)S(1)}, f32[1,3,6,16,640]{4,3,2,1,0:T(8,128)}, u32[]{:S(2)}) copy-start(f32[1,3,6,16,640]{4,3,2,1,0:T(8,128)} %ae.5) | copy-start | bytes 2211844
  0.6 17.9 %copy-start.2 = (f32[1,3,6,16,640]{4,3,2,1,0:T(8,128)S(1)}, f32[1,3,6,16,640]{4,3,2,1,0:T(8,128)}, u32[]{:S(2)}) copy-start(f32[1,3,6,16,640]{4,3,2,1,0:T(8,128)} %m.3) | copy-start | bytes 2211844
  0.7 17.9 %copy-start.1 = (f32[1,3,6,16,640]{4,3,2,1,0:T(8,128)S(1)}, f32[1,3,6,16,640]{4,3,2,1,0:T(8,128)}, u32[]{:S(2)}) copy-start(f32[1,3,6,16,640]{4,3,2,1,0:T(8,128)} %e.3) | copy-start | bytes 2211844
  1.9 15.0 %collective-permute-start = (f32[24,640]{1,0:T(8,128)S(1)}, f32[24,640]{1,0:T(8,128)S(1)}, u32[]{:S(2)}, u32[]{:S(2)}) collective-permute-start(f32[24,640]{1,0:T(8,128)S(1)} %get-tuple-element.11), channel_id=1, source_target_pairs={{0,1},{2,3},{4,5},{6,7},{8,9},{10,11},{12,13},{14,15},{16,17},{18,... | collective-permute-start | bytes 184328 | tf_op jit(solution)/shard_map/ppermute | solution.py:24
  3.8 14.7 %copy-start.7 = (f32[1,3]{1,0:T(1,128)S(1)}, f32[1,3]{1,0:T(1,128)}, u32[]{:S(2)}) copy-start(f32[1,3]{1,0:T(1,128)} %amplitude.1) | copy-start | bytes 40
  3.8 14.7 %collective-permute-start.1 = (f32[24,640]{1,0:T(8,128)S(1)}, f32[24,640]{1,0:T(8,128)S(1)}, u32[]{:S(2)}, u32[]{:S(2)}) collective-permute-start(f32[24,640]{1,0:T(8,128)S(1)} %get-tuple-element.12), channel_id=1, source_target_pairs={{1,2},{3,4},{5,6},{7,8},{9,10},{11,12},{13,14},{15,16},{17,18},{19... | collective-permute-start | bytes 184328 | tf_op jit(solution)/shard_map/ppermute | solution.py:24
  20.9 7.5 %copy-start.3 = (f32[1,3,6,16,640]{4,3,2,1,0:T(8,128)S(1)}, f32[1,3,6,16,640]{4,3,2,1,0:T(8,128)}, u32[]{:S(2)}) copy-start(f32[1,3,6,16,640]{4,3,2,1,0:T(8,128)} %am.3) | copy-start | bytes 2211844
  20.9 7.4 %copy-start.4 = (s32[6,16,640]{2,1,0:T(8,128)S(1)}, s32[6,16,640]{2,1,0:T(8,128)}, u32[]{:S(2)}) copy-start(s32[6,16,640]{2,1,0:T(8,128)} %labels.3) | copy-start | bytes 737284
  20.9 7.4 %copy-start.5 = (f32[8]{0:T(128)S(1)}, f32[8]{0:T(128)}, u32[]{:S(2)}) copy-start(f32[8]{0:T(128)} %perm.1) | copy-start | bytes 100
  21.0 7.4 %copy-start.6 = (f32[8]{0:T(128)S(1)}, f32[8]{0:T(128)}, u32[]{:S(2)}) copy-start(f32[8]{0:T(128)} %cond.1) | copy-start | bytes 100
  21.0 17.8 %all-to-all-start = ((f32[16,4,16,128]{3,2,1,0:T(8,128)}), f32[16,4,16,128]{3,2,1,0:T(8,128)S(1)}, u32[]{:S(2)}, u32[]{:S(2)}) async-start(f32[16,4,16,128]{3,2,1,0:T(8,128)} %shard_map.122), calls=%async_computation | async-start | bytes 1048576 | tf_op jit(solution)/shard_map/all_to_all | solution.py:344

commit v5 on v4

--- a/solution.py
+++ b/solution.py
@@ -84,7 +84,7 @@
     return widen(source, width), widen(update, width)
 
 
-def edge_kernel(e, m, ae, am, labels, perms, conds, near, far, perm, cond, e_last, m_last, ae_last, am_last, e_first, ae_first, marks, sems):
+def edge_kernel(e, m, ae, am, labels, perms, conds, far, near, perm, cond, e_last, m_last, ae_last, am_last, e_first, ae_first, marks, sems):
     _, _, depth, rows, width = e.shape
     last = rows - 1
     planes = pl.ds(0, depth)
@@ -161,7 +161,7 @@
     return blocks
 
 
-def correlation_kernel(ports, e, m, ae, near, far, cells, amplitude, packed, stage, sems):
+def correlation_kernel(ports, e, m, ae, far, near, cells, amplitude, packed, stage, sems):
     _, _, depth, rows, width = e.shape
     share = width // ports
     tile = lax.axis_index("tile")
@@ -226,7 +226,7 @@
             factors[i, group] = look_up(mine, entries)
 
 
-def field_kernel(ports, ae, am, labels, near, far, perm, cond, new_e, new_m, factors):
+def field_kernel(ports, ae, am, labels, far, near, perm, cond, new_e, new_m, factors):
     depth, rows, width = labels.shape
     share_factors(ports, labels, perm, cond, factors)
     source, update = gains(perm, cond, width)
@@ -317,7 +317,7 @@
         return jax.ShapeDtypeStruct(shape, jnp.float32)
 
     edge = array(4 * depth, width)
-    near, far = call(
+    far, near = call(
         edge_kernel,
         (electric, magnetic, adjoint_electric, adjoint_magnetic, region_labels, permittivity_table, conductivity_table),
         (HBM,) * 7,
@@ -329,11 +329,12 @@
             VMEM((count, EDGE, width), jnp.float32) for count in (3, 2, 3, 2, 2, 2)
         ] + [VMEM((2, EDGE, width), jnp.int32), pltpu.SemaphoreType.DMA((10,))],
     )
-    near, far = swap(near, "tile", 0), swap(far, "tile", 1)
+    far = swap(far, "tile", 1)
+    near = swap(near, "tile", 0)
     shares = array(ports, 2 * depth // PLANES, rows, LANES)
     (packed,) = call(
         functools.partial(correlation_kernel, ports),
-        (electric, magnetic, adjoint_electric, near, far, port_cells, port_amplitude),
+        (electric, magnetic, adjoint_electric, far, near, port_cells, port_amplitude),
         (VMEM,) * 5 + (SMEM,) * 2,
         (shares,),
         (HBM,),
@@ -344,7 +345,7 @@
     gathered = lax.all_to_all(packed, "port", 0, 0, tiled=True)
     new_electric, new_magnetic, factors = call(
         functools.partial(field_kernel, ports),
-        (adjoint_electric, adjoint_magnetic, region_labels, near, far, permittivity_table, conductivity_table),
+        (adjoint_electric, adjoint_magnetic, region_labels, far, near, permittivity_table, conductivity_table),
         (VMEM, HBM_BLOCK, HBM_BLOCK, VMEM, VMEM) + (SMEM,) * 2,
         (array(1, 3, depth, rows, width), array(1, 3, depth, rows, width), array(3, depth // PLANES, rows, LANES)),
         (HBM_BLOCK, HBM_BLOCK, VMEM),

time: 39.8 us -> 42.9 us (1.078)
  waiting for transfers between devices: 9.57 us -> 12.9 us
    all_to_all x1, waiting for transfers between devices: 7.9 us -> 12.4 us  [on_device(): gathered = lax.all_to_all(packed, 'port', 0, 0, tiled=True)]
    ppermute x2, waiting for transfers between devices: 1.67 us -> 0.56 us  [swap(): lax.ppermute(value, axis, [(i, i + 1) for i in pairs] + [(i + 1, i) for i...]
    ppermute x2, starting transfers between devices: 14.3 us -> 13.7 us  [swap(): lax.ppermute(value, axis, [(i, i + 1) for i in pairs] + [(i + 1, i) for i...]
    all_to_all x1, starting transfers between devices: 7.4 us -> 7.83 us  [on_device(): gathered = lax.all_to_all(packed, 'port', 0, 0, tiled=True)]
where the time goes in v5:
time: 42.9 us; the launch traced here: 42.6 us
  starting transfers between devices  21.5 us (50%)
  waiting for transfers between devices  12.9 us (30%)
  Pallas kernels  6.74 us (16%)
  between operations  1.42 us (3%)
    ppermute x2, starting transfers between devices, swap(): lax.ppermute(value, axis, [(i, i + 1) for i in pairs] + [(i + 1, i) for i...  13.7 us
    all_to_all x1, waiting for transfers between devices, on_device(): gathered = lax.all_to_all(packed, 'port', 0, 0, tiled=True)  12.4 us
    all_to_all x1, starting transfers between devices, on_device(): gathered = lax.all_to_all(packed, 'port', 0, 0, tiled=True)  7.83 us
    pallas_call x4, Pallas kernels, call(): pl.pallas_call(kernel, out_shape=tuple((space(out.shape, out.dtype) if sp...  6.74 us
  transfers between devices with their start and end apart: 3, of which 2 were waited for; matrix products, arithmetic and copies ran while one was open for 0% of the time, Pallas kernels for 6%

profile of v5, /device:TPU:48, one launch (start us, length us, event | category | flops | bytes accessed | tf_op | source)
XLA Modules:
  0.0 42.6 jit_solution(7968479335434623342)
XLA Ops:
  0.6 0.0 copy-start
  0.6 0.0 copy-start.2
  0.7 0.0 copy-start.1
  0.7 1.2 %shard_map.120 = (f32[24,640]{1,0:T(8,128)S(1)}, f32[24,640]{1,0:T(8,128)S(1)}) custom-call(f32[1,3,6,16,640]{4,3,2,1,0:T(8,128)} %e.3, f32[1,3,6,16,640]{4,3,2,1,0:T(8,128)} %m.3, f32[1,3,6,16,640]{4,3,2,1,0:T(8,128)} %ae.5, f32[1,3,6,16,640]{4,3,2,1,0:T(8,128)} %am.3, s32[6,16,640]{2,1,0:T(8,128)} %labels.3, f32[8]{0:T(128)} %perm.1, f32[8]{0:T(128)} %cond.1), custom_call_target="tpu_custom_call" | custom-call | flops 614400 | bytes 3440640 | tf_op jit(solution)/shard_map/pallas_call | solution.py:289
  1.9 11.7 %collective-permute-start = (f32[24,640]{1,0:T(8,128)S(1)}, f32[24,640]{1,0:T(8,128)S(1)}, u32[]{:S(2)}, u32[]{:S(2)}) collective-permute-start(f32[24,640]{1,0:T(8,128)S(1)} %get-tuple-element.11), channel_id=1, source_target_pairs={{1,2},{3,4},{5,6},{7,8},{9,10},{11,12},{13,14},{15,16},{17,18},{19... | collective-permute-start | bytes 184328 | tf_op jit(solution)/shard_map/ppermute | solution.py:24
  13.6 0.0 copy-start.7
  13.6 1.9 %collective-permute-start.1 = (f32[24,640]{1,0:T(8,128)S(1)}, f32[24,640]{1,0:T(8,128)S(1)}, u32[]{:S(2)}, u32[]{:S(2)}) collective-permute-start(f32[24,640]{1,0:T(8,128)S(1)} %get-tuple-element.12), channel_id=1, source_target_pairs={{0,1},{2,3},{4,5},{6,7},{8,9},{10,11},{12,13},{14,15},{16,17},{18,... | collective-permute-start | bytes 184328 | tf_op jit(solution)/shard_map/ppermute | solution.py:24
  16.2 0.0 collective-permute-done.far
  16.2 0.6 %collective-permute-done.1.near = f32[24,640]{1,0:T(8,128)S(1)} collective-permute-done((f32[24,640]{1,0:T(8,128)S(1)}, f32[24,640]{1,0:T(8,128)S(1)}, u32[]{:S(2)}, u32[]{:S(2)}) %collective-permute-start.1) | collective-permute-done | bytes 61472 | tf_op jit(solution)/shard_map/ppermute | solution.py:24
  16.8 0.0 copy-done
  16.8 0.0 copy-done.2
  16.8 0.0 copy-done.1
  16.8 0.0 copy-done.7
  16.8 2.3 %shard_map.122 = f32[16,4,16,128]{3,2,1,0:T(8,128)} custom-call(f32[1,3,6,16,640]{4,3,2,1,0:T(8,128)S(1)} %copy-done.1, f32[1,3,6,16,640]{4,3,2,1,0:T(8,128)S(1)} %copy-done.2, f32[1,3,6,16,640]{4,3,2,1,0:T(8,128)S(1)} %copy-done, f32[24,640]{1,0:T(8,128)S(1)} %collective-permute-done.far, f32[24,640]{1,0:T(8,128)S(1)} %collective-permute-done.1.near, ...), custom_call_target="tpu_custom_call" | custom-call | flops 3686400 | bytes 2703360 | tf_op jit(solution)/shard_map/pallas_call | solution.py:289
  19.1 0.0 copy-start.3
  19.2 0.0 copy-start.4
  19.2 0.0 copy-start.5
  19.2 0.0 copy-start.6
  19.2 7.8 %all-to-all-start = ((f32[16,4,16,128]{3,2,1,0:T(8,128)}), f32[16,4,16,128]{3,2,1,0:T(8,128)S(1)}, u32[]{:S(2)}, u32[]{:S(2)}) async-start(f32[16,4,16,128]{3,2,1,0:T(8,128)} %shard_map.122), calls=%async_computation | async-start | bytes 1048576 | tf_op jit(solution)/shard_map/all_to_all | solution.py:345
  27.0 0.0 copy-done.3
  27.0 0.0 copy-done.4
  27.0 0.0 copy-done.5
  27.1 0.0 copy-done.6
  27.1 2.4 %shard_map.121 = (f32[1,3,6,16,640]{4,3,2,1,0:T(8,128)}, f32[1,3,6,16,640]{4,3,2,1,0:T(8,128)}, f32[3,2,16,128]{3,2,1,0:T(8,128)S(1)}) custom-call(f32[1,3,6,16,640]{4,3,2,1,0:T(8,128)S(1)} %copy-done, f32[1,3,6,16,640]{4,3,2,1,0:T(8,128)S(1)} %copy-done.3, s32[6,16,640]{2,1,0:T(8,128)S(1)} %copy-done.4, f32[24,640]{1,0:T(8,128)S(1)} %collective-permute-done.far, ...), custom_call_target="tpu_custom_call" | custom-call | flops 4915200 | bytes 3194880 | tf_op jit(solution)/shard_map/pallas_call | solution.py:289
  29.5 12.4 %all-to-all-done.gathered = f32[16,4,16,128]{3,2,1,0:T(8,128)S(1)} async-done(((f32[16,4,16,128]{3,2,1,0:T(8,128)}), f32[16,4,16,128]{3,2,1,0:T(8,128)S(1)}, u32[]{:S(2)}, u32[]{:S(2)}) %all-to-all-start) | async-done | bytes 524320 | tf_op jit(solution)/shard_map/all_to_all | solution.py:345
  41.9 0.7 %shard_map.123 = (f32[6,16,40]{2,1,0:T(8,128)}, f32[6,16,40]{2,1,0:T(8,128)}) custom-call(f32[16,4,16,128]{3,2,1,0:T(8,128)S(1)} %all-to-all-done.gathered, f32[3,2,16,128]{3,2,1,0:T(8,128)S(1)} %get-tuple-element.15.factors), custom_call_target="tpu_custom_call" | custom-call | flops 245760 | bytes 737280 | tf_op jit(solution)/shard_map/pallas_call | solution.py:289
Async XLA Ops:
  0.6 16.2 %copy-start = (f32[1,3,6,16,640]{4,3,2,1,0:T(8,128)S(1)}, f32[1,3,6,16,640]{4,3,2,1,0:T(8,128)}, u32[]{:S(2)}) copy-start(f32[1,3,6,16,640]{4,3,2,1,0:T(8,128)} %ae.5) | copy-start | bytes 2211844
  0.6 16.2 %copy-start.2 = (f32[1,3,6,16,640]{4,3,2,1,0:T(8,128)S(1)}, f32[1,3,6,16,640]{4,3,2,1,0:T(8,128)}, u32[]{:S(2)}) copy-start(f32[1,3,6,16,640]{4,3,2,1,0:T(8,128)} %m.3) | copy-start | bytes 2211844
  0.7 16.1 %copy-start.1 = (f32[1,3,6,16,640]{4,3,2,1,0:T(8,128)S(1)}, f32[1,3,6,16,640]{4,3,2,1,0:T(8,128)}, u32[]{:S(2)}) copy-start(f32[1,3,6,16,640]{4,3,2,1,0:T(8,128)} %e.3) | copy-start | bytes 2211844
  1.9 14.3 %collective-permute-start = (f32[24,640]{1,0:T(8,128)S(1)}, f32[24,640]{1,0:T(8,128)S(1)}, u32[]{:S(2)}, u32[]{:S(2)}) collective-permute-start(f32[24,640]{1,0:T(8,128)S(1)} %get-tuple-element.11), channel_id=1, source_target_pairs={{1,2},{3,4},{5,6},{7,8},{9,10},{11,12},{13,14},{15,16},{17,18},{19... | collective-permute-start | bytes 184328 | tf_op jit(solution)/shard_map/ppermute | solution.py:24
  13.6 3.2 %copy-start.7 = (f32[1,3]{1,0:T(1,128)S(1)}, f32[1,3]{1,0:T(1,128)}, u32[]{:S(2)}) copy-start(f32[1,3]{1,0:T(1,128)} %amplitude.1) | copy-start | bytes 40
  13.6 3.1 %collective-permute-start.1 = (f32[24,640]{1,0:T(8,128)S(1)}, f32[24,640]{1,0:T(8,128)S(1)}, u32[]{:S(2)}, u32[]{:S(2)}) collective-permute-start(f32[24,640]{1,0:T(8,128)S(1)} %get-tuple-element.12), channel_id=1, source_target_pairs={{0,1},{2,3},{4,5},{6,7},{8,9},{10,11},{12,13},{14,15},{16,17},{18,... | collective-permute-start | bytes 184328 | tf_op jit(solution)/shard_map/ppermute | solution.py:24
  19.1 7.9 %copy-start.3 = (f32[1,3,6,16,640]{4,3,2,1,0:T(8,128)S(1)}, f32[1,3,6,16,640]{4,3,2,1,0:T(8,128)}, u32[]{:S(2)}) copy-start(f32[1,3,6,16,640]{4,3,2,1,0:T(8,128)} %am.3) | copy-start | bytes 2211844
  19.2 7.9 %copy-start.4 = (s32[6,16,640]{2,1,0:T(8,128)S(1)}, s32[6,16,640]{2,1,0:T(8,128)}, u32[]{:S(2)}) copy-start(s32[6,16,640]{2,1,0:T(8,128)} %labels.3) | copy-start | bytes 737284
  19.2 7.9 %copy-start.5 = (f32[8]{0:T(128)S(1)}, f32[8]{0:T(128)}, u32[]{:S(2)}) copy-start(f32[8]{0:T(128)} %perm.1) | copy-start | bytes 100
  19.2 7.9 %copy-start.6 = (f32[8]{0:T(128)S(1)}, f32[8]{0:T(128)}, u32[]{:S(2)}) copy-start(f32[8]{0:T(128)} %cond.1) | copy-start | bytes 100
  19.2 22.7 %all-to-all-start = ((f32[16,4,16,128]{3,2,1,0:T(8,128)}), f32[16,4,16,128]{3,2,1,0:T(8,128)S(1)}, u32[]{:S(2)}, u32[]{:S(2)}) async-start(f32[16,4,16,128]{3,2,1,0:T(8,128)} %shard_map.122), calls=%async_computation | async-start | bytes 1048576 | tf_op jit(solution)/shard_map/all_to_all | solution.py:345

commit v6 on v4

--- a/solution.py
+++ b/solution.py
@@ -19,9 +19,10 @@
 HBM_BLOCK = None
 
 
-def swap(value, axis, first):
-    pairs = range(first, lax.axis_size(axis) - 1, 2)
-    return lax.ppermute(value, axis, [(i, i + 1) for i in pairs] + [(i + 1, i) for i in pairs])
+def from_behind(value, axis, steps):
+    count = lax.axis_size(axis)
+    first, last = (max(0, -steps), min(count, count - steps))
+    return lax.ppermute(value, axis, [(source, source + steps) for source in range(first, last)])
 
 
 def lane_iota(shape):
@@ -84,7 +85,7 @@
     return widen(source, width), widen(update, width)
 
 
-def edge_kernel(e, m, ae, am, labels, perms, conds, near, far, perm, cond, e_last, m_last, ae_last, am_last, e_first, ae_first, marks, sems):
+def edge_kernel(e, m, ae, am, labels, perms, conds, to_ahead, to_behind, perm, cond, e_last, m_last, ae_last, am_last, e_first, ae_first, marks, sems):
     _, _, depth, rows, width = e.shape
     last = rows - 1
     planes = pl.ds(0, depth)
@@ -103,8 +104,6 @@
     copies = [pltpu.make_async_copy(src, dst, sems.at[i]) for i, (src, dst) in enumerate(moves)]
     for copy in copies:
         copy.start()
-    odd = lax.rem(lax.axis_index("tile"), 2) == 1
-
     def plane_next(value):
         return jnp.where(row_iota(value.shape) < depth - 1, pltpu.roll(value, EDGE - 1, 0), 0.0)
 
@@ -123,20 +122,12 @@
     down = (e_first[0], e_first[1], first_gain * ae_first[0], first_gain * ae_first[1])
     for i, (above, below) in enumerate(zip(up, down, strict=True)):
         at = i * depth
-        near[at : at + depth, :] = jnp.where(odd, below, above)[:depth]
-        far[at : at + depth, :] = jnp.where(odd, above, below)[:depth]
-
-
-def from_tiles(near, far):
-    odd = lax.rem(lax.axis_index("tile"), 2) == 1
-
-    def above(i):
-        return jnp.where(odd, near[i : i + 1, :], far[i : i + 1, :])
-
-    def below(i):
-        return jnp.where(odd, far[i : i + 1, :], near[i : i + 1, :])
-
-    return above, below
+        to_ahead[at : at + depth, :] = above[:depth]
+        to_behind[at : at + depth, :] = below[:depth]
+
+
+def line_of(ref):
+    return lambda i: ref[i : i + 1, :]
 
 
 def pack(planes, share, ports):
@@ -161,11 +152,11 @@
     return blocks
 
 
-def correlation_kernel(ports, e, m, ae, near, far, cells, amplitude, packed, stage, sems):
+def correlation_kernel(ports, e, m, ae, behind, ahead, cells, amplitude, packed, stage, sems):
     _, _, depth, rows, width = e.shape
     share = width // ports
     tile = lax.axis_index("tile")
-    above, below = from_tiles(near, far)
+    above, below = line_of(behind), line_of(ahead)
     plane_cells = lax.axis_size("tile") * rows * width
     target = cells[0] - tile * (rows * width)
     inside = jnp.where(tile > 0, 1.0, 0.0)
@@ -226,11 +217,11 @@
             factors[i, group] = look_up(mine, entries)
 
 
-def field_kernel(ports, ae, am, labels, near, far, perm, cond, new_e, new_m, factors):
+def field_kernel(ports, ae, am, labels, behind, ahead, perm, cond, new_e, new_m, factors):
     depth, rows, width = labels.shape
     share_factors(ports, labels, perm, cond, factors)
     source, update = gains(perm, cond, width)
-    above, below = from_tiles(near, far)
+    above, below = line_of(behind), line_of(ahead)
     inside = jnp.where(lax.axis_index("tile") > 0, 1.0, 0.0)
     zero = jnp.zeros((rows, width), jnp.float32)
 
@@ -317,7 +308,7 @@
         return jax.ShapeDtypeStruct(shape, jnp.float32)
 
     edge = array(4 * depth, width)
-    near, far = call(
+    to_ahead, to_behind = call(
         edge_kernel,
         (electric, magnetic, adjoint_electric, adjoint_magnetic, region_labels, permittivity_table, conductivity_table),
         (HBM,) * 7,
@@ -329,11 +320,12 @@
             VMEM((count, EDGE, width), jnp.float32) for count in (3, 2, 3, 2, 2, 2)
         ] + [VMEM((2, EDGE, width), jnp.int32), pltpu.SemaphoreType.DMA((10,))],
     )
-    near, far = swap(near, "tile", 0), swap(far, "tile", 1)
+    behind = from_behind(to_ahead, "tile", 1)
+    ahead = from_behind(to_behind, "tile", -1)
     shares = array(ports, 2 * depth // PLANES, rows, LANES)
     (packed,) = call(
         functools.partial(correlation_kernel, ports),
-        (electric, magnetic, adjoint_electric, near, far, port_cells, port_amplitude),
+        (electric, magnetic, adjoint_electric, behind, ahead, port_cells, port_amplitude),
         (VMEM,) * 5 + (SMEM,) * 2,
         (shares,),
         (HBM,),
@@ -344,7 +336,7 @@
     gathered = lax.all_to_all(packed, "port", 0, 0, tiled=True)
     new_electric, new_magnetic, factors = call(
         functools.partial(field_kernel, ports),
-        (adjoint_electric, adjoint_magnetic, region_labels, near, far, permittivity_table, conductivity_table),
+        (adjoint_electric, adjoint_magnetic, region_labels, behind, ahead, permittivity_table, conductivity_table),
         (VMEM, HBM_BLOCK, HBM_BLOCK, VMEM, VMEM) + (SMEM,) * 2,
         (array(1, 3, depth, rows, width), array(1, 3, depth, rows, width), array(3, depth // PLANES, rows, LANES)),
         (HBM_BLOCK, HBM_BLOCK, VMEM),

time: 39.8 us -> 39.1 us (0.982)
  starting transfers between devices: 21.7 us -> 21.1 us
    ppermute x2, starting transfers between devices: 14.3 us -> 13.7 us  [from_behind(): lax.ppermute(value, axis, [(source, source + steps) for source in range(f...]
where the time goes in v6:
time: 39.1 us; the launch traced here: 38.8 us
  starting transfers between devices  21.1 us (54%)
  waiting for transfers between devices  9.42 us (24%)
  Pallas kernels  6.76 us (17%)
  between operations  1.41 us (4%)
    ppermute x2, starting transfers between devices, from_behind(): lax.ppermute(value, axis, [(source, source + steps) for source in range(f...  13.7 us
    all_to_all x1, waiting for transfers between devices, on_device(): gathered = lax.all_to_all(packed, 'port', 0, 0, tiled=True)  7.89 us
    all_to_all x1, starting transfers between devices, on_device(): gathered = lax.all_to_all(packed, 'port', 0, 0, tiled=True)  7.5 us
    pallas_call x4, Pallas kernels, call(): pl.pallas_call(kernel, out_shape=tuple((space(out.shape, out.dtype) if sp...  6.76 us
    ppermute x2, waiting for transfers between devices, from_behind(): lax.ppermute(value, axis, [(source, source + steps) for source in range(f...  1.53 us
  transfers between devices with their start and end apart: 3, of which 2 were waited for; matrix products, arithmetic and copies ran while one was open for 0% of the time, Pallas kernels for 6%

profile of v6, /device:TPU:48, one launch (start us, length us, event | category | flops | bytes accessed | tf_op | source)
XLA Modules:
  0.0 38.8 jit_solution(16577888594895548847)
XLA Ops:
  0.6 0.0 copy-start
  0.6 0.0 copy-start.2
  0.7 0.0 copy-start.1
  0.7 1.2 %shard_map.120 = (f32[24,640]{1,0:T(8,128)S(1)}, f32[24,640]{1,0:T(8,128)S(1)}) custom-call(f32[1,3,6,16,640]{4,3,2,1,0:T(8,128)} %e.3, f32[1,3,6,16,640]{4,3,2,1,0:T(8,128)} %m.3, f32[1,3,6,16,640]{4,3,2,1,0:T(8,128)} %ae.5, f32[1,3,6,16,640]{4,3,2,1,0:T(8,128)} %am.3, s32[6,16,640]{2,1,0:T(8,128)} %labels.3, f32[8]{0:T(128)} %perm.1, f32[8]{0:T(128)} %cond.1), custom_call_target="tpu_custom_call" | custom-call | flops 614400 | bytes 3440640 | tf_op jit(solution)/shard_map/pallas_call | solution.py:280
  1.9 1.9 %collective-permute-start = (f32[24,640]{1,0:T(8,128)S(1)}, f32[24,640]{1,0:T(8,128)S(1)}, u32[]{:S(2)}, u32[]{:S(2)}) collective-permute-start(f32[24,640]{1,0:T(8,128)S(1)} %get-tuple-element.11), channel_id=1, source_target_pairs={{0,1},{1,2},{2,3},{3,4},{4,5},{5,6},{6,7},{7,8},{8,9},{9,10},{10,1... | collective-permute-start | bytes 184328 | tf_op jit(solution)/shard_map/ppermute | solution.py:25
  3.8 0.0 copy-start.7
  3.8 11.7 %collective-permute-start.1 = (f32[24,640]{1,0:T(8,128)S(1)}, f32[24,640]{1,0:T(8,128)S(1)}, u32[]{:S(2)}, u32[]{:S(2)}) collective-permute-start(f32[24,640]{1,0:T(8,128)S(1)} %get-tuple-element.12), channel_id=1, source_target_pairs={{1,0},{2,1},{3,2},{4,3},{5,4},{6,5},{7,6},{8,7},{9,8},{10,9},{11,1... | collective-permute-start | bytes 184328 | tf_op jit(solution)/shard_map/ppermute | solution.py:25
  16.2 0.0 collective-permute-done.behind
  16.2 1.5 %collective-permute-done.1.ahead = f32[24,640]{1,0:T(8,128)S(1)} collective-permute-done((f32[24,640]{1,0:T(8,128)S(1)}, f32[24,640]{1,0:T(8,128)S(1)}, u32[]{:S(2)}, u32[]{:S(2)}) %collective-permute-start.1) | collective-permute-done | bytes 61472 | tf_op jit(solution)/shard_map/ppermute | solution.py:25
  17.8 0.0 copy-done
  17.8 0.0 copy-done.2
  17.8 0.0 copy-done.1
  17.8 0.0 copy-done.7
  17.8 2.3 %shard_map.122 = f32[16,4,16,128]{3,2,1,0:T(8,128)} custom-call(f32[1,3,6,16,640]{4,3,2,1,0:T(8,128)S(1)} %copy-done.1, f32[1,3,6,16,640]{4,3,2,1,0:T(8,128)S(1)} %copy-done.2, f32[1,3,6,16,640]{4,3,2,1,0:T(8,128)S(1)} %copy-done, f32[24,640]{1,0:T(8,128)S(1)} %collective-permute-done.behind, f32[24,640]{1,0:T(8,128)S(1)} %collective-permute-done.1.ahead, ...), custom_call_target="tpu_custom_call" | custom-call | flops 3686400 | bytes 2703360 | tf_op jit(solution)/shard_map/pallas_call | solution.py:280
  20.1 0.0 copy-start.3
  20.1 0.0 copy-start.4
  20.1 0.0 copy-start.5
  20.2 0.0 copy-start.6
  20.2 7.5 %all-to-all-start = ((f32[16,4,16,128]{3,2,1,0:T(8,128)}), f32[16,4,16,128]{3,2,1,0:T(8,128)S(1)}, u32[]{:S(2)}, u32[]{:S(2)}) async-start(f32[16,4,16,128]{3,2,1,0:T(8,128)} %shard_map.122), calls=%async_computation | async-start | bytes 1048576 | tf_op jit(solution)/shard_map/all_to_all | solution.py:336
  27.7 0.0 copy-done.3
  27.7 0.0 copy-done.4
  27.7 0.0 copy-done.5
  27.7 0.0 copy-done.6
  27.7 2.4 %shard_map.121 = (f32[1,3,6,16,640]{4,3,2,1,0:T(8,128)}, f32[1,3,6,16,640]{4,3,2,1,0:T(8,128)}, f32[3,2,16,128]{3,2,1,0:T(8,128)S(1)}) custom-call(f32[1,3,6,16,640]{4,3,2,1,0:T(8,128)S(1)} %copy-done, f32[1,3,6,16,640]{4,3,2,1,0:T(8,128)S(1)} %copy-done.3, s32[6,16,640]{2,1,0:T(8,128)S(1)} %copy-done.4, f32[24,640]{1,0:T(8,128)S(1)} %collective-permute-done.behind, ...), custom_call_target="tpu_custom_call" | custom-call | flops 4915200 | bytes 3194880 | tf_op jit(solution)/shard_map/pallas_call | solution.py:280
  30.1 7.9 %all-to-all-done.gathered = f32[16,4,16,128]{3,2,1,0:T(8,128)S(1)} async-done(((f32[16,4,16,128]{3,2,1,0:T(8,128)}), f32[16,4,16,128]{3,2,1,0:T(8,128)S(1)}, u32[]{:S(2)}, u32[]{:S(2)}) %all-to-all-start) | async-done | bytes 524320 | tf_op jit(solution)/shard_map/all_to_all | solution.py:336
  38.0 0.7 %shard_map.123 = (f32[6,16,40]{2,1,0:T(8,128)}, f32[6,16,40]{2,1,0:T(8,128)}) custom-call(f32[16,4,16,128]{3,2,1,0:T(8,128)S(1)} %all-to-all-done.gathered, f32[3,2,16,128]{3,2,1,0:T(8,128)S(1)} %get-tuple-element.15.factors), custom_call_target="tpu_custom_call" | custom-call | flops 245760 | bytes 737280 | tf_op jit(solution)/shard_map/pallas_call | solution.py:280
Async XLA Ops:
  0.6 17.1 %copy-start = (f32[1,3,6,16,640]{4,3,2,1,0:T(8,128)S(1)}, f32[1,3,6,16,640]{4,3,2,1,0:T(8,128)}, u32[]{:S(2)}) copy-start(f32[1,3,6,16,640]{4,3,2,1,0:T(8,128)} %ae.5) | copy-start | bytes 2211844
  0.6 17.1 %copy-start.2 = (f32[1,3,6,16,640]{4,3,2,1,0:T(8,128)S(1)}, f32[1,3,6,16,640]{4,3,2,1,0:T(8,128)}, u32[]{:S(2)}) copy-start(f32[1,3,6,16,640]{4,3,2,1,0:T(8,128)} %m.3) | copy-start | bytes 2211844
  0.7 17.1 %copy-start.1 = (f32[1,3,6,16,640]{4,3,2,1,0:T(8,128)S(1)}, f32[1,3,6,16,640]{4,3,2,1,0:T(8,128)}, u32[]{:S(2)}) copy-start(f32[1,3,6,16,640]{4,3,2,1,0:T(8,128)} %e.3) | copy-start | bytes 2211844
  1.9 14.3 %collective-permute-start = (f32[24,640]{1,0:T(8,128)S(1)}, f32[24,640]{1,0:T(8,128)S(1)}, u32[]{:S(2)}, u32[]{:S(2)}) collective-permute-start(f32[24,640]{1,0:T(8,128)S(1)} %get-tuple-element.11), channel_id=1, source_target_pairs={{0,1},{1,2},{2,3},{3,4},{4,5},{5,6},{6,7},{7,8},{8,9},{9,10},{10,1... | collective-permute-start | bytes 184328 | tf_op jit(solution)/shard_map/ppermute | solution.py:25
  3.8 13.9 %copy-start.7 = (f32[1,3]{1,0:T(1,128)S(1)}, f32[1,3]{1,0:T(1,128)}, u32[]{:S(2)}) copy-start(f32[1,3]{1,0:T(1,128)} %amplitude.1) | copy-start | bytes 40
  3.8 13.9 %collective-permute-start.1 = (f32[24,640]{1,0:T(8,128)S(1)}, f32[24,640]{1,0:T(8,128)S(1)}, u32[]{:S(2)}, u32[]{:S(2)}) collective-permute-start(f32[24,640]{1,0:T(8,128)S(1)} %get-tuple-element.12), channel_id=1, source_target_pairs={{1,0},{2,1},{3,2},{4,3},{5,4},{6,5},{7,6},{8,7},{9,8},{10,9},{11,1... | collective-permute-start | bytes 184328 | tf_op jit(solution)/shard_map/ppermute | solution.py:25
  20.1 7.5 %copy-start.3 = (f32[1,3,6,16,640]{4,3,2,1,0:T(8,128)S(1)}, f32[1,3,6,16,640]{4,3,2,1,0:T(8,128)}, u32[]{:S(2)}) copy-start(f32[1,3,6,16,640]{4,3,2,1,0:T(8,128)} %am.3) | copy-start | bytes 2211844
  20.1 7.5 %copy-start.4 = (s32[6,16,640]{2,1,0:T(8,128)S(1)}, s32[6,16,640]{2,1,0:T(8,128)}, u32[]{:S(2)}) copy-start(s32[6,16,640]{2,1,0:T(8,128)} %labels.3) | copy-start | bytes 737284
  20.1 7.5 %copy-start.5 = (f32[8]{0:T(128)S(1)}, f32[8]{0:T(128)}, u32[]{:S(2)}) copy-start(f32[8]{0:T(128)} %perm.1) | copy-start | bytes 100
  20.2 7.5 %copy-start.6 = (f32[8]{0:T(128)S(1)}, f32[8]{0:T(128)}, u32[]{:S(2)}) copy-start(f32[8]{0:T(128)} %cond.1) | copy-start | bytes 100
  20.2 17.9 %all-to-all-start = ((f32[16,4,16,128]{3,2,1,0:T(8,128)}), f32[16,4,16,128]{3,2,1,0:T(8,128)S(1)}, u32[]{:S(2)}, u32[]{:S(2)}) async-start(f32[16,4,16,128]{3,2,1,0:T(8,128)} %shard_map.122), calls=%async_computation | async-start | bytes 1048576 | tf_op jit(solution)/shard_map/all_to_all | solution.py:336

commit v7 on v6

--- a/solution.py
+++ b/solution.py
@@ -85,10 +85,12 @@
     return widen(source, width), widen(update, width)
 
 
-def edge_kernel(e, m, ae, am, labels, perms, conds, to_ahead, to_behind, perm, cond, e_last, m_last, ae_last, am_last, e_first, ae_first, marks, sems):
+def edge_kernel(e, m, ae, am, labels, perms, conds, to_ahead, to_behind, ae_last, ae_first, e_first, perm, cond, e_last, m_last, am_last, marks, sems):
     _, _, depth, rows, width = e.shape
     last = rows - 1
     planes = pl.ds(0, depth)
+    for ref in (ae_last, ae_first, e_first, e_last, m_last, am_last):
+        ref[:, depth:, :] = jnp.zeros((ref.shape[0], EDGE - depth, width), jnp.float32)
     moves = (
         (perms, perm),
         (conds, cond),
@@ -105,7 +107,7 @@
     for copy in copies:
         copy.start()
     def plane_next(value):
-        return jnp.where(row_iota(value.shape) < depth - 1, pltpu.roll(value, EDGE - 1, 0), 0.0)
+        return pltpu.roll(value, EDGE - 1, 0)
 
     for copy in copies:
         copy.wait()
@@ -152,14 +154,13 @@
     return blocks
 
 
-def correlation_kernel(ports, e, m, ae, behind, ahead, cells, amplitude, packed, stage, sems):
+def correlation_kernel(ports, e, m, ae, cells, amplitude, packed, base, stage, sems):
     _, _, depth, rows, width = e.shape
     share = width // ports
+    groups = depth // PLANES
     tile = lax.axis_index("tile")
-    above, below = line_of(behind), line_of(ahead)
     plane_cells = lax.axis_size("tile") * rows * width
     target = cells[0] - tile * (rows * width)
-    inside = jnp.where(tile > 0, 1.0, 0.0)
     position = row_iota((rows, width)) * width + lane_iota((rows, width))
 
     def at(ref, c, z):
@@ -170,16 +171,13 @@
     sums_a, sums_b, copies = [], [], []
     for z in range(depth):
         ex, ey, ez = (at(e, c, z) for c in range(3))
-        next_y, next_z = below(z), below(depth + z)
         fx = at(m, 0, z) - TIMESTEP * ((lane_next(ez) - ez) - (at(e, 1, z + 1) - ey))
-        fy = at(m, 1, z) - TIMESTEP * ((at(e, 0, z + 1) - ex) - (row_next(ez, next_z) - ez))
-        fz = at(m, 2, z) - TIMESTEP * ((row_next(ey, next_y) - ey) - (lane_next(ex) - ex))
-        prev_y = inside * (above(z) + TIMESTEP * ez[0:1])
-        prev_z = inside * (above(depth + z) - TIMESTEP * ey[0:1])
+        fy = at(m, 1, z) - TIMESTEP * ((at(e, 0, z + 1) - ex) - (row_next(ez, 0.0) - ez))
+        fz = at(m, 2, z) - TIMESTEP * ((row_next(ey, 0.0) - ey) - (lane_next(ex) - ex))
         hit = position == target - z * plane_cells
         drive_x = ((fz - lane_prev(fz)) - (fy - fy_prev)) - jnp.where(hit, amplitude[0, 0], 0.0)
-        drive_y = ((fx - fx_prev) - (fz - row_prev(fz, prev_z))) - jnp.where(hit, amplitude[0, 1], 0.0)
-        drive_z = ((fy - row_prev(fy, prev_y)) - (fx - lane_prev(fx))) - jnp.where(
+        drive_y = ((fx - fx_prev) - (fz - row_prev(fz, 0.0))) - jnp.where(hit, amplitude[0, 1], 0.0)
+        drive_z = ((fy - row_prev(fy, 0.0)) - (fx - lane_prev(fx))) - jnp.where(
             hit, amplitude[0, 2], 0.0
         )
         ax, ay, az = (at(ae, c, z) for c in range(3))
@@ -192,9 +190,53 @@
                 slab = f * (depth // PLANES) + group
                 for port, block in enumerate(pack(sums, share, ports)):
                     stage[port, slab] = block
+                    if f == 1:
+                        base[port, group : group + 1] = block[:1]
+                        base[port, groups + group : groups + group + 1] = block[rows - 1 :]
                 copies.append(pltpu.make_async_copy(stage.at[:, slab], packed.at[:, slab], sems.at[slab]))
                 copies[-1].start()
             sums_a, sums_b = [], []
+    for copy in copies:
+        copy.wait()
+
+
+def rim_kernel(ports, behind, ahead, ae_last, ae_first, e_first, base, packed, patched, stage, sems):
+    del packed
+    depth = behind.shape[0] // 4
+    width = behind.shape[1]
+    rows = patched.shape[2]
+    groups = depth // PLANES
+    share = width // ports
+    inside = jnp.where(lax.axis_index("tile") > 0, 1.0, 0.0)
+
+    def part(ref, i):
+        return ref[i * depth : (i + 1) * depth, :]
+
+    at_y, at_z = TIMESTEP * part(ahead, 1), -TIMESTEP * part(ahead, 0)
+    plane_before = jnp.concatenate([jnp.zeros((1, width), jnp.float32), at_y[:-1]], axis=0)
+    drive_x = (at_z - lane_prev(at_z)) - (at_y - plane_before)
+    ax, ay, az = (ae_last[c, :depth] for c in range(3))
+    last = ax * drive_x - ay * at_z + az * at_y
+    prev_y = inside * (part(behind, 0) + TIMESTEP * e_first[1, :depth])
+    prev_z = inside * (part(behind, 1) - TIMESTEP * e_first[0, :depth])
+    first = ae_first[0, :depth] * prev_z - ae_first[1, :depth] * prev_y
+    planes = [
+        jnp.concatenate(
+            [side[g * PLANES + j : g * PLANES + j + 1] for side in (first, last) for g in range(groups)], axis=0
+        )
+        for j in range(PLANES)
+    ]
+    for port, block in enumerate(pack(planes, share, ports)):
+        stage[port] = base[port, : 2 * groups] + block
+    copies = [
+        pltpu.make_async_copy(
+            stage.at[:, side * groups + g], patched.at[:, groups + g, side * (rows - 1)], sems.at[side * groups + g]
+        )
+        for side in range(2)
+        for g in range(groups)
+    ]
+    for copy in copies:
+        copy.start()
     for copy in copies:
         copy.wait()
 
@@ -275,14 +317,15 @@
                 ref[group * PLANES + j] = moved[:, :share]
 
 
-def call(kernel, inputs, spaces, outs, out_spaces, flops, moved, scratch=()):
+def call(kernel, inputs, spaces, outs, out_spaces, flops, moved, scratch=(), aliases=()):
     inputs = [pltpu.with_memory_space_constraint(x, space) if space in (VMEM, HBM) else x for x, space in zip(inputs, spaces, strict=True)]
     return pl.pallas_call(
         kernel,
-        out_shape=tuple(space(out.shape, out.dtype) if space is VMEM else out for out, space in zip(outs, out_spaces, strict=True)),
+        out_shape=tuple(space(out.shape, out.dtype) if space in (VMEM, HBM) else out for out, space in zip(outs, out_spaces, strict=True)),
         in_specs=[pl.BlockSpec(memory_space=VMEM if space is HBM_BLOCK else space) for space in spaces],
         out_specs=tuple(pl.BlockSpec(memory_space=VMEM if space is HBM_BLOCK else space) for space in out_spaces),
         scratch_shapes=scratch,
+        input_output_aliases=dict(aliases),
         compiler_params=pltpu.CompilerParams(vmem_limit_bytes=VMEM_LIMIT),
         cost_estimate=pl.CostEstimate(flops=flops, bytes_accessed=moved, transcendentals=0),
     )(*inputs)
@@ -308,30 +351,42 @@
         return jax.ShapeDtypeStruct(shape, jnp.float32)
 
     edge = array(4 * depth, width)
-    to_ahead, to_behind = call(
+    to_ahead, to_behind, *kept = call(
         edge_kernel,
         (electric, magnetic, adjoint_electric, adjoint_magnetic, region_labels, permittivity_table, conductivity_table),
         (HBM,) * 7,
-        (edge, edge),
-        (VMEM, VMEM),
+        (edge, edge) + tuple(array(count, EDGE, width) for count in (3, 2, 2)),
+        (VMEM,) * 5,
         10 * cells,
         cells * 4 * 14,
         [SMEM(permittivity_table.shape, jnp.float32)] * 2 + [
-            VMEM((count, EDGE, width), jnp.float32) for count in (3, 2, 3, 2, 2, 2)
+            VMEM((count, EDGE, width), jnp.float32) for count in (3, 2, 2)
         ] + [VMEM((2, EDGE, width), jnp.int32), pltpu.SemaphoreType.DMA((10,))],
     )
     behind = from_behind(to_ahead, "tile", 1)
     ahead = from_behind(to_behind, "tile", -1)
     shares = array(ports, 2 * depth // PLANES, rows, LANES)
+    sems = pltpu.SemaphoreType.DMA((shares.shape[1],))
+    packed, base = call(
+        functools.partial(correlation_kernel, ports),
+        (electric, magnetic, adjoint_electric, port_cells, port_amplitude),
+        (VMEM,) * 3 + (SMEM,) * 2,
+        (shares, array(ports, EDGE, LANES)),
+        (HBM, VMEM),
+        60 * cells,
+        cells * 4 * 11,
+        [VMEM(shares.shape, jnp.float32), sems],
+    )
     (packed,) = call(
-        functools.partial(correlation_kernel, ports),
-        (electric, magnetic, adjoint_electric, behind, ahead, port_cells, port_amplitude),
-        (VMEM,) * 5 + (SMEM,) * 2,
+        functools.partial(rim_kernel, ports),
+        (behind, ahead, *kept, base, packed),
+        (VMEM,) * 6 + (HBM,),
         (shares,),
         (HBM,),
-        60 * cells,
-        cells * 4 * 11,
-        [VMEM(shares.shape, jnp.float32), pltpu.SemaphoreType.DMA((shares.shape[1],))],
+        2 * cells,
+        cells,
+        [VMEM((ports, 2 * depth // PLANES, LANES), jnp.float32), sems],
+        {6: 0},
     )
     gathered = lax.all_to_all(packed, "port", 0, 0, tiled=True)
     new_electric, new_magnetic, factors = call(

time: 39.1 us -> 38.7 us (0.990)
  waiting for transfers between devices: 9.42 us -> 7.86 us
  Pallas kernels: 6.76 us -> 7.63 us
  starting transfers between devices: 21.1 us -> 21.5 us
    ppermute x2, waiting for transfers between devices: 1.53 us -> 0.01 us  [from_behind(): lax.ppermute(value, axis, [(source, source + steps) for source in range(f...]
    pallas_call x4 -> x5, Pallas kernels: 6.76 us -> 7.63 us  [call(): pl.pallas_call(kernel, out_shape=tuple((space(out.shape, out.dtype) if sp...]
  transfers between devices with their start and end apart: 3 -> 3, of which waited for: 2 -> 1; matrix products, arithmetic and copies ran while one was open for 0% -> 0% of each run, Pallas kernels for 6% -> 12%
where the time goes in v7:
time: 38.7 us; the launch traced here: 38.5 us
  starting transfers between devices  21.5 us (56%)
  waiting for transfers between devices  7.86 us (20%)
  Pallas kernels  7.63 us (20%)
  between operations  1.46 us (4%)
    ppermute x2, starting transfers between devices, from_behind(): lax.ppermute(value, axis, [(source, source + steps) for source in range(f...  13.7 us
    all_to_all x1, waiting for transfers between devices, on_device(): gathered = lax.all_to_all(packed, 'port', 0, 0, tiled=True)  7.85 us
    all_to_all x1, starting transfers between devices, on_device(): gathered = lax.all_to_all(packed, 'port', 0, 0, tiled=True)  7.83 us
    pallas_call x5, Pallas kernels, call(): pl.pallas_call(kernel, out_shape=tuple((space(out.shape, out.dtype) if sp...  7.63 us
  transfers between devices with their start and end apart: 3, of which 1 were waited for; matrix products, arithmetic and copies ran while one was open for 0% of the time, Pallas kernels for 12%

profile of v7, /device:TPU:48, one launch (start us, length us, event | category | flops | bytes accessed | tf_op | source)
XLA Modules:
  0.0 38.5 jit_solution(3235808221893732701)
XLA Ops:
  0.6 0.0 copy-start
  0.6 0.0 copy-start.3
  0.7 0.0 copy-start.2
  0.7 1.2 %shard_map.120 = (f32[24,640]{1,0:T(8,128)S(1)}, f32[24,640]{1,0:T(8,128)S(1)}, f32[3,8,640]{2,1,0:T(8,128)S(1)}, f32[2,8,640]{2,1,0:T(8,128)S(1)}, f32[2,8,640]{2,1,0:T(8,128)S(1)}) custom-call(f32[1,3,6,16,640]{4,3,2,1,0:T(8,128)} %e.3, f32[1,3,6,16,640]{4,3,2,1,0:T(8,128)} %m.3, f32[1,3,6,16,640]{4,3,2,1,0:T(8,128)} %ae.5, f32[1,3,6,16,640]{4,3,2,1,0:T(8,128)} %am.3, ...), custom_call_target="tpu_custom_call" | custom-call | flops 614400 | bytes 3440640 | tf_op jit(solution)/shard_map/pallas_call | solution.py:322
  1.9 1.9 %collective-permute-start = (f32[24,640]{1,0:T(8,128)S(1)}, f32[24,640]{1,0:T(8,128)S(1)}, u32[]{:S(2)}, u32[]{:S(2)}) collective-permute-start(f32[24,640]{1,0:T(8,128)S(1)} %get-tuple-element.16), channel_id=1, source_target_pairs={{0,1},{1,2},{2,3},{3,4},{4,5},{5,6},{6,7},{7,8},{8,9},{9,10},{10,1... | collective-permute-start | bytes 184328 | tf_op jit(solution)/shard_map/ppermute | solution.py:25
  3.8 0.0 copy-start.7
  3.9 11.7 %collective-permute-start.1 = (f32[24,640]{1,0:T(8,128)S(1)}, f32[24,640]{1,0:T(8,128)S(1)}, u32[]{:S(2)}, u32[]{:S(2)}) collective-permute-start(f32[24,640]{1,0:T(8,128)S(1)} %get-tuple-element.17), channel_id=1, source_target_pairs={{1,0},{2,1},{3,2},{4,3},{5,4},{6,5},{7,6},{8,7},{9,8},{10,9},{11,1... | collective-permute-start | bytes 184328 | tf_op jit(solution)/shard_map/ppermute | solution.py:25
  16.2 0.0 copy-done
  16.3 0.0 copy-done.3
  16.3 0.0 copy-done.2
  16.3 0.0 copy-done.7
  16.3 2.3 %shard_map.122 = (f32[16,4,16,128]{3,2,1,0:T(8,128)}, f32[16,8,128]{2,1,0:T(8,128)S(1)}) custom-call(f32[1,3,6,16,640]{4,3,2,1,0:T(8,128)S(1)} %copy-done.2, f32[1,3,6,16,640]{4,3,2,1,0:T(8,128)S(1)} %copy-done.3, f32[1,3,6,16,640]{4,3,2,1,0:T(8,128)S(1)} %copy-done, s32[1]{0:T(128)S(6)} %copy.15.cells, f32[1,3]{1,0:T(1,128)S(1)} %copy-done.7), custom_call_target="tpu_custom_call" | custom-call | flops 3686400 | bytes 2703360 | tf_op jit(solution)/shard_map/pallas_call | solution.py:322
  18.6 0.0 collective-permute-done.behind
  18.6 0.0 collective-permute-done.1.ahead
  18.6 0.8 %shard_map.123 = f32[16,4,16,128]{3,2,1,0:T(8,128)} custom-call(f32[24,640]{1,0:T(8,128)S(1)} %collective-permute-done.behind, f32[24,640]{1,0:T(8,128)S(1)} %collective-permute-done.1.ahead, f32[3,8,640]{2,1,0:T(8,128)S(1)} %get-tuple-element.20.ae_last, f32[2,8,640]{2,1,0:T(8,128)S(1)} %get-tuple-element.21.ae_first, ...), custom_call_target="tpu_custom_call", output_to_operand_aliasing={{}: (6, {})} | custom-call | flops 122880 | bytes 61440 | tf_op jit(solution)/shard_map/pallas_call | solution.py:322
  19.5 0.0 copy-start.1
  19.5 0.0 copy-start.4
  19.5 0.0 copy-start.5
  19.5 0.0 copy-start.6
  19.5 7.8 %all-to-all-start = ((f32[16,4,16,128]{3,2,1,0:T(8,128)}), f32[16,4,16,128]{3,2,1,0:T(8,128)S(1)}, u32[]{:S(2)}, u32[]{:S(2)}) async-start(f32[16,4,16,128]{3,2,1,0:T(8,128)} %shard_map.123), calls=%async_computation | async-start | bytes 1048576 | tf_op jit(solution)/shard_map/all_to_all | solution.py:391
  27.4 0.0 copy-done.1
  27.4 0.0 copy-done.4
  27.4 0.0 copy-done.5
  27.4 0.0 copy-done.6
  27.4 2.5 %shard_map.121 = (f32[1,3,6,16,640]{4,3,2,1,0:T(8,128)}, f32[1,3,6,16,640]{4,3,2,1,0:T(8,128)}, f32[3,2,16,128]{3,2,1,0:T(8,128)S(1)}) custom-call(f32[1,3,6,16,640]{4,3,2,1,0:T(8,128)S(1)} %copy-done, f32[1,3,6,16,640]{4,3,2,1,0:T(8,128)S(1)} %copy-done.1, s32[6,16,640]{2,1,0:T(8,128)S(1)} %copy-done.4, f32[24,640]{1,0:T(8,128)S(1)} %collective-permute-done.behind, ...), custom_call_target="tpu_custom_call" | custom-call | flops 4915200 | bytes 3194880 | tf_op jit(solution)/shard_map/pallas_call | solution.py:322
  29.9 7.9 %all-to-all-done.gathered = f32[16,4,16,128]{3,2,1,0:T(8,128)S(1)} async-done(((f32[16,4,16,128]{3,2,1,0:T(8,128)}), f32[16,4,16,128]{3,2,1,0:T(8,128)S(1)}, u32[]{:S(2)}, u32[]{:S(2)}) %all-to-all-start) | async-done | bytes 524320 | tf_op jit(solution)/shard_map/all_to_all | solution.py:391
  37.7 0.7 %shard_map.124 = (f32[6,16,40]{2,1,0:T(8,128)}, f32[6,16,40]{2,1,0:T(8,128)}) custom-call(f32[16,4,16,128]{3,2,1,0:T(8,128)S(1)} %all-to-all-done.gathered, f32[3,2,16,128]{3,2,1,0:T(8,128)S(1)} %get-tuple-element.25.factors), custom_call_target="tpu_custom_call" | custom-call | flops 245760 | bytes 737280 | tf_op jit(solution)/shard_map/pallas_call | solution.py:322
Async XLA Ops:
  0.6 15.6 %copy-start = (f32[1,3,6,16,640]{4,3,2,1,0:T(8,128)S(1)}, f32[1,3,6,16,640]{4,3,2,1,0:T(8,128)}, u32[]{:S(2)}) copy-start(f32[1,3,6,16,640]{4,3,2,1,0:T(8,128)} %ae.5) | copy-start | bytes 2211844
  0.6 15.6 %copy-start.3 = (f32[1,3,6,16,640]{4,3,2,1,0:T(8,128)S(1)}, f32[1,3,6,16,640]{4,3,2,1,0:T(8,128)}, u32[]{:S(2)}) copy-start(f32[1,3,6,16,640]{4,3,2,1,0:T(8,128)} %m.3) | copy-start | bytes 2211844
  0.7 15.6 %copy-start.2 = (f32[1,3,6,16,640]{4,3,2,1,0:T(8,128)S(1)}, f32[1,3,6,16,640]{4,3,2,1,0:T(8,128)}, u32[]{:S(2)}) copy-start(f32[1,3,6,16,640]{4,3,2,1,0:T(8,128)} %e.3) | copy-start | bytes 2211844
  1.9 16.7 %collective-permute-start = (f32[24,640]{1,0:T(8,128)S(1)}, f32[24,640]{1,0:T(8,128)S(1)}, u32[]{:S(2)}, u32[]{:S(2)}) collective-permute-start(f32[24,640]{1,0:T(8,128)S(1)} %get-tuple-element.16), channel_id=1, source_target_pairs={{0,1},{1,2},{2,3},{3,4},{4,5},{5,6},{6,7},{7,8},{8,9},{9,10},{10,1... | collective-permute-start | bytes 184328 | tf_op jit(solution)/shard_map/ppermute | solution.py:25
  3.8 12.4 %copy-start.7 = (f32[1,3]{1,0:T(1,128)S(1)}, f32[1,3]{1,0:T(1,128)}, u32[]{:S(2)}) copy-start(f32[1,3]{1,0:T(1,128)} %amplitude.1) | copy-start | bytes 40
  3.9 14.8 %collective-permute-start.1 = (f32[24,640]{1,0:T(8,128)S(1)}, f32[24,640]{1,0:T(8,128)S(1)}, u32[]{:S(2)}, u32[]{:S(2)}) collective-permute-start(f32[24,640]{1,0:T(8,128)S(1)} %get-tuple-element.17), channel_id=1, source_target_pairs={{1,0},{2,1},{3,2},{4,3},{5,4},{6,5},{7,6},{8,7},{9,8},{10,9},{11,1... | collective-permute-start | bytes 184328 | tf_op jit(solution)/shard_map/ppermute | solution.py:25
  19.5 7.9 %copy-start.1 = (f32[1,3,6,16,640]{4,3,2,1,0:T(8,128)S(1)}, f32[1,3,6,16,640]{4,3,2,1,0:T(8,128)}, u32[]{:S(2)}) copy-start(f32[1,3,6,16,640]{4,3,2,1,0:T(8,128)} %am.3) | copy-start | bytes 2211844
  19.5 7.9 %copy-start.4 = (s32[6,16,640]{2,1,0:T(8,128)S(1)}, s32[6,16,640]{2,1,0:T(8,128)}, u32[]{:S(2)}) copy-start(s32[6,16,640]{2,1,0:T(8,128)} %labels.3) | copy-start | bytes 737284
  19.5 7.9 %copy-start.5 = (f32[8]{0:T(128)S(1)}, f32[8]{0:T(128)}, u32[]{:S(2)}) copy-start(f32[8]{0:T(128)} %perm.1) | copy-start | bytes 100
  19.5 7.9 %copy-start.6 = (f32[8]{0:T(128)S(1)}, f32[8]{0:T(128)}, u32[]{:S(2)}) copy-start(f32[8]{0:T(128)} %cond.1) | copy-start | bytes 100
  19.5 18.2 %all-to-all-start = ((f32[16,4,16,128]{3,2,1,0:T(8,128)}), f32[16,4,16,128]{3,2,1,0:T(8,128)S(1)}, u32[]{:S(2)}, u32[]{:S(2)}) async-start(f32[16,4,16,128]{3,2,1,0:T(8,128)} %shard_map.123), calls=%async_computation | async-start | bytes 1048576 | tf_op jit(solution)/shard_map/all_to_all | solution.py:391

commit v8 on v7

--- a/solution.py
+++ b/solution.py
@@ -85,7 +85,7 @@
     return widen(source, width), widen(update, width)
 
 
-def edge_kernel(e, m, ae, am, labels, perms, conds, to_ahead, to_behind, ae_last, ae_first, e_first, perm, cond, e_last, m_last, am_last, marks, sems):
+def edge_kernel(e, m, ae, am, labels, perms, conds, amplitude, to_ahead, to_behind, ae_last, ae_first, e_first, push, perm, cond, force, e_last, m_last, am_last, marks, sems):
     _, _, depth, rows, width = e.shape
     last = rows - 1
     planes = pl.ds(0, depth)
@@ -94,6 +94,7 @@
     moves = (
         (perms, perm),
         (conds, cond),
+        (amplitude, force),
         (ae.at[0, :, :, last], ae_last.at[:, planes]),
         (ae.at[0, pl.ds(1, 2), :, 0], ae_first.at[:, planes]),
         (labels.at[:, last], marks.at[0, planes]),
@@ -112,6 +113,8 @@
     for copy in copies:
         copy.wait()
     source, _ = gains(perm, cond, width)
+    for c in range(3):
+        push[c] = jnp.full(push.shape[1:], force[0, c], jnp.float32)
     last_gain, first_gain = (look_up(marks[i], source) for i in range(2))
     ex, ey, ez = (e_last[c] for c in range(3))
     sx, sy, sz = (last_gain * ae_last[c] for c in range(3))
@@ -154,13 +157,13 @@
     return blocks
 
 
-def correlation_kernel(ports, e, m, ae, cells, amplitude, packed, base, stage, sems):
+def drive_shares(ports, e, m, ae, cells, amplitude, drives):
     _, _, depth, rows, width = e.shape
     share = width // ports
-    groups = depth // PLANES
     tile = lax.axis_index("tile")
     plane_cells = lax.axis_size("tile") * rows * width
     target = cells[0] - tile * (rows * width)
+    push = [jnp.concatenate([amplitude[c, :1]] * (width // LANES), axis=1) for c in range(3)]
     position = row_iota((rows, width)) * width + lane_iota((rows, width))
 
     def at(ref, c, z):
@@ -168,40 +171,73 @@
 
     zero = jnp.zeros((rows, width), jnp.float32)
     fx_prev, fy_prev = zero, zero
-    sums_a, sums_b, copies = [], [], []
+    sums = []
     for z in range(depth):
         ex, ey, ez = (at(e, c, z) for c in range(3))
         fx = at(m, 0, z) - TIMESTEP * ((lane_next(ez) - ez) - (at(e, 1, z + 1) - ey))
         fy = at(m, 1, z) - TIMESTEP * ((at(e, 0, z + 1) - ex) - (row_next(ez, 0.0) - ez))
         fz = at(m, 2, z) - TIMESTEP * ((row_next(ey, 0.0) - ey) - (lane_next(ex) - ex))
         hit = position == target - z * plane_cells
-        drive_x = ((fz - lane_prev(fz)) - (fy - fy_prev)) - jnp.where(hit, amplitude[0, 0], 0.0)
-        drive_y = ((fx - fx_prev) - (fz - row_prev(fz, 0.0))) - jnp.where(hit, amplitude[0, 1], 0.0)
+        drive_x = ((fz - lane_prev(fz)) - (fy - fy_prev)) - jnp.where(hit, push[0], 0.0)
+        drive_y = ((fx - fx_prev) - (fz - row_prev(fz, 0.0))) - jnp.where(hit, push[1], 0.0)
         drive_z = ((fy - row_prev(fy, 0.0)) - (fx - lane_prev(fx))) - jnp.where(
-            hit, amplitude[0, 2], 0.0
+            hit, push[2], 0.0
         )
         ax, ay, az = (at(ae, c, z) for c in range(3))
-        sums_a.append(ax * ex + ay * ey + az * ez)
-        sums_b.append(ax * drive_x + ay * drive_y + az * drive_z)
+        sums.append(ax * drive_x + ay * drive_y + az * drive_z)
         fx_prev, fy_prev = fx, fy
         if z % PLANES == PLANES - 1:
-            group = z // PLANES
-            for f, sums in enumerate((sums_a, sums_b)):
-                slab = f * (depth // PLANES) + group
-                for port, block in enumerate(pack(sums, share, ports)):
-                    stage[port, slab] = block
-                    if f == 1:
-                        base[port, group : group + 1] = block[:1]
-                        base[port, groups + group : groups + group + 1] = block[rows - 1 :]
-                copies.append(pltpu.make_async_copy(stage.at[:, slab], packed.at[:, slab], sems.at[slab]))
-                copies[-1].start()
-            sums_a, sums_b = [], []
-    for copy in copies:
-        copy.wait()
-
-
-def rim_kernel(ports, behind, ahead, ae_last, ae_first, e_first, base, packed, patched, stage, sems):
-    del packed
+            for port, block in enumerate(pack(sums, share, ports)):
+                drives[port, z // PLANES] = block
+            sums = []
+
+
+def at_seam():
+    return lax.axis_index("tile") == lax.axis_size("tile") // 2
+
+
+def electric_shares(ports, e, ae, packed, stage, sems):
+    _, _, depth, _, width = e.shape
+    groups = depth // PLANES
+    copies = []
+    for group in range(groups):
+        planes = []
+        for z in range(group * PLANES, (group + 1) * PLANES):
+            ax, ay, az = (ae[0, c, z] for c in range(3))
+            planes.append(ax * e[0, 0, z] + ay * e[0, 1, z] + az * e[0, 2, z])
+        for port, block in enumerate(pack(planes, width // ports, ports)):
+            stage[port, group] = block
+        copies.append(pltpu.make_async_copy(stage.at[:, group], packed.at[:, group], sems.at[group]))
+        copies[-1].start()
+    return copies
+
+
+def early_kernel(ports, e, ae, edge, packed, edge_out, stage, sems):
+    del edge, edge_out
+
+    @pl.when(at_seam())
+    def _():
+        for copy in electric_shares(ports, e, ae, packed, stage, sems):
+            copy.wait()
+
+
+def late_kernel(ports, e, m, ae, cells, amplitude, packed_in, packed, drives, stage, sems):
+    del packed_in
+
+    @pl.when(jnp.logical_not(at_seam()))
+    def _():
+        copies = electric_shares(ports, e, ae, packed, stage, sems)
+        drive_shares(ports, e, m, ae, cells, amplitude, drives)
+        for copy in copies:
+            copy.wait()
+
+    @pl.when(at_seam())
+    def _():
+        drive_shares(ports, e, m, ae, cells, amplitude, drives)
+
+
+def rim_kernel(ports, behind, ahead, ae_last, ae_first, e_first, drives_in, packed, drives, patched, sem):
+    del drives_in, packed
     depth = behind.shape[0] // 4
     width = behind.shape[1]
     rows = patched.shape[2]
@@ -227,18 +263,12 @@
         for j in range(PLANES)
     ]
     for port, block in enumerate(pack(planes, share, ports)):
-        stage[port] = base[port, : 2 * groups] + block
-    copies = [
-        pltpu.make_async_copy(
-            stage.at[:, side * groups + g], patched.at[:, groups + g, side * (rows - 1)], sems.at[side * groups + g]
-        )
-        for side in range(2)
-        for g in range(groups)
-    ]
-    for copy in copies:
-        copy.start()
-    for copy in copies:
-        copy.wait()
+        for g in range(groups):
+            drives[port, g, :1] = drives[port, g, :1] + block[g : g + 1]
+            drives[port, g, rows - 1 :] = drives[port, g, rows - 1 :] + block[groups + g : groups + g + 1]
+    copy = pltpu.make_async_copy(drives, patched.at[:, pl.ds(groups, groups)], sem.at[0])
+    copy.start()
+    copy.wait()
 
 
 def share_factors(ports, labels, perm, cond, factors):
@@ -351,42 +381,55 @@
         return jax.ShapeDtypeStruct(shape, jnp.float32)
 
     edge = array(4 * depth, width)
-    to_ahead, to_behind, *kept = call(
+    to_ahead, to_behind, *kept, push = call(
         edge_kernel,
-        (electric, magnetic, adjoint_electric, adjoint_magnetic, region_labels, permittivity_table, conductivity_table),
-        (HBM,) * 7,
-        (edge, edge) + tuple(array(count, EDGE, width) for count in (3, 2, 2)),
-        (VMEM,) * 5,
+        (electric, magnetic, adjoint_electric, adjoint_magnetic, region_labels, permittivity_table, conductivity_table, port_amplitude),
+        (HBM,) * 8,
+        (edge, edge) + tuple(array(count, EDGE, width) for count in (3, 2, 2)) + (array(3, EDGE, LANES),),
+        (VMEM,) * 6,
         10 * cells,
         cells * 4 * 14,
-        [SMEM(permittivity_table.shape, jnp.float32)] * 2 + [
+        [SMEM(permittivity_table.shape, jnp.float32)] * 2 + [SMEM(port_amplitude.shape, jnp.float32)] + [
             VMEM((count, EDGE, width), jnp.float32) for count in (3, 2, 2)
-        ] + [VMEM((2, EDGE, width), jnp.int32), pltpu.SemaphoreType.DMA((10,))],
+        ] + [VMEM((2, EDGE, width), jnp.int32), pltpu.SemaphoreType.DMA((11,))],
     )
     behind = from_behind(to_ahead, "tile", 1)
+    shares = array(ports, 2 * depth // PLANES, rows, LANES)
+    half = array(ports, depth // PLANES, rows, LANES)
+    stage = [VMEM(half.shape, jnp.float32), pltpu.SemaphoreType.DMA((half.shape[1],))]
+    packed, to_behind = call(
+        functools.partial(early_kernel, ports),
+        (electric, adjoint_electric, to_behind),
+        (VMEM,) * 3,
+        (shares, edge),
+        (HBM, VMEM),
+        cells,
+        cells,
+        stage,
+        {2: 1},
+    )
     ahead = from_behind(to_behind, "tile", -1)
-    shares = array(ports, 2 * depth // PLANES, rows, LANES)
-    sems = pltpu.SemaphoreType.DMA((shares.shape[1],))
-    packed, base = call(
-        functools.partial(correlation_kernel, ports),
-        (electric, magnetic, adjoint_electric, port_cells, port_amplitude),
-        (VMEM,) * 3 + (SMEM,) * 2,
-        (shares, array(ports, EDGE, LANES)),
+    packed, drives = call(
+        functools.partial(late_kernel, ports),
+        (electric, magnetic, adjoint_electric, port_cells, push, packed),
+        (VMEM,) * 3 + (SMEM, VMEM, HBM),
+        (shares, half),
         (HBM, VMEM),
         60 * cells,
         cells * 4 * 11,
-        [VMEM(shares.shape, jnp.float32), sems],
-    )
-    (packed,) = call(
+        stage,
+        {5: 0},
+    )
+    _, packed = call(
         functools.partial(rim_kernel, ports),
-        (behind, ahead, *kept, base, packed),
+        (behind, ahead, *kept, drives, packed),
         (VMEM,) * 6 + (HBM,),
-        (shares,),
-        (HBM,),
+        (half, shares),
+        (VMEM, HBM),
         2 * cells,
         cells,
-        [VMEM((ports, 2 * depth // PLANES, LANES), jnp.float32), sems],
-        {6: 0},
+        [pltpu.SemaphoreType.DMA((1,))],
+        {5: 0, 6: 1},
     )
     gathered = lax.all_to_all(packed, "port", 0, 0, tiled=True)
     new_electric, new_magnetic, factors = call(

time: 38.7 us -> 37.8 us (0.977)
  starting transfers between devices: 21.5 us -> 20.3 us
  waiting for transfers between devices: 7.86 us -> 8.34 us
    ppermute x2, starting transfers between devices: 13.7 us -> 12.8 us  [from_behind(): lax.ppermute(value, axis, [(source, source + steps) for source in range(f...]
    ppermute x2, waiting for transfers between devices: 0.01 us -> 0.5 us  [from_behind(): lax.ppermute(value, axis, [(source, source + steps) for source in range(f...]
    pallas_call x5 -> x6, Pallas kernels: 7.63 us -> 7.38 us  [call(): pl.pallas_call(kernel, out_shape=tuple((space(out.shape, out.dtype) if sp...]
  transfers between devices with their start and end apart: 3 -> 3, of which waited for: 1 -> 2; matrix products, arithmetic and copies ran while one was open for 0% -> 0% of each run, Pallas kernels for 12% -> 12%
where the time goes in v8:
time: 37.8 us; the launch traced here: 37.5 us
  starting transfers between devices  20.3 us (54%)
  waiting for transfers between devices  8.34 us (22%)
  Pallas kernels  7.38 us (20%)
  between operations  1.44 us (4%)
    ppermute x2, starting transfers between devices, from_behind(): lax.ppermute(value, axis, [(source, source + steps) for source in range(f...  12.8 us
    all_to_all x1, waiting for transfers between devices, on_device(): gathered = lax.all_to_all(packed, 'port', 0, 0, tiled=True)  7.85 us
    all_to_all x1, starting transfers between devices, on_device(): gathered = lax.all_to_all(packed, 'port', 0, 0, tiled=True)  7.5 us
    pallas_call x6, Pallas kernels, call(): pl.pallas_call(kernel, out_shape=tuple((space(out.shape, out.dtype) if sp...  7.38 us
  transfers between devices with their start and end apart: 3, of which 2 were waited for; matrix products, arithmetic and copies ran while one was open for 0% of the time, Pallas kernels for 12%

profile of v8, /device:TPU:48, one launch (start us, length us, event | category | flops | bytes accessed | tf_op | source)
XLA Modules:
  0.0 37.5 jit_solution(15991792281523048367)
XLA Ops:
  0.6 0.0 copy-start
  0.6 0.0 copy-start.1
  0.7 1.2 %shard_map.120 = (f32[24,640]{1,0:T(8,128)S(1)}, f32[24,640]{1,0:T(8,128)S(1)}, f32[3,8,640]{2,1,0:T(8,128)S(1)}, f32[2,8,640]{2,1,0:T(8,128)S(1)}, f32[2,8,640]{2,1,0:T(8,128)S(1)}, /*index=5*/f32[3,8,128]{2,1,0:T(8,128)S(1)}) custom-call(f32[1,3,6,16,640]{4,3,2,1,0:T(8,128)} %e.5, f32[1,3,6,16,640]{4,3,2,1,0:T(8,128)} %m.3, f32[1,3,6,16,640]{4,3,2,1,0:T(8,128)} %ae.7, ...), custom_call_target="tpu_custom_call" | custom-call | flops 614400 | bytes 3440640 | tf_op jit(solution)/shard_map/pallas_call | solution.py:352
  1.9 1.9 %collective-permute-start = (f32[24,640]{1,0:T(8,128)S(1)}, f32[24,640]{1,0:T(8,128)S(1)}, u32[]{:S(2)}, u32[]{:S(2)}) collective-permute-start(f32[24,640]{1,0:T(8,128)S(1)} %get-tuple-element.20), channel_id=1, source_target_pairs={{0,1},{1,2},{2,3},{3,4},{4,5},{5,6},{6,7},{7,8},{8,9},{9,10},{10,1... | collective-permute-start | bytes 184328 | tf_op jit(solution)/shard_map/ppermute | solution.py:25
  3.8 0.0 copy-done
  3.8 0.0 copy-done.1
  3.8 0.0 copy-start.2
  3.8 1.0 %shard_map.121 = (f32[16,4,16,128]{3,2,1,0:T(8,128)}, f32[24,640]{1,0:T(8,128)S(1)}) custom-call(f32[1,3,6,16,640]{4,3,2,1,0:T(8,128)S(1)} %copy-done.1, f32[1,3,6,16,640]{4,3,2,1,0:T(8,128)S(1)} %copy-done, f32[24,640]{1,0:T(8,128)S(1)} %get-tuple-element.21.edge), custom_call_target="tpu_custom_call", output_to_operand_aliasing={{1}: (2, {})} | custom-call | flops 61440 | bytes 61440 | tf_op jit(solution)/shard_map/pallas_call | solution.py:352
  4.8 10.9 %collective-permute-start.1 = (f32[24,640]{1,0:T(8,128)S(1)}, f32[24,640]{1,0:T(8,128)S(1)}, u32[]{:S(2)}, u32[]{:S(2)}) collective-permute-start(f32[24,640]{1,0:T(8,128)S(1)} %get-tuple-element.22), channel_id=1, source_target_pairs={{1,0},{2,1},{3,2},{4,3},{5,4},{6,5},{7,6},{8,7},{9,8},{10,9},{11,1... | collective-permute-start | bytes 184328 | tf_op jit(solution)/shard_map/ppermute | solution.py:25
  16.4 0.0 copy-done.2
  16.4 1.0 %shard_map.123 = (f32[16,4,16,128]{3,2,1,0:T(8,128)}, f32[16,2,16,128]{3,2,1,0:T(8,128)S(1)}) custom-call(f32[1,3,6,16,640]{4,3,2,1,0:T(8,128)S(1)} %copy-done.1, f32[1,3,6,16,640]{4,3,2,1,0:T(8,128)S(1)} %copy-done.2, f32[1,3,6,16,640]{4,3,2,1,0:T(8,128)S(1)} %copy-done, s32[1]{0:T(128)S(6)} %copy.21.cells, ...), custom_call_target="tpu_custom_call", output_to_operand_aliasing={{0}: (5, {})} | custom-call | flops 3686400 | bytes 2703360 | tf_op jit(solution)/shard_map/pallas_call | solution.py:352
  17.4 0.0 collective-permute-done.behind
  17.4 0.5 %collective-permute-done.1.ahead = f32[24,640]{1,0:T(8,128)S(1)} collective-permute-done((f32[24,640]{1,0:T(8,128)S(1)}, f32[24,640]{1,0:T(8,128)S(1)}, u32[]{:S(2)}, u32[]{:S(2)}) %collective-permute-start.1) | collective-permute-done | bytes 61472 | tf_op jit(solution)/shard_map/ppermute | solution.py:25
  17.9 0.9 %shard_map.124 = (f32[16,2,16,128]{3,2,1,0:T(8,128)S(1)}, f32[16,4,16,128]{3,2,1,0:T(8,128)}) custom-call(f32[24,640]{1,0:T(8,128)S(1)} %collective-permute-done.behind, f32[24,640]{1,0:T(8,128)S(1)} %collective-permute-done.1.ahead, f32[3,8,640]{2,1,0:T(8,128)S(1)} %get-tuple-element.25.ae_last, ...), custom_call_target="tpu_custom_call", output_to_operand_aliasing={{0}: (5, {}), {1}: (6, {})} | custom-call | flops 122880 | bytes 61440 | tf_op jit(solution)/shard_map/pallas_call | solution.py:352
  18.9 0.0 copy-start.3
  18.9 0.0 copy-start.4
  18.9 0.0 copy-start.5
  18.9 0.0 copy-start.6
  18.9 7.5 %all-to-all-start = ((f32[16,4,16,128]{3,2,1,0:T(8,128)}), f32[16,4,16,128]{3,2,1,0:T(8,128)S(1)}, u32[]{:S(2)}, u32[]{:S(2)}) async-start(f32[16,4,16,128]{3,2,1,0:T(8,128)} %get-tuple-element.32), calls=%async_computation | async-start | bytes 1048576 | tf_op jit(solution)/shard_map/all_to_all | solution.py:434
  26.4 0.0 copy-done.3
  26.4 0.0 copy-done.4
  26.4 0.0 copy-done.5
  26.4 0.0 copy-done.6
  26.4 2.5 %shard_map.122 = (f32[1,3,6,16,640]{4,3,2,1,0:T(8,128)}, f32[1,3,6,16,640]{4,3,2,1,0:T(8,128)}, f32[3,2,16,128]{3,2,1,0:T(8,128)S(1)}) custom-call(f32[1,3,6,16,640]{4,3,2,1,0:T(8,128)S(1)} %copy-done, f32[1,3,6,16,640]{4,3,2,1,0:T(8,128)S(1)} %copy-done.3, s32[6,16,640]{2,1,0:T(8,128)S(1)} %copy-done.4, f32[24,640]{1,0:T(8,128)S(1)} %collective-permute-done.behind, ...), custom_call_target="tpu_custom_call" | custom-call | flops 4915200 | bytes 3194880 | tf_op jit(solution)/shard_map/pallas_call | solution.py:352
  28.9 7.8 %all-to-all-done.gathered = f32[16,4,16,128]{3,2,1,0:T(8,128)S(1)} async-done(((f32[16,4,16,128]{3,2,1,0:T(8,128)}), f32[16,4,16,128]{3,2,1,0:T(8,128)S(1)}, u32[]{:S(2)}, u32[]{:S(2)}) %all-to-all-start) | async-done | bytes 524320 | tf_op jit(solution)/shard_map/all_to_all | solution.py:434
  36.8 0.7 %shard_map.125 = (f32[6,16,40]{2,1,0:T(8,128)}, f32[6,16,40]{2,1,0:T(8,128)}) custom-call(f32[16,4,16,128]{3,2,1,0:T(8,128)S(1)} %all-to-all-done.gathered, f32[3,2,16,128]{3,2,1,0:T(8,128)S(1)} %get-tuple-element.33.factors), custom_call_target="tpu_custom_call" | custom-call | flops 245760 | bytes 737280 | tf_op jit(solution)/shard_map/pallas_call | solution.py:352
Async XLA Ops:
  0.6 3.2 %copy-start = (f32[1,3,6,16,640]{4,3,2,1,0:T(8,128)S(1)}, f32[1,3,6,16,640]{4,3,2,1,0:T(8,128)}, u32[]{:S(2)}) copy-start(f32[1,3,6,16,640]{4,3,2,1,0:T(8,128)} %ae.7) | copy-start | bytes 2211844
  0.6 3.2 %copy-start.1 = (f32[1,3,6,16,640]{4,3,2,1,0:T(8,128)S(1)}, f32[1,3,6,16,640]{4,3,2,1,0:T(8,128)}, u32[]{:S(2)}) copy-start(f32[1,3,6,16,640]{4,3,2,1,0:T(8,128)} %e.5) | copy-start | bytes 2211844
  1.9 15.6 %collective-permute-start = (f32[24,640]{1,0:T(8,128)S(1)}, f32[24,640]{1,0:T(8,128)S(1)}, u32[]{:S(2)}, u32[]{:S(2)}) collective-permute-start(f32[24,640]{1,0:T(8,128)S(1)} %get-tuple-element.20), channel_id=1, source_target_pairs={{0,1},{1,2},{2,3},{3,4},{4,5},{5,6},{6,7},{7,8},{8,9},{9,10},{10,1... | collective-permute-start | bytes 184328 | tf_op jit(solution)/shard_map/ppermute | solution.py:25
  3.8 12.6 %copy-start.2 = (f32[1,3,6,16,640]{4,3,2,1,0:T(8,128)S(1)}, f32[1,3,6,16,640]{4,3,2,1,0:T(8,128)}, u32[]{:S(2)}) copy-start(f32[1,3,6,16,640]{4,3,2,1,0:T(8,128)} %m.3) | copy-start | bytes 2211844
  4.8 13.1 %collective-permute-start.1 = (f32[24,640]{1,0:T(8,128)S(1)}, f32[24,640]{1,0:T(8,128)S(1)}, u32[]{:S(2)}, u32[]{:S(2)}) collective-permute-start(f32[24,640]{1,0:T(8,128)S(1)} %get-tuple-element.22), channel_id=1, source_target_pairs={{1,0},{2,1},{3,2},{4,3},{5,4},{6,5},{7,6},{8,7},{9,8},{10,9},{11,1... | collective-permute-start | bytes 184328 | tf_op jit(solution)/shard_map/ppermute | solution.py:25
  18.9 7.5 %copy-start.3 = (f32[1,3,6,16,640]{4,3,2,1,0:T(8,128)S(1)}, f32[1,3,6,16,640]{4,3,2,1,0:T(8,128)}, u32[]{:S(2)}) copy-start(f32[1,3,6,16,640]{4,3,2,1,0:T(8,128)} %am.3) | copy-start | bytes 2211844
  18.9 7.5 %copy-start.4 = (s32[6,16,640]{2,1,0:T(8,128)S(1)}, s32[6,16,640]{2,1,0:T(8,128)}, u32[]{:S(2)}) copy-start(s32[6,16,640]{2,1,0:T(8,128)} %labels.3) | copy-start | bytes 737284
  18.9 7.5 %copy-start.5 = (f32[8]{0:T(128)S(1)}, f32[8]{0:T(128)}, u32[]{:S(2)}) copy-start(f32[8]{0:T(128)} %perm.1) | copy-start | bytes 100
  18.9 7.5 %copy-start.6 = (f32[8]{0:T(128)S(1)}, f32[8]{0:T(128)}, u32[]{:S(2)}) copy-start(f32[8]{0:T(128)} %cond.1) | copy-start | bytes 100
  18.9 17.9 %all-to-all-start = ((f32[16,4,16,128]{3,2,1,0:T(8,128)}), f32[16,4,16,128]{3,2,1,0:T(8,128)S(1)}, u32[]{:S(2)}, u32[]{:S(2)}) async-start(f32[16,4,16,128]{3,2,1,0:T(8,128)} %get-tuple-element.32), calls=%async_computation | async-start | bytes 1048576 | tf_op jit(solution)/shard_map/all_to_all | solution.py:434

commit v9 on v8

--- a/solution.py
+++ b/solution.py
@@ -213,7 +213,7 @@
 
 
 def early_kernel(ports, e, ae, edge, packed, edge_out, stage, sems):
-    del edge, edge_out
+    edge_out[...] = edge[...]
 
     @pl.when(at_seam())
     def _():
@@ -236,8 +236,8 @@
         drive_shares(ports, e, m, ae, cells, amplitude, drives)
 
 
-def rim_kernel(ports, behind, ahead, ae_last, ae_first, e_first, drives_in, packed, drives, patched, sem):
-    del drives_in, packed
+def rim_kernel(ports, behind, ahead, ae_last, ae_first, e_first, drives, packed, patched, stage, sems):
+    del packed
     depth = behind.shape[0] // 4
     width = behind.shape[1]
     rows = patched.shape[2]
@@ -262,13 +262,18 @@
         )
         for j in range(PLANES)
     ]
-    for port, block in enumerate(pack(planes, share, ports)):
-        for g in range(groups):
-            drives[port, g, :1] = drives[port, g, :1] + block[g : g + 1]
-            drives[port, g, rows - 1 :] = drives[port, g, rows - 1 :] + block[groups + g : groups + g + 1]
-    copy = pltpu.make_async_copy(drives, patched.at[:, pl.ds(groups, groups)], sem.at[0])
-    copy.start()
-    copy.wait()
+    blocks = pack(planes, share, ports)
+    row = row_iota((rows, LANES))
+    copies = []
+    for g in range(groups):
+        for port, block in enumerate(blocks):
+            edges = jnp.where(row == 0, block[g : g + 1], block[groups + g : groups + g + 1])
+            inner = jnp.logical_and(row > 0, row < rows - 1)
+            stage[port, g] = drives[port, g] + jnp.where(inner, 0.0, edges)
+        copies.append(pltpu.make_async_copy(stage.at[:, g], patched.at[:, groups + g], sems.at[g]))
+        copies[-1].start()
+    for copy in copies:
+        copy.wait()
 
 
 def share_factors(ports, labels, perm, cond, factors):
@@ -406,7 +411,6 @@
         cells,
         cells,
         stage,
-        {2: 1},
     )
     ahead = from_behind(to_behind, "tile", -1)
     packed, drives = call(
@@ -420,16 +424,16 @@
         stage,
         {5: 0},
     )
-    _, packed = call(
+    (packed,) = call(
         functools.partial(rim_kernel, ports),
         (behind, ahead, *kept, drives, packed),
         (VMEM,) * 6 + (HBM,),
-        (half, shares),
-        (VMEM, HBM),
+        (shares,),
+        (HBM,),
         2 * cells,
         cells,
-        [pltpu.SemaphoreType.DMA((1,))],
-        {5: 0, 6: 1},
+        stage,
+        {6: 0},
     )
     gathered = lax.all_to_all(packed, "port", 0, 0, tiled=True)
     new_electric, new_magnetic, factors = call(

time: 37.8 us -> 37.8 us (level)
  no operation moved by 1% of the time
where the time goes in v9:
time: 37.8 us; the launch traced here: 37.5 us
  starting transfers between devices  20.3 us (54%)
  waiting for transfers between devices  8.35 us (22%)
  Pallas kernels  7.4 us (20%)
  between operations  1.44 us (4%)
    ppermute x2, starting transfers between devices, from_behind(): lax.ppermute(value, axis, [(source, source + steps) for source in range(f...  12.8 us
    all_to_all x1, waiting for transfers between devices, on_device(): gathered = lax.all_to_all(packed, 'port', 0, 0, tiled=True)  7.85 us
    all_to_all x1, starting transfers between devices, on_device(): gathered = lax.all_to_all(packed, 'port', 0, 0, tiled=True)  7.5 us
    pallas_call x6, Pallas kernels, call(): pl.pallas_call(kernel, out_shape=tuple((space(out.shape, out.dtype) if sp...  7.4 us
  transfers between devices with their start and end apart: 3, of which 2 were waited for; matrix products, arithmetic and copies ran while one was open for 0% of the time, Pallas kernels for 12%

profile of v9, /device:TPU:48, one launch (start us, length us, event | category | flops | bytes accessed | tf_op | source)
XLA Modules:
  0.0 37.5 jit_solution(16750985445961405381)
XLA Ops:
  0.6 0.0 copy-start
  0.6 0.0 copy-start.1
  0.7 1.2 %shard_map.120 = (f32[24,640]{1,0:T(8,128)S(1)}, f32[24,640]{1,0:T(8,128)S(1)}, f32[3,8,640]{2,1,0:T(8,128)S(1)}, f32[2,8,640]{2,1,0:T(8,128)S(1)}, f32[2,8,640]{2,1,0:T(8,128)S(1)}, /*index=5*/f32[3,8,128]{2,1,0:T(8,128)S(1)}) custom-call(f32[1,3,6,16,640]{4,3,2,1,0:T(8,128)} %e.5, f32[1,3,6,16,640]{4,3,2,1,0:T(8,128)} %m.3, f32[1,3,6,16,640]{4,3,2,1,0:T(8,128)} %ae.7, ...), custom_call_target="tpu_custom_call" | custom-call | flops 614400 | bytes 3440640 | tf_op jit(solution)/shard_map/pallas_call | solution.py:357
  1.9 1.9 %collective-permute-start = (f32[24,640]{1,0:T(8,128)S(1)}, f32[24,640]{1,0:T(8,128)S(1)}, u32[]{:S(2)}, u32[]{:S(2)}) collective-permute-start(f32[24,640]{1,0:T(8,128)S(1)} %get-tuple-element.19), channel_id=1, source_target_pairs={{0,1},{1,2},{2,3},{3,4},{4,5},{5,6},{6,7},{7,8},{8,9},{9,10},{10,1... | collective-permute-start | bytes 184328 | tf_op jit(solution)/shard_map/ppermute | solution.py:25
  3.8 0.0 copy-done
  3.8 0.0 copy-done.1
  3.8 0.0 copy-start.2
  3.8 1.0 %shard_map.121 = (f32[16,4,16,128]{3,2,1,0:T(8,128)}, f32[24,640]{1,0:T(8,128)S(1)}) custom-call(f32[1,3,6,16,640]{4,3,2,1,0:T(8,128)S(1)} %copy-done.1, f32[1,3,6,16,640]{4,3,2,1,0:T(8,128)S(1)} %copy-done, f32[24,640]{1,0:T(8,128)S(1)} %get-tuple-element.20.edge), custom_call_target="tpu_custom_call" | custom-call | flops 61440 | bytes 61440 | tf_op jit(solution)/shard_map/pallas_call | solution.py:357
  4.8 10.9 %collective-permute-start.1 = (f32[24,640]{1,0:T(8,128)S(1)}, f32[24,640]{1,0:T(8,128)S(1)}, u32[]{:S(2)}, u32[]{:S(2)}) collective-permute-start(f32[24,640]{1,0:T(8,128)S(1)} %get-tuple-element.21), channel_id=1, source_target_pairs={{1,0},{2,1},{3,2},{4,3},{5,4},{6,5},{7,6},{8,7},{9,8},{10,9},{11,1... | collective-permute-start | bytes 184328 | tf_op jit(solution)/shard_map/ppermute | solution.py:25
  16.4 0.0 copy-done.2
  16.4 1.0 %shard_map.123 = (f32[16,4,16,128]{3,2,1,0:T(8,128)}, f32[16,2,16,128]{3,2,1,0:T(8,128)S(1)}) custom-call(f32[1,3,6,16,640]{4,3,2,1,0:T(8,128)S(1)} %copy-done.1, f32[1,3,6,16,640]{4,3,2,1,0:T(8,128)S(1)} %copy-done.2, f32[1,3,6,16,640]{4,3,2,1,0:T(8,128)S(1)} %copy-done, s32[1]{0:T(128)S(6)} %copy.17.cells, ...), custom_call_target="tpu_custom_call", output_to_operand_aliasing={{0}: (5, {})} | custom-call | flops 3686400 | bytes 2703360 | tf_op jit(solution)/shard_map/pallas_call | solution.py:357
  17.4 0.0 collective-permute-done.behind
  17.4 0.5 %collective-permute-done.1.ahead = f32[24,640]{1,0:T(8,128)S(1)} collective-permute-done((f32[24,640]{1,0:T(8,128)S(1)}, f32[24,640]{1,0:T(8,128)S(1)}, u32[]{:S(2)}, u32[]{:S(2)}) %collective-permute-start.1) | collective-permute-done | bytes 61472 | tf_op jit(solution)/shard_map/ppermute | solution.py:25
  17.9 0.9 %shard_map.124 = f32[16,4,16,128]{3,2,1,0:T(8,128)} custom-call(f32[24,640]{1,0:T(8,128)S(1)} %collective-permute-done.behind, f32[24,640]{1,0:T(8,128)S(1)} %collective-permute-done.1.ahead, f32[3,8,640]{2,1,0:T(8,128)S(1)} %get-tuple-element.24.ae_last, f32[2,8,640]{2,1,0:T(8,128)S(1)} %get-tuple-element.25.ae_first, ...), custom_call_target="tpu_custom_call", output_to_operand_aliasing={{}: (6, {})} | custom-call | flops 122880 | bytes 61440 | tf_op jit(solution)/shard_map/pallas_call | solution.py:357
  18.9 0.0 copy-start.3
  18.9 0.0 copy-start.4
  18.9 0.0 copy-start.5
  18.9 0.0 copy-start.6
  18.9 7.5 %all-to-all-start = ((f32[16,4,16,128]{3,2,1,0:T(8,128)}), f32[16,4,16,128]{3,2,1,0:T(8,128)S(1)}, u32[]{:S(2)}, u32[]{:S(2)}) async-start(f32[16,4,16,128]{3,2,1,0:T(8,128)} %shard_map.124), calls=%async_computation | async-start | bytes 1048576 | tf_op jit(solution)/shard_map/all_to_all | solution.py:438
  26.4 0.0 copy-done.3
  26.4 0.0 copy-done.4
  26.4 0.0 copy-done.5
  26.5 0.0 copy-done.6
  26.5 2.5 %shard_map.122 = (f32[1,3,6,16,640]{4,3,2,1,0:T(8,128)}, f32[1,3,6,16,640]{4,3,2,1,0:T(8,128)}, f32[3,2,16,128]{3,2,1,0:T(8,128)S(1)}) custom-call(f32[1,3,6,16,640]{4,3,2,1,0:T(8,128)S(1)} %copy-done, f32[1,3,6,16,640]{4,3,2,1,0:T(8,128)S(1)} %copy-done.3, s32[6,16,640]{2,1,0:T(8,128)S(1)} %copy-done.4, f32[24,640]{1,0:T(8,128)S(1)} %collective-permute-done.behind, ...), custom_call_target="tpu_custom_call" | custom-call | flops 4915200 | bytes 3194880 | tf_op jit(solution)/shard_map/pallas_call | solution.py:357
  28.9 7.9 %all-to-all-done.gathered = f32[16,4,16,128]{3,2,1,0:T(8,128)S(1)} async-done(((f32[16,4,16,128]{3,2,1,0:T(8,128)}), f32[16,4,16,128]{3,2,1,0:T(8,128)S(1)}, u32[]{:S(2)}, u32[]{:S(2)}) %all-to-all-start) | async-done | bytes 524320 | tf_op jit(solution)/shard_map/all_to_all | solution.py:438
  36.8 0.7 %shard_map.125 = (f32[6,16,40]{2,1,0:T(8,128)}, f32[6,16,40]{2,1,0:T(8,128)}) custom-call(f32[16,4,16,128]{3,2,1,0:T(8,128)S(1)} %all-to-all-done.gathered, f32[3,2,16,128]{3,2,1,0:T(8,128)S(1)} %get-tuple-element.31.factors), custom_call_target="tpu_custom_call" | custom-call | flops 245760 | bytes 737280 | tf_op jit(solution)/shard_map/pallas_call | solution.py:357
Async XLA Ops:
  0.6 3.2 %copy-start = (f32[1,3,6,16,640]{4,3,2,1,0:T(8,128)S(1)}, f32[1,3,6,16,640]{4,3,2,1,0:T(8,128)}, u32[]{:S(2)}) copy-start(f32[1,3,6,16,640]{4,3,2,1,0:T(8,128)} %ae.7) | copy-start | bytes 2211844
  0.6 3.2 %copy-start.1 = (f32[1,3,6,16,640]{4,3,2,1,0:T(8,128)S(1)}, f32[1,3,6,16,640]{4,3,2,1,0:T(8,128)}, u32[]{:S(2)}) copy-start(f32[1,3,6,16,640]{4,3,2,1,0:T(8,128)} %e.5) | copy-start | bytes 2211844
  1.9 15.6 %collective-permute-start = (f32[24,640]{1,0:T(8,128)S(1)}, f32[24,640]{1,0:T(8,128)S(1)}, u32[]{:S(2)}, u32[]{:S(2)}) collective-permute-start(f32[24,640]{1,0:T(8,128)S(1)} %get-tuple-element.19), channel_id=1, source_target_pairs={{0,1},{1,2},{2,3},{3,4},{4,5},{5,6},{6,7},{7,8},{8,9},{9,10},{10,1... | collective-permute-start | bytes 184328 | tf_op jit(solution)/shard_map/ppermute | solution.py:25
  3.8 12.6 %copy-start.2 = (f32[1,3,6,16,640]{4,3,2,1,0:T(8,128)S(1)}, f32[1,3,6,16,640]{4,3,2,1,0:T(8,128)}, u32[]{:S(2)}) copy-start(f32[1,3,6,16,640]{4,3,2,1,0:T(8,128)} %m.3) | copy-start | bytes 2211844
  4.8 13.1 %collective-permute-start.1 = (f32[24,640]{1,0:T(8,128)S(1)}, f32[24,640]{1,0:T(8,128)S(1)}, u32[]{:S(2)}, u32[]{:S(2)}) collective-permute-start(f32[24,640]{1,0:T(8,128)S(1)} %get-tuple-element.21), channel_id=1, source_target_pairs={{1,0},{2,1},{3,2},{4,3},{5,4},{6,5},{7,6},{8,7},{9,8},{10,9},{11,1... | collective-permute-start | bytes 184328 | tf_op jit(solution)/shard_map/ppermute | solution.py:25
  18.9 7.5 %copy-start.3 = (f32[1,3,6,16,640]{4,3,2,1,0:T(8,128)S(1)}, f32[1,3,6,16,640]{4,3,2,1,0:T(8,128)}, u32[]{:S(2)}) copy-start(f32[1,3,6,16,640]{4,3,2,1,0:T(8,128)} %am.3) | copy-start | bytes 2211844
  18.9 7.5 %copy-start.4 = (s32[6,16,640]{2,1,0:T(8,128)S(1)}, s32[6,16,640]{2,1,0:T(8,128)}, u32[]{:S(2)}) copy-start(s32[6,16,640]{2,1,0:T(8,128)} %labels.3) | copy-start | bytes 737284
  18.9 7.5 %copy-start.5 = (f32[8]{0:T(128)S(1)}, f32[8]{0:T(128)}, u32[]{:S(2)}) copy-start(f32[8]{0:T(128)} %perm.1) | copy-start | bytes 100
  18.9 7.5 %copy-start.6 = (f32[8]{0:T(128)S(1)}, f32[8]{0:T(128)}, u32[]{:S(2)}) copy-start(f32[8]{0:T(128)} %cond.1) | copy-start | bytes 100
  18.9 17.9 %all-to-all-start = ((f32[16,4,16,128]{3,2,1,0:T(8,128)}), f32[16,4,16,128]{3,2,1,0:T(8,128)S(1)}, u32[]{:S(2)}, u32[]{:S(2)}) async-start(f32[16,4,16,128]{3,2,1,0:T(8,128)} %shard_map.124), calls=%async_computation | async-start | bytes 1048576 | tf_op jit(solution)/shard_map/all_to_all | solution.py:438

commit v10 on v9

--- a/solution.py
+++ b/solution.py
@@ -89,41 +89,51 @@
     _, _, depth, rows, width = e.shape
     last = rows - 1
     planes = pl.ds(0, depth)
-    for ref in (ae_last, ae_first, e_first, e_last, m_last, am_last):
-        ref[:, depth:, :] = jnp.zeros((ref.shape[0], EDGE - depth, width), jnp.float32)
     moves = (
         (perms, perm),
         (conds, cond),
-        (amplitude, force),
-        (ae.at[0, :, :, last], ae_last.at[:, planes]),
-        (ae.at[0, pl.ds(1, 2), :, 0], ae_first.at[:, planes]),
         (labels.at[:, last], marks.at[0, planes]),
         (labels.at[:, 0], marks.at[1, planes]),
         (e.at[0, :, :, last], e_last.at[:, planes]),
+        (m.at[0, pl.ds(1, 2), :, last], m_last.at[:, planes]),
+        (ae.at[0, :, :, last], ae_last.at[:, planes]),
+        (am.at[0, pl.ds(1, 2), :, last], am_last.at[:, planes]),
+        (ae.at[0, pl.ds(1, 2), :, 0], ae_first.at[:, planes]),
         (e.at[0, pl.ds(1, 2), :, 0], e_first.at[:, planes]),
-        (m.at[0, pl.ds(1, 2), :, last], m_last.at[:, planes]),
-        (am.at[0, pl.ds(1, 2), :, last], am_last.at[:, planes]),
+        (amplitude, force),
     )
     copies = [pltpu.make_async_copy(src, dst, sems.at[i]) for i, (src, dst) in enumerate(moves)]
     for copy in copies:
         copy.start()
+    for ref in (e_last, ae_last):
+        ref[0, depth:, :] = jnp.zeros((EDGE - depth, width), jnp.float32)
+
+    def wait(first, count):
+        for copy in copies[first : first + count]:
+            copy.wait()
+
     def plane_next(value):
         return pltpu.roll(value, EDGE - 1, 0)
 
-    for copy in copies:
-        copy.wait()
+    wait(0, 2)
     source, _ = gains(perm, cond, width)
+    wait(2, 2)
+    last_gain, first_gain = (look_up(marks[i], source) for i in range(2))
+    wait(4, 2)
+    ex, ey, ez = (e_last[c] for c in range(3))
+    up = [
+        m_last[0] - TIMESTEP * ((plane_next(ex) - ex) + ez),
+        m_last[1] + TIMESTEP * (ey + (lane_next(ex) - ex)),
+    ]
+    wait(6, 2)
+    sx, sy, sz = (last_gain * ae_last[c] for c in range(3))
+    up += [
+        am_last[0] + ((plane_next(sx) - sx) + sz),
+        am_last[1] - (sy + (lane_next(sx) - sx)),
+    ]
+    wait(8, 3)
     for c in range(3):
         push[c] = jnp.full(push.shape[1:], force[0, c], jnp.float32)
-    last_gain, first_gain = (look_up(marks[i], source) for i in range(2))
-    ex, ey, ez = (e_last[c] for c in range(3))
-    sx, sy, sz = (last_gain * ae_last[c] for c in range(3))
-    up = (
-        m_last[0] - TIMESTEP * ((plane_next(ex) - ex) + ez),
-        m_last[1] + TIMESTEP * (ey + (lane_next(ex) - ex)),
-        am_last[0] + ((plane_next(sx) - sx) + sz),
-        am_last[1] - (sy + (lane_next(sx) - sx)),
-    )
     down = (e_first[0], e_first[1], first_gain * ae_first[0], first_gain * ae_first[1])
     for i, (above, below) in enumerate(zip(up, down, strict=True)):
         at = i * depth
@@ -157,15 +167,9 @@
     return blocks
 
 
-def drive_shares(ports, e, m, ae, cells, amplitude, drives):
+def drive_shares(ports, e, m, ae, drives):
     _, _, depth, rows, width = e.shape
     share = width // ports
-    tile = lax.axis_index("tile")
-    plane_cells = lax.axis_size("tile") * rows * width
-    target = cells[0] - tile * (rows * width)
-    push = [jnp.concatenate([amplitude[c, :1]] * (width // LANES), axis=1) for c in range(3)]
-    position = row_iota((rows, width)) * width + lane_iota((rows, width))
-
     def at(ref, c, z):
         return ref[0, c, z] if z < depth else jnp.zeros((rows, width), jnp.float32)
 
@@ -177,12 +181,9 @@
         fx = at(m, 0, z) - TIMESTEP * ((lane_next(ez) - ez) - (at(e, 1, z + 1) - ey))
         fy = at(m, 1, z) - TIMESTEP * ((at(e, 0, z + 1) - ex) - (row_next(ez, 0.0) - ez))
         fz = at(m, 2, z) - TIMESTEP * ((row_next(ey, 0.0) - ey) - (lane_next(ex) - ex))
-        hit = position == target - z * plane_cells
-        drive_x = ((fz - lane_prev(fz)) - (fy - fy_prev)) - jnp.where(hit, push[0], 0.0)
-        drive_y = ((fx - fx_prev) - (fz - row_prev(fz, 0.0))) - jnp.where(hit, push[1], 0.0)
-        drive_z = ((fy - row_prev(fy, 0.0)) - (fx - lane_prev(fx))) - jnp.where(
-            hit, push[2], 0.0
-        )
+        drive_x = ((fz - lane_prev(fz)) - (fy - fy_prev))
+        drive_y = ((fx - fx_prev) - (fz - row_prev(fz, 0.0)))
+        drive_z = ((fy - row_prev(fy, 0.0)) - (fx - lane_prev(fx)))
         ax, ay, az = (at(ae, c, z) for c in range(3))
         sums.append(ax * drive_x + ay * drive_y + az * drive_z)
         fx_prev, fy_prev = fx, fy
@@ -212,31 +213,56 @@
     return copies
 
 
-def early_kernel(ports, e, ae, edge, packed, edge_out, stage, sems):
+def all_shares(ports, e, m, ae, packed, drives, stage, sems):
+    copies = electric_shares(ports, e, ae, packed, stage, sems)
+    drive_shares(ports, e, m, ae, drives)
+    for copy in copies:
+        copy.wait()
+
+
+def early_kernel(ports, e, m, ae, edge, packed, drives, edge_out, stage, sems):
     edge_out[...] = edge[...]
 
     @pl.when(at_seam())
     def _():
-        for copy in electric_shares(ports, e, ae, packed, stage, sems):
-            copy.wait()
-
-
-def late_kernel(ports, e, m, ae, cells, amplitude, packed_in, packed, drives, stage, sems):
+        all_shares(ports, e, m, ae, packed, drives, stage, sems)
+
+
+def late_kernel(ports, e, m, ae, packed_in, drives_in, packed, drives, stage, sems):
     del packed_in
+
+    @pl.when(at_seam())
+    def _():
+        drives[...] = drives_in[...]
 
     @pl.when(jnp.logical_not(at_seam()))
     def _():
-        copies = electric_shares(ports, e, ae, packed, stage, sems)
-        drive_shares(ports, e, m, ae, cells, amplitude, drives)
-        for copy in copies:
-            copy.wait()
-
-    @pl.when(at_seam())
+        all_shares(ports, e, m, ae, packed, drives, stage, sems)
+
+
+def subtract_source(share, ae, cells, amplitude, drives):
+    _, _, depth, rows, width = ae.shape
+    own = rows * width
+    plane_cells = lax.axis_size("tile") * own
+    z = lax.div(cells[0], plane_cells)
+    local = cells[0] - z * plane_cells - lax.axis_index("tile") * own
+
+    @pl.when(jnp.logical_and(local >= 0, local < own))
     def _():
-        drive_shares(ports, e, m, ae, cells, amplitude, drives)
-
-
-def rim_kernel(ports, behind, ahead, ae_last, ae_first, e_first, drives, packed, patched, stage, sems):
+        x = lax.div(local, width)
+        y = local - x * width
+        slot, group = lax.div(y, share), lax.div(z, PLANES)
+        at = (z - group * PLANES) * share + (y - slot * share)
+        line = jnp.zeros((1, width), jnp.float32)
+        for c in range(3):
+            push = jnp.concatenate([amplitude[c, :1]] * (width // LANES), axis=1)
+            line = line + push * ae[0, c, z, pl.ds(x, 1), :]
+        amount = jnp.sum(jnp.where(lane_iota((1, width)) == y, line, 0.0), axis=1, keepdims=True)
+        change = jnp.where(lane_iota((1, LANES)) == at, amount, 0.0)
+        drives[slot, group, pl.ds(x, 1), :] = drives[slot, group, pl.ds(x, 1), :] - change
+
+
+def rim_kernel(ports, behind, ahead, ae_last, ae_first, e_first, ae, cells, amplitude, drives, packed, patched, stage, sems):
     del packed
     depth = behind.shape[0] // 4
     width = behind.shape[1]
@@ -262,16 +288,18 @@
         )
         for j in range(PLANES)
     ]
-    blocks = pack(planes, share, ports)
     row = row_iota((rows, LANES))
-    copies = []
-    for g in range(groups):
-        for port, block in enumerate(blocks):
+    inner = jnp.logical_and(row > 0, row < rows - 1)
+    for port, block in enumerate(pack(planes, share, ports)):
+        for g in range(groups):
             edges = jnp.where(row == 0, block[g : g + 1], block[groups + g : groups + g + 1])
-            inner = jnp.logical_and(row > 0, row < rows - 1)
             stage[port, g] = drives[port, g] + jnp.where(inner, 0.0, edges)
-        copies.append(pltpu.make_async_copy(stage.at[:, g], patched.at[:, groups + g], sems.at[g]))
-        copies[-1].start()
+    subtract_source(share, ae, cells, amplitude, stage)
+    copies = [
+        pltpu.make_async_copy(stage.at[:, g], patched.at[:, groups + g], sems.at[g]) for g in range(groups)
+    ]
+    for copy in copies:
+        copy.start()
     for copy in copies:
         copy.wait()
 
@@ -402,12 +430,13 @@
     shares = array(ports, 2 * depth // PLANES, rows, LANES)
     half = array(ports, depth // PLANES, rows, LANES)
     stage = [VMEM(half.shape, jnp.float32), pltpu.SemaphoreType.DMA((half.shape[1],))]
-    packed, to_behind = call(
+    fields = (electric, magnetic, adjoint_electric)
+    packed, drives, to_behind = call(
         functools.partial(early_kernel, ports),
-        (electric, adjoint_electric, to_behind),
-        (VMEM,) * 3,
-        (shares, edge),
-        (HBM, VMEM),
+        (*fields, to_behind),
+        (VMEM,) * 4,
+        (shares, half, edge),
+        (HBM, VMEM, VMEM),
         cells,
         cells,
         stage,
@@ -415,25 +444,25 @@
     ahead = from_behind(to_behind, "tile", -1)
     packed, drives = call(
         functools.partial(late_kernel, ports),
-        (electric, magnetic, adjoint_electric, port_cells, push, packed),
-        (VMEM,) * 3 + (SMEM, VMEM, HBM),
+        (*fields, packed, drives),
+        (VMEM,) * 3 + (HBM, VMEM),
         (shares, half),
         (HBM, VMEM),
         60 * cells,
         cells * 4 * 11,
         stage,
-        {5: 0},
+        {3: 0},
     )
     (packed,) = call(
         functools.partial(rim_kernel, ports),
-        (behind, ahead, *kept, drives, packed),
-        (VMEM,) * 6 + (HBM,),
+        (behind, ahead, *kept, adjoint_electric, port_cells, push, drives, packed),
+        (VMEM,) * 6 + (SMEM, VMEM, VMEM, HBM),
         (shares,),
         (HBM,),
         2 * cells,
         cells,
         stage,
-        {6: 0},
+        {9: 0},
     )
     gathered = lax.all_to_all(packed, "port", 0, 0, tiled=True)
     new_electric, new_magnetic, factors = call(

time: 37.8 us -> 37.8 us (level)
  starting transfers between devices: 20.3 us -> 19.3 us
  waiting for transfers between devices: 8.35 us -> 9.34 us
    ppermute x2, starting transfers between devices: 12.8 us -> 11.8 us  [from_behind(): lax.ppermute(value, axis, [(source, source + steps) for source in range(f...]
    ppermute x2, waiting for transfers between devices: 0.5 us -> 1.47 us  [from_behind(): lax.ppermute(value, axis, [(source, source + steps) for source in range(f...]
where the time goes in v10:
time: 37.8 us; the launch traced here: 37.5 us
  starting transfers between devices  19.3 us (51%)
  waiting for transfers between devices  9.34 us (25%)
  Pallas kernels  7.36 us (19%)
  between operations  1.44 us (4%)
    ppermute x2, starting transfers between devices, from_behind(): lax.ppermute(value, axis, [(source, source + steps) for source in range(f...  11.8 us
    all_to_all x1, waiting for transfers between devices, on_device(): gathered = lax.all_to_all(packed, 'port', 0, 0, tiled=True)  7.87 us
    all_to_all x1, starting transfers between devices, on_device(): gathered = lax.all_to_all(packed, 'port', 0, 0, tiled=True)  7.5 us
    pallas_call x6, Pallas kernels, call(): pl.pallas_call(kernel, out_shape=tuple((space(out.shape, out.dtype) if sp...  7.36 us
    ppermute x2, waiting for transfers between devices, from_behind(): lax.ppermute(value, axis, [(source, source + steps) for source in range(f...  1.47 us
  transfers between devices with their start and end apart: 3, of which 2 were waited for; matrix products, arithmetic and copies ran while one was open for 0% of the time, Pallas kernels for 12%

profile of v10, /device:TPU:48, one launch (start us, length us, event | category | flops | bytes accessed | tf_op | source)
XLA Modules:
  0.0 37.5 jit_solution(14382987885804671483)
XLA Ops:
  0.6 0.0 copy-start
  0.6 0.0 copy-start.2
  0.7 0.0 copy-start.1
  0.7 1.3 %shard_map.120 = (f32[24,640]{1,0:T(8,128)S(1)}, f32[24,640]{1,0:T(8,128)S(1)}, f32[3,8,640]{2,1,0:T(8,128)S(1)}, f32[2,8,640]{2,1,0:T(8,128)S(1)}, f32[2,8,640]{2,1,0:T(8,128)S(1)}, /*index=5*/f32[3,8,128]{2,1,0:T(8,128)S(1)}) custom-call(f32[1,3,6,16,640]{4,3,2,1,0:T(8,128)} %e.5, f32[1,3,6,16,640]{4,3,2,1,0:T(8,128)} %m.5, f32[1,3,6,16,640]{4,3,2,1,0:T(8,128)} %ae.9, ...), custom_call_target="tpu_custom_call" | custom-call | flops 614400 | bytes 3440640 | tf_op jit(solution)/shard_map/pallas_call | solution.py:385
  1.9 1.9 %collective-permute-start = (f32[24,640]{1,0:T(8,128)S(1)}, f32[24,640]{1,0:T(8,128)S(1)}, u32[]{:S(2)}, u32[]{:S(2)}) collective-permute-start(f32[24,640]{1,0:T(8,128)S(1)} %get-tuple-element.20), channel_id=1, source_target_pairs={{0,1},{1,2},{2,3},{3,4},{4,5},{5,6},{6,7},{7,8},{8,9},{9,10},{10,1... | collective-permute-start | bytes 184328 | tf_op jit(solution)/shard_map/ppermute | solution.py:25
  3.9 0.0 copy-done
  3.9 0.0 copy-done.2
  3.9 0.0 copy-done.1
  3.9 1.9 %shard_map.121 = (f32[16,4,16,128]{3,2,1,0:T(8,128)}, f32[16,2,16,128]{3,2,1,0:T(8,128)S(1)}, f32[24,640]{1,0:T(8,128)S(1)}) custom-call(f32[1,3,6,16,640]{4,3,2,1,0:T(8,128)S(1)} %copy-done.1, f32[1,3,6,16,640]{4,3,2,1,0:T(8,128)S(1)} %copy-done.2, f32[1,3,6,16,640]{4,3,2,1,0:T(8,128)S(1)} %copy-done, f32[24,640]{1,0:T(8,128)S(1)} %get-tuple-element.21.edge), custom_call_target="tpu_custom_call" | custom-call | flops 61440 | bytes 61440 | tf_op jit(solution)/shard_map/pallas_call | solution.py:385
  5.8 9.9 %collective-permute-start.1 = (f32[24,640]{1,0:T(8,128)S(1)}, f32[24,640]{1,0:T(8,128)S(1)}, u32[]{:S(2)}, u32[]{:S(2)}) collective-permute-start(f32[24,640]{1,0:T(8,128)S(1)} %get-tuple-element.22), channel_id=1, source_target_pairs={{1,0},{2,1},{3,2},{4,3},{5,4},{6,5},{7,6},{8,7},{9,8},{10,9},{11,1... | collective-permute-start | bytes 184328 | tf_op jit(solution)/shard_map/ppermute | solution.py:25
  16.3 0.1 shard_map.123
  16.4 0.0 collective-permute-done.behind
  16.4 1.5 %collective-permute-done.1.ahead = f32[24,640]{1,0:T(8,128)S(1)} collective-permute-done((f32[24,640]{1,0:T(8,128)S(1)}, f32[24,640]{1,0:T(8,128)S(1)}, u32[]{:S(2)}, u32[]{:S(2)}) %collective-permute-start.1) | collective-permute-done | bytes 61472 | tf_op jit(solution)/shard_map/ppermute | solution.py:25
  17.9 1.0 %shard_map.124 = f32[16,4,16,128]{3,2,1,0:T(8,128)} custom-call(f32[24,640]{1,0:T(8,128)S(1)} %collective-permute-done.behind, f32[24,640]{1,0:T(8,128)S(1)} %collective-permute-done.1.ahead, f32[3,8,640]{2,1,0:T(8,128)S(1)} %get-tuple-element.25.ae_last, f32[2,8,640]{2,1,0:T(8,128)S(1)} %get-tuple-element.26.ae_first, ...), custom_call_target="tpu_custom_call", output_to_operand_aliasing={{}: (9, {})} | custom-call | flops 122880 | bytes 61440 | tf_op jit(solution)/shard_map/pallas_call | solution.py:385
  18.8 0.0 copy-start.3
  18.8 0.0 copy-start.4
  18.8 0.0 copy-start.5
  18.9 0.0 copy-start.6
  18.9 7.5 %all-to-all-start = ((f32[16,4,16,128]{3,2,1,0:T(8,128)}), f32[16,4,16,128]{3,2,1,0:T(8,128)S(1)}, u32[]{:S(2)}, u32[]{:S(2)}) async-start(f32[16,4,16,128]{3,2,1,0:T(8,128)} %shard_map.124), calls=%async_computation | async-start | bytes 1048576 | tf_op jit(solution)/shard_map/all_to_all | solution.py:467
  26.4 0.0 copy-done.3
  26.4 0.0 copy-done.4
  26.4 0.0 copy-done.5
  26.4 0.0 copy-done.6
  26.4 2.5 %shard_map.122 = (f32[1,3,6,16,640]{4,3,2,1,0:T(8,128)}, f32[1,3,6,16,640]{4,3,2,1,0:T(8,128)}, f32[3,2,16,128]{3,2,1,0:T(8,128)S(1)}) custom-call(f32[1,3,6,16,640]{4,3,2,1,0:T(8,128)S(1)} %copy-done, f32[1,3,6,16,640]{4,3,2,1,0:T(8,128)S(1)} %copy-done.3, s32[6,16,640]{2,1,0:T(8,128)S(1)} %copy-done.4, f32[24,640]{1,0:T(8,128)S(1)} %collective-permute-done.behind, ...), custom_call_target="tpu_custom_call" | custom-call | flops 4915200 | bytes 3194880 | tf_op jit(solution)/shard_map/pallas_call | solution.py:385
  28.9 7.9 %all-to-all-done.gathered = f32[16,4,16,128]{3,2,1,0:T(8,128)S(1)} async-done(((f32[16,4,16,128]{3,2,1,0:T(8,128)}), f32[16,4,16,128]{3,2,1,0:T(8,128)S(1)}, u32[]{:S(2)}, u32[]{:S(2)}) %all-to-all-start) | async-done | bytes 524320 | tf_op jit(solution)/shard_map/all_to_all | solution.py:467
  36.7 0.7 %shard_map.125 = (f32[6,16,40]{2,1,0:T(8,128)}, f32[6,16,40]{2,1,0:T(8,128)}) custom-call(f32[16,4,16,128]{3,2,1,0:T(8,128)S(1)} %all-to-all-done.gathered, f32[3,2,16,128]{3,2,1,0:T(8,128)S(1)} %get-tuple-element.33.factors), custom_call_target="tpu_custom_call" | custom-call | flops 245760 | bytes 737280 | tf_op jit(solution)/shard_map/pallas_call | solution.py:385
Async XLA Ops:
  0.6 3.2 %copy-start = (f32[1,3,6,16,640]{4,3,2,1,0:T(8,128)S(1)}, f32[1,3,6,16,640]{4,3,2,1,0:T(8,128)}, u32[]{:S(2)}) copy-start(f32[1,3,6,16,640]{4,3,2,1,0:T(8,128)} %ae.9) | copy-start | bytes 2211844
  0.6 3.2 %copy-start.2 = (f32[1,3,6,16,640]{4,3,2,1,0:T(8,128)S(1)}, f32[1,3,6,16,640]{4,3,2,1,0:T(8,128)}, u32[]{:S(2)}) copy-start(f32[1,3,6,16,640]{4,3,2,1,0:T(8,128)} %m.5) | copy-start | bytes 2211844
  0.7 3.2 %copy-start.1 = (f32[1,3,6,16,640]{4,3,2,1,0:T(8,128)S(1)}, f32[1,3,6,16,640]{4,3,2,1,0:T(8,128)}, u32[]{:S(2)}) copy-start(f32[1,3,6,16,640]{4,3,2,1,0:T(8,128)} %e.5) | copy-start | bytes 2211844
  1.9 14.4 %collective-permute-start = (f32[24,640]{1,0:T(8,128)S(1)}, f32[24,640]{1,0:T(8,128)S(1)}, u32[]{:S(2)}, u32[]{:S(2)}) collective-permute-start(f32[24,640]{1,0:T(8,128)S(1)} %get-tuple-element.20), channel_id=1, source_target_pairs={{0,1},{1,2},{2,3},{3,4},{4,5},{5,6},{6,7},{7,8},{8,9},{9,10},{10,1... | collective-permute-start | bytes 184328 | tf_op jit(solution)/shard_map/ppermute | solution.py:25
  5.8 12.1 %collective-permute-start.1 = (f32[24,640]{1,0:T(8,128)S(1)}, f32[24,640]{1,0:T(8,128)S(1)}, u32[]{:S(2)}, u32[]{:S(2)}) collective-permute-start(f32[24,640]{1,0:T(8,128)S(1)} %get-tuple-element.22), channel_id=1, source_target_pairs={{1,0},{2,1},{3,2},{4,3},{5,4},{6,5},{7,6},{8,7},{9,8},{10,9},{11,1... | collective-permute-start | bytes 184328 | tf_op jit(solution)/shard_map/ppermute | solution.py:25
  18.8 7.5 %copy-start.3 = (f32[1,3,6,16,640]{4,3,2,1,0:T(8,128)S(1)}, f32[1,3,6,16,640]{4,3,2,1,0:T(8,128)}, u32[]{:S(2)}) copy-start(f32[1,3,6,16,640]{4,3,2,1,0:T(8,128)} %am.3) | copy-start | bytes 2211844
  18.8 7.5 %copy-start.4 = (s32[6,16,640]{2,1,0:T(8,128)S(1)}, s32[6,16,640]{2,1,0:T(8,128)}, u32[]{:S(2)}) copy-start(s32[6,16,640]{2,1,0:T(8,128)} %labels.3) | copy-start | bytes 737284
  18.8 7.5 %copy-start.5 = (f32[8]{0:T(128)S(1)}, f32[8]{0:T(128)}, u32[]{:S(2)}) copy-start(f32[8]{0:T(128)} %perm.1) | copy-start | bytes 100
  18.9 7.5 %copy-start.6 = (f32[8]{0:T(128)S(1)}, f32[8]{0:T(128)}, u32[]{:S(2)}) copy-start(f32[8]{0:T(128)} %cond.1) | copy-start | bytes 100
  18.9 17.9 %all-to-all-start = ((f32[16,4,16,128]{3,2,1,0:T(8,128)}), f32[16,4,16,128]{3,2,1,0:T(8,128)S(1)}, u32[]{:S(2)}, u32[]{:S(2)}) async-start(f32[16,4,16,128]{3,2,1,0:T(8,128)} %shard_map.124), calls=%async_computation | async-start | bytes 1048576 | tf_op jit(solution)/shard_map/all_to_all | solution.py:467

commit v11 on v9

--- a/solution.py
+++ b/solution.py
@@ -331,25 +331,33 @@
         here = after
 
 
-def gradient_kernel(gathered, factors, grad_perm, grad_cond):
-    ports, slabs, rows, _ = gathered.shape
+def gradient_kernel(gathered, factors, grad_perm, grad_cond, perm_stage, cond_stage, sems):
+    ports = gathered.shape[0]
     depth, _, share = grad_perm.shape
     groups = depth // PLANES
-    sums = []
-    for slab in range(slabs):
+
+    def total_of(slab):
         total = gathered[0, slab]
         for port in range(1, ports):
             total = total + gathered[port, slab]
-        sums.append(total)
+        return total
+
+    copies = []
     for group in range(groups):
-        corr_a, corr_b = sums[group], sums[groups + group]
+        corr_a, corr_b = total_of(group), total_of(groups + group)
         factor, permittivity, conductivity = (factors[i, group] for i in range(3))
         by_perm = factor * (conductivity * corr_a - corr_b)
         by_cond = factor * (-permittivity * corr_a - HALF_STEP * corr_b)
         for j in range(PLANES):
-            for ref, value in ((grad_perm, by_perm), (grad_cond, by_cond)):
+            for ref, value in ((perm_stage, by_perm), (cond_stage, by_cond)):
                 moved = pltpu.roll(value, LANES - j * share, 1) if j else value
                 ref[group * PLANES + j] = moved[:, :share]
+        part = pl.ds(group * PLANES, PLANES)
+        for i, (src, dst) in enumerate(((perm_stage, grad_perm), (cond_stage, grad_cond))):
+            copies.append(pltpu.make_async_copy(src.at[part], dst.at[part], sems.at[2 * group + i]))
+            copies[-1].start()
+    for copy in copies:
+        copy.wait()
 
 
 def call(kernel, inputs, spaces, outs, out_spaces, flops, moved, scratch=(), aliases=()):
@@ -451,9 +459,10 @@
         (gathered, factors),
         (VMEM,) * 2,
         (gradient, gradient),
-        (HBM_BLOCK,) * 2,
+        (HBM,) * 2,
         4 * cells,
         cells * 4 * 3,
+        [VMEM(gradient.shape, jnp.float32)] * 2 + [pltpu.SemaphoreType.DMA((2 * depth // PLANES,))],
     )
     return (new_electric, new_magnetic, gradient_perm, gradient_cond)
 

time: 37.8 us -> 37.8 us (level)
  no operation moved by 1% of the time
where the time goes in v11:
time: 37.8 us; the launch traced here: 37.6 us
  starting transfers between devices  20.3 us (54%)
  waiting for transfers between devices  8.35 us (22%)
  Pallas kernels  7.41 us (20%)
  between operations  1.44 us (4%)
    ppermute x2, starting transfers between devices, from_behind(): lax.ppermute(value, axis, [(source, source + steps) for source in range(f...  12.8 us
    all_to_all x1, waiting for transfers between devices, on_device(): gathered = lax.all_to_all(packed, 'port', 0, 0, tiled=True)  7.85 us
    all_to_all x1, starting transfers between devices, on_device(): gathered = lax.all_to_all(packed, 'port', 0, 0, tiled=True)  7.5 us
    pallas_call x6, Pallas kernels, call(): pl.pallas_call(kernel, out_shape=tuple((space(out.shape, out.dtype) if sp...  7.41 us
  transfers between devices with their start and end apart: 3, of which 2 were waited for; matrix products, arithmetic and copies ran while one was open for 0% of the time, Pallas kernels for 12%

profile of v11, /device:TPU:48, one launch (start us, length us, event | category | flops | bytes accessed | tf_op | source)
XLA Modules:
  0.0 37.6 jit_solution(17620049129046168528)
XLA Ops:
  0.6 0.0 copy-start
  0.6 0.0 copy-start.1
  0.7 1.2 %shard_map.120 = (f32[24,640]{1,0:T(8,128)S(1)}, f32[24,640]{1,0:T(8,128)S(1)}, f32[3,8,640]{2,1,0:T(8,128)S(1)}, f32[2,8,640]{2,1,0:T(8,128)S(1)}, f32[2,8,640]{2,1,0:T(8,128)S(1)}, /*index=5*/f32[3,8,128]{2,1,0:T(8,128)S(1)}) custom-call(f32[1,3,6,16,640]{4,3,2,1,0:T(8,128)} %e.5, f32[1,3,6,16,640]{4,3,2,1,0:T(8,128)} %m.3, f32[1,3,6,16,640]{4,3,2,1,0:T(8,128)} %ae.7, ...), custom_call_target="tpu_custom_call" | custom-call | flops 614400 | bytes 3440640 | tf_op jit(solution)/shard_map/pallas_call | solution.py:365
  1.9 1.9 %collective-permute-start = (f32[24,640]{1,0:T(8,128)S(1)}, f32[24,640]{1,0:T(8,128)S(1)}, u32[]{:S(2)}, u32[]{:S(2)}) collective-permute-start(f32[24,640]{1,0:T(8,128)S(1)} %get-tuple-element.19), channel_id=1, source_target_pairs={{0,1},{1,2},{2,3},{3,4},{4,5},{5,6},{6,7},{7,8},{8,9},{9,10},{10,1... | collective-permute-start | bytes 184328 | tf_op jit(solution)/shard_map/ppermute | solution.py:25
  3.8 0.0 copy-done
  3.8 0.0 copy-done.1
  3.8 0.0 copy-start.2
  3.8 1.0 %shard_map.121 = (f32[16,4,16,128]{3,2,1,0:T(8,128)}, f32[24,640]{1,0:T(8,128)S(1)}) custom-call(f32[1,3,6,16,640]{4,3,2,1,0:T(8,128)S(1)} %copy-done.1, f32[1,3,6,16,640]{4,3,2,1,0:T(8,128)S(1)} %copy-done, f32[24,640]{1,0:T(8,128)S(1)} %get-tuple-element.20.edge), custom_call_target="tpu_custom_call" | custom-call | flops 61440 | bytes 61440 | tf_op jit(solution)/shard_map/pallas_call | solution.py:365
  4.8 10.9 %collective-permute-start.1 = (f32[24,640]{1,0:T(8,128)S(1)}, f32[24,640]{1,0:T(8,128)S(1)}, u32[]{:S(2)}, u32[]{:S(2)}) collective-permute-start(f32[24,640]{1,0:T(8,128)S(1)} %get-tuple-element.21), channel_id=1, source_target_pairs={{1,0},{2,1},{3,2},{4,3},{5,4},{6,5},{7,6},{8,7},{9,8},{10,9},{11,1... | collective-permute-start | bytes 184328 | tf_op jit(solution)/shard_map/ppermute | solution.py:25
  16.4 0.0 copy-done.2
  16.4 1.0 %shard_map.123 = (f32[16,4,16,128]{3,2,1,0:T(8,128)}, f32[16,2,16,128]{3,2,1,0:T(8,128)S(1)}) custom-call(f32[1,3,6,16,640]{4,3,2,1,0:T(8,128)S(1)} %copy-done.1, f32[1,3,6,16,640]{4,3,2,1,0:T(8,128)S(1)} %copy-done.2, f32[1,3,6,16,640]{4,3,2,1,0:T(8,128)S(1)} %copy-done, s32[1]{0:T(128)S(6)} %copy.17.cells, ...), custom_call_target="tpu_custom_call", output_to_operand_aliasing={{0}: (5, {})} | custom-call | flops 3686400 | bytes 2703360 | tf_op jit(solution)/shard_map/pallas_call | solution.py:365
  17.4 0.0 collective-permute-done.behind
  17.4 0.5 %collective-permute-done.1.ahead = f32[24,640]{1,0:T(8,128)S(1)} collective-permute-done((f32[24,640]{1,0:T(8,128)S(1)}, f32[24,640]{1,0:T(8,128)S(1)}, u32[]{:S(2)}, u32[]{:S(2)}) %collective-permute-start.1) | collective-permute-done | bytes 61472 | tf_op jit(solution)/shard_map/ppermute | solution.py:25
  17.9 0.9 %shard_map.124 = f32[16,4,16,128]{3,2,1,0:T(8,128)} custom-call(f32[24,640]{1,0:T(8,128)S(1)} %collective-permute-done.behind, f32[24,640]{1,0:T(8,128)S(1)} %collective-permute-done.1.ahead, f32[3,8,640]{2,1,0:T(8,128)S(1)} %get-tuple-element.24.ae_last, f32[2,8,640]{2,1,0:T(8,128)S(1)} %get-tuple-element.25.ae_first, ...), custom_call_target="tpu_custom_call", output_to_operand_aliasing={{}: (6, {})} | custom-call | flops 122880 | bytes 61440 | tf_op jit(solution)/shard_map/pallas_call | solution.py:365
  18.9 0.0 copy-start.3
  18.9 0.0 copy-start.4
  18.9 0.0 copy-start.5
  18.9 0.0 copy-start.6
  18.9 7.5 %all-to-all-start = ((f32[16,4,16,128]{3,2,1,0:T(8,128)}), f32[16,4,16,128]{3,2,1,0:T(8,128)S(1)}, u32[]{:S(2)}, u32[]{:S(2)}) async-start(f32[16,4,16,128]{3,2,1,0:T(8,128)} %shard_map.124), calls=%async_computation | async-start | bytes 1048576 | tf_op jit(solution)/shard_map/all_to_all | solution.py:446
  26.4 0.0 copy-done.3
  26.4 0.0 copy-done.4
  26.4 0.0 copy-done.5
  26.5 0.0 copy-done.6
  26.5 2.5 %shard_map.122 = (f32[1,3,6,16,640]{4,3,2,1,0:T(8,128)}, f32[1,3,6,16,640]{4,3,2,1,0:T(8,128)}, f32[3,2,16,128]{3,2,1,0:T(8,128)S(1)}) custom-call(f32[1,3,6,16,640]{4,3,2,1,0:T(8,128)S(1)} %copy-done, f32[1,3,6,16,640]{4,3,2,1,0:T(8,128)S(1)} %copy-done.3, s32[6,16,640]{2,1,0:T(8,128)S(1)} %copy-done.4, f32[24,640]{1,0:T(8,128)S(1)} %collective-permute-done.behind, ...), custom_call_target="tpu_custom_call" | custom-call | flops 4915200 | bytes 3194880 | tf_op jit(solution)/shard_map/pallas_call | solution.py:365
  28.9 7.9 %all-to-all-done.gathered = f32[16,4,16,128]{3,2,1,0:T(8,128)S(1)} async-done(((f32[16,4,16,128]{3,2,1,0:T(8,128)}), f32[16,4,16,128]{3,2,1,0:T(8,128)S(1)}, u32[]{:S(2)}, u32[]{:S(2)}) %all-to-all-start) | async-done | bytes 524320 | tf_op jit(solution)/shard_map/all_to_all | solution.py:446
  36.8 0.8 %shard_map.125 = (f32[6,16,40]{2,1,0:T(8,128)}, f32[6,16,40]{2,1,0:T(8,128)}) custom-call(f32[16,4,16,128]{3,2,1,0:T(8,128)S(1)} %all-to-all-done.gathered, f32[3,2,16,128]{3,2,1,0:T(8,128)S(1)} %get-tuple-element.31.factors), custom_call_target="tpu_custom_call" | custom-call | flops 245760 | bytes 737280 | tf_op jit(solution)/shard_map/pallas_call | solution.py:365
Async XLA Ops:
  0.6 3.2 %copy-start = (f32[1,3,6,16,640]{4,3,2,1,0:T(8,128)S(1)}, f32[1,3,6,16,640]{4,3,2,1,0:T(8,128)}, u32[]{:S(2)}) copy-start(f32[1,3,6,16,640]{4,3,2,1,0:T(8,128)} %ae.7) | copy-start | bytes 2211844
  0.6 3.2 %copy-start.1 = (f32[1,3,6,16,640]{4,3,2,1,0:T(8,128)S(1)}, f32[1,3,6,16,640]{4,3,2,1,0:T(8,128)}, u32[]{:S(2)}) copy-start(f32[1,3,6,16,640]{4,3,2,1,0:T(8,128)} %e.5) | copy-start | bytes 2211844
  1.9 15.6 %collective-permute-start = (f32[24,640]{1,0:T(8,128)S(1)}, f32[24,640]{1,0:T(8,128)S(1)}, u32[]{:S(2)}, u32[]{:S(2)}) collective-permute-start(f32[24,640]{1,0:T(8,128)S(1)} %get-tuple-element.19), channel_id=1, source_target_pairs={{0,1},{1,2},{2,3},{3,4},{4,5},{5,6},{6,7},{7,8},{8,9},{9,10},{10,1... | collective-permute-start | bytes 184328 | tf_op jit(solution)/shard_map/ppermute | solution.py:25
  3.8 12.6 %copy-start.2 = (f32[1,3,6,16,640]{4,3,2,1,0:T(8,128)S(1)}, f32[1,3,6,16,640]{4,3,2,1,0:T(8,128)}, u32[]{:S(2)}) copy-start(f32[1,3,6,16,640]{4,3,2,1,0:T(8,128)} %m.3) | copy-start | bytes 2211844
  4.8 13.1 %collective-permute-start.1 = (f32[24,640]{1,0:T(8,128)S(1)}, f32[24,640]{1,0:T(8,128)S(1)}, u32[]{:S(2)}, u32[]{:S(2)}) collective-permute-start(f32[24,640]{1,0:T(8,128)S(1)} %get-tuple-element.21), channel_id=1, source_target_pairs={{1,0},{2,1},{3,2},{4,3},{5,4},{6,5},{7,6},{8,7},{9,8},{10,9},{11,1... | collective-permute-start | bytes 184328 | tf_op jit(solution)/shard_map/ppermute | solution.py:25
  18.9 7.5 %copy-start.3 = (f32[1,3,6,16,640]{4,3,2,1,0:T(8,128)S(1)}, f32[1,3,6,16,640]{4,3,2,1,0:T(8,128)}, u32[]{:S(2)}) copy-start(f32[1,3,6,16,640]{4,3,2,1,0:T(8,128)} %am.3) | copy-start | bytes 2211844
  18.9 7.5 %copy-start.4 = (s32[6,16,640]{2,1,0:T(8,128)S(1)}, s32[6,16,640]{2,1,0:T(8,128)}, u32[]{:S(2)}) copy-start(s32[6,16,640]{2,1,0:T(8,128)} %labels.3) | copy-start | bytes 737284
  18.9 7.5 %copy-start.5 = (f32[8]{0:T(128)S(1)}, f32[8]{0:T(128)}, u32[]{:S(2)}) copy-start(f32[8]{0:T(128)} %perm.1) | copy-start | bytes 100
  18.9 7.5 %copy-start.6 = (f32[8]{0:T(128)S(1)}, f32[8]{0:T(128)}, u32[]{:S(2)}) copy-start(f32[8]{0:T(128)} %cond.1) | copy-start | bytes 100
  18.9 17.9 %all-to-all-start = ((f32[16,4,16,128]{3,2,1,0:T(8,128)}), f32[16,4,16,128]{3,2,1,0:T(8,128)S(1)}, u32[]{:S(2)}, u32[]{:S(2)}) async-start(f32[16,4,16,128]{3,2,1,0:T(8,128)} %shard_map.124), calls=%async_computation | async-start | bytes 1048576 | tf_op jit(solution)/shard_map/all_to_all | solution.py:446
